TPU v7x, 128 devices: a whole 4x4x4 slice. The times are simulated.
128 devices in a mesh: qrow: 8 (over z_lo, y), kcol: 16 (over z_hi, x, core).
Axes of the slice: x: 4, y: 4, z: 4 (z_hi: 2, z_lo: 2; z = z_hi * 2 + z_lo), core: 2. Of those that a mesh axis runs over, the one named last changes fastest.
Arguments:
- queries: bfloat16 [16384, 1024], P(('qrow', 'kcol')), may hold values from -100 to 100
- keys: bfloat16 [16384, 128], P(('qrow', 'kcol')), may hold values from -5 to 5
- values: bfloat16 [16384, 128], P(('qrow', 'kcol')), may hold values from -5 to 5
- query_feats: bfloat16 [16384, 512], P(('qrow', 'kcol')), may hold values from -5 to 5
- key_feats: bfloat16 [16384, 512], P(('qrow', 'kcol')), may hold values from -5 to 5
- block_pos: int32 [128], replicated, may hold values from 0 to 127, as said below
Outputs:
- query_grad: float32 [16384, 512], P(('qrow', 'kcol'))
- key_grad: float32 [16384, 512], P(('qrow', 'kcol'))
Inputs may be any that keep to these rules, and one draw needn't show every extreme that they name: A permutation of the 128 sequence blocks: owner o holds block block_pos[o]; the owners 16 k to 16 k + 15 hold the blocks 16 k to 16 k + 15 in some order.
All inputs are finite; a program needn't handle non-finite values.
Results may differ from a plain program's by a relative error of at most 0.0022.
Values may be sent and summed in bfloat16 or wider, within the bound.
No kernel may reach another device: no remote copies, remote signals or barrier semaphores. Data moves between devices by JAX's collectives and lax.ppermute only.
A program may use at most 128 MiB of HBM per device.

v0:
```python
import math

import jax
import jax.numpy as jnp
from jax import lax
from jax.sharding import PartitionSpec as P

FLOOR_SCORE = -1e30


def in_one_piece(arrays, axis, dim, along):
    widths = [a.shape[along] for a in arrays]
    both = jnp.concatenate(arrays, axis=along)
    whole = lax.all_gather(both, axis, axis=dim, tiled=True)
    return tuple(jnp.split(whole, [sum(widths[:k]) for k in range(1, len(widths))], axis=along))


def from_everyone(array, axis):
    size = lax.axis_size(axis)
    return lax.all_to_all(
        jnp.broadcast_to(array[None], (size, *array.shape)), axis, 0, 0, tiled=True
    )


def taken_together(array, axis):
    return from_everyone(array, axis).max(axis=0)


def of_everyone(array, axis):
    everything = from_everyone(array, axis)
    return jnp.sum(everything, axis=0)


def split_up(array, dim, size):
    before, after = (array.shape[:dim], array.shape[dim + 1 :])
    return jnp.moveaxis(array.reshape(*before, size, -1, *after), dim, 0)


def sum_at_owner(array, axis, dim):
    parts = split_up(array, dim, lax.axis_size(axis))
    arrived = lax.all_to_all(parts, axis, split_axis=0, concat_axis=0, tiled=True)
    return arrived.sum(axis=0)


def contract_last(left, right):
    return lax.dot_general(
        left, right, (((1,), (1,)), ((), ())), preferred_element_type=jnp.float32
    )


def contract_first(left, right):
    return lax.dot_general(
        left, right, (((0,), (0,)), ((), ())), preferred_element_type=jnp.float32
    )


def masked_scores(q_head, key_block, pos_rows, pos_keys):
    scale = 1.0 / math.sqrt(q_head.shape[1])
    scores = contract_last(q_head, key_block) * scale
    allowed = pos_rows[:, None] >= pos_keys[None, :]
    return (allowed, scores)


def local_stats(q_head, key_block, pos_rows, pos_keys):
    allowed, scores = masked_scores(q_head, key_block, pos_rows, pos_keys)
    highest = jnp.max(jnp.where(allowed, scores, FLOOR_SCORE), axis=1)
    summed = jnp.sum(jnp.where(allowed, jnp.exp(scores - highest[:, None]), 0.0), axis=1)
    return (highest, summed)


def error_block(q_head, qf_head, key_block, kf_block, pos_rows, pos_keys, highest, totals, counts):
    allowed, scores = masked_scores(q_head, key_block, pos_rows, pos_keys)
    teacher = jnp.where(allowed, jnp.exp(scores - highest[:, None]), 0.0) / totals[:, None]
    feat_scale = 1.0 / math.sqrt(qf_head.shape[1])
    student = jnp.where(
        allowed, contract_last(qf_head, kf_block) * feat_scale / counts[:, None], 0.0
    )
    return (allowed, teacher - student)


def per_device(queries, keys, values, query_feats, key_feats, block_pos):
    query_groups = lax.axis_size("qrow")
    key_groups = lax.axis_size("kcol")
    group_row = lax.axis_index("qrow")
    group_col = lax.axis_index("kcol")
    block_len = queries.shape[0]
    head_size = keys.shape[1]
    head_count = queries.shape[1] // head_size
    feat_size = query_feats.shape[1] // head_count
    offsets = jnp.arange(block_len, dtype=jnp.int32)
    owners_here = lax.dynamic_slice_in_dim(block_pos, group_row * key_groups, key_groups, 0)
    pos_rows = (owners_here[:, None] * block_len + offsets[None, :]).reshape(-1)
    owner_grid = block_pos.reshape(query_groups, key_groups)
    owners_cols = lax.dynamic_slice_in_dim(owner_grid, group_col, 1, 1)[:, 0]
    pos_keys = (owners_cols[:, None] * block_len + offsets[None, :]).reshape(-1)
    counts = (pos_rows + 1).astype(jnp.float32)
    roots = jnp.sqrt(counts)
    q_tile, qf_tile = in_one_piece((queries, query_feats), "kcol", 0, 1)
    k_tile, v_tile, kf_tile = in_one_piece((keys, values, key_feats), "qrow", 0, 1)
    n_rows = q_tile.shape[0]
    n_keys = k_tile.shape[0]

    def stats_head(head_index, carry):
        highs, sums = carry
        q_head = lax.dynamic_slice_in_dim(q_tile, head_index * head_size, head_size, 1)
        highest, summed = local_stats(q_head, k_tile, pos_rows, pos_keys)
        highs = lax.dynamic_update_slice_in_dim(highs, highest[:, None], head_index, 1)
        sums = lax.dynamic_update_slice_in_dim(sums, summed[:, None], head_index, 1)
        return (highs, sums)

    start_stats = (
        jnp.zeros((n_rows, head_count), jnp.float32),
        jnp.zeros((n_rows, head_count), jnp.float32),
    )
    highs, sums = lax.fori_loop(0, head_count, stats_head, start_stats)
    best = taken_together(highs.astype(jnp.bfloat16), "kcol").astype(highs.dtype)
    sums = of_everyone(sums * jnp.exp(highs - best), "kcol")
    highs = best

    def head_slices(head_index):
        q_head = lax.dynamic_slice_in_dim(q_tile, head_index * head_size, head_size, 1)
        qf_head = lax.dynamic_slice_in_dim(qf_tile, head_index * feat_size, feat_size, 1)
        kf_head = lax.dynamic_slice_in_dim(kf_tile, head_index * feat_size, feat_size, 1)
        highest = lax.dynamic_slice_in_dim(highs, head_index, 1, 1)[:, 0]
        summed = lax.dynamic_slice_in_dim(sums, head_index, 1, 1)[:, 0]
        return (q_head, qf_head, kf_head, highest, summed)

    def mixing_head(head_index, mixed):
        q_head, qf_head, kf_head, highest, summed = head_slices(head_index)
        allowed, error = error_block(
            q_head, qf_head, k_tile, kf_head, pos_rows, pos_keys, highest, summed, counts
        )
        result = jnp.dot(error.astype(jnp.bfloat16), v_tile, preferred_element_type=jnp.float32)
        return lax.dynamic_update_slice_in_dim(mixed, result, head_index * head_size, 1)

    mixed = lax.fori_loop(
        0, head_count, mixing_head, jnp.zeros((n_rows, head_count * head_size), jnp.float32)
    )
    mixed_b = lax.psum(mixed, "kcol").astype(jnp.bfloat16)
    key_scale = 1.0 / math.sqrt(head_size)

    def grad_head(head_index, carry):
        q_grads, k_grads = carry
        q_head, qf_head, kf_head, highest, summed = head_slices(head_index)
        mixed_head = lax.dynamic_slice_in_dim(mixed_b, head_index * head_size, head_size, 1)
        allowed, error = error_block(
            q_head, qf_head, k_tile, kf_head, pos_rows, pos_keys, highest, summed, counts
        )
        coupled = contract_last(mixed_head, v_tile) * key_scale
        weights = jnp.where(allowed, roots[:, None] * error + coupled, 0.0).astype(jnp.bfloat16)
        q_part = -jnp.dot(weights, kf_head, preferred_element_type=jnp.float32)
        k_part = -contract_first(weights, qf_head)
        q_grads = lax.dynamic_update_slice_in_dim(q_grads, q_part, head_index * feat_size, 1)
        k_grads = lax.dynamic_update_slice_in_dim(k_grads, k_part, head_index * feat_size, 1)
        return (q_grads, k_grads)

    start_grads = (
        jnp.zeros((n_rows, head_count * feat_size), jnp.float32),
        jnp.zeros((n_keys, head_count * feat_size), jnp.float32),
    )
    q_grads, k_grads = lax.fori_loop(0, head_count, grad_head, start_grads)
    query_grad = lax.psum_scatter(q_grads, "kcol", scatter_dimension=0, tiled=True)
    key_grad = sum_at_owner(k_grads, "qrow", 0)
    return (query_grad, key_grad)


def solution(mesh):
    return jax.shard_map(
        per_device,
        mesh=mesh,
        in_specs=(
            P(("qrow", "kcol"), None),
            P(("qrow", "kcol"), None),
            P(("qrow", "kcol"), None),
            P(("qrow", "kcol"), None),
            P(("qrow", "kcol"), None),
            P(),
        ),
        out_specs=(P(("qrow", "kcol"), None), P(("qrow", "kcol"), None)),
        check_vma=False,
    )
```

profile of v0, /device:TPU:0, one launch (start us, length us, event | category | flops | bytes accessed | tf_op | source)
XLA Modules:
  0.0 653.7 jit_solution(6674891095405500071)
XLA Ops:
  12.4 40.4 %all-gather.5.cloned.1.call-done = bf16[1024,768]{1,0:T(8,128)(2,1)} async-done(((bf16[128,768]{1,0:T(8,128)(2,1)}), bf16[1024,768]{1,0:T(8,128)(2,1)}) %all-gather.5.cloned.1.call-update) | async-done | bytes 1572880 | tf_op jit(solution)/shard_map/all_gather | solution.py:14
  54.6 63.7 %all-gather.3.cloned.1.call-done = bf16[2048,1536]{1,0:T(8,128)(2,1)} async-done(((bf16[128,1536]{1,0:T(8,128)(2,1)}), bf16[2048,1536]{1,0:T(8,128)(2,1)}) %all-gather.3.cloned.1.call-update) | async-done | bytes 6291472 | tf_op jit(solution)/shard_map/all_gather | solution.py:14
  122.9 43.0 %while.48 = (s32[]{:T(128)}, f32[2048,8]{0,1:T(8,128)S(1)}, f32[2048,8]{0,1:T(8,128)S(1)}, bf16[2048,1024]{1,0:T(8,128)(2,1)}, bf16[1024,128]{1,0:T(8,128)(2,1)S...) while((s32[]{:T(128)}, f32[2048,8]{0,1:T(8,128)S(1)}, ...), condition=%wide.region_3.4_spmd.clone, body=%wide.region_0.3_spmd.clone.sunk | while | flops 555744256 | bytes 17658128 | solution.py:115
  165.9 15.8 %all_to_all.15 = bf16[16,2048,8]{1,2,0:T(8,128)(2,1)S(1)} all-to-all(bf16[16,2048,8]{1,2,0:T(8,128)(2,1)S(1)} %broadcast_in_dim.82), channel_id=1, replica_groups=mesh['qrow'=8,'kcol'=16] {'kcol'}, dimensions={0} | all-to-all | bytes 1048576 | tf_op jit(solution)/shard_map/all_to_all | solution.py:20
  187.4 17.9 %all-to-all-done.1 = f32[16,2048,8]{1,2,0:T(8,128)} async-done(((f32[16,2048,8]{1,2,0:T(8,128)}), f32[16,2048,8]{1,2,0:T(8,128)}, u32[]{:S(2)}, u32[]{:S(2)}) %all-to-all-start.1) | async-done | bytes 1048608 | tf_op jit(solution)/shard_map/all_to_all | solution.py:20
  210.8 127.6 %while.49 = (s32[]{:T(128)}, f32[2048,1024]{1,0:T(8,128)}, bf16[2048,1024]{1,0:T(8,128)(2,1)}, bf16[1024,128]{1,0:T(8,128)(2,1)S(1)}, f32[2048,8]{0,1:T(8,128)S(...) while((s32[]{:T(128)}, f32[2048,1024]{1,0:T(8,128)}, ...), condition=%wide.region_7.8_spmd.clone.clone, body=%wide.region_6.7_spmd.clone.clone.sunk | while | flops 1363155968 | bytes 19752808 | solution.py:136
  212.8 5.5 fusion.104
  218.3 8.5 %convolution_dynamic-update-slice_fusion.2 = f32[2048,1024]{1,0:T(8,128)} fusion(f32[2048,1024]{1,0:T(8,128)} %get-tuple-element.1063, s32[]{:T(128)S(6)} %select_n.198, bf16[1024,128]{1,0:T(8,128)(2,1)} %get-tuple-element.1087, f32[2048,1024]{1,0:T(8,128)} %fusion.104, f32[2048]{0:T(1024)} %get-tuple-element.991, f32[2048]{0:T(1024)} %bitcast.76, ...), kind=kOutput, calls=%fused_computation.23.clone.1 | convolution fusion | flops 826277888 | bytes 10524160 | tf_op jit(solution)/shard_map/while/body/eval_jaxpr/dot_general | solution.py:133
  228.8 5.5 fusion.104
  234.3 8.5 %convolution_dynamic-update-slice_fusion.2 = f32[2048,1024]{1,0:T(8,128)} fusion(f32[2048,1024]{1,0:T(8,128)} %get-tuple-element.1063, s32[]{:T(128)S(6)} %select_n.198, bf16[1024,128]{1,0:T(8,128)(2,1)} %get-tuple-element.1087, f32[2048,1024]{1,0:T(8,128)} %fusion.104, f32[2048]{0:T(1024)} %get-tuple-element.991, f32[2048]{0:T(1024)} %bitcast.76, ...), kind=kOutput, calls=%fused_computation.23.clone.1 | convolution fusion | flops 826277888 | bytes 10524160 | tf_op jit(solution)/shard_map/while/body/eval_jaxpr/dot_general | solution.py:133
  244.7 5.5 fusion.104
  250.2 8.4 %convolution_dynamic-update-slice_fusion.2 = f32[2048,1024]{1,0:T(8,128)} fusion(f32[2048,1024]{1,0:T(8,128)} %get-tuple-element.1063, s32[]{:T(128)S(6)} %select_n.198, bf16[1024,128]{1,0:T(8,128)(2,1)} %get-tuple-element.1087, f32[2048,1024]{1,0:T(8,128)} %fusion.104, f32[2048]{0:T(1024)} %get-tuple-element.991, f32[2048]{0:T(1024)} %bitcast.76, ...), kind=kOutput, calls=%fused_computation.23.clone.1 | convolution fusion | flops 826277888 | bytes 10524160 | tf_op jit(solution)/shard_map/while/body/eval_jaxpr/dot_general | solution.py:133
  260.6 5.5 fusion.104
  266.1 8.5 %convolution_dynamic-update-slice_fusion.2 = f32[2048,1024]{1,0:T(8,128)} fusion(f32[2048,1024]{1,0:T(8,128)} %get-tuple-element.1063, s32[]{:T(128)S(6)} %select_n.198, bf16[1024,128]{1,0:T(8,128)(2,1)} %get-tuple-element.1087, f32[2048,1024]{1,0:T(8,128)} %fusion.104, f32[2048]{0:T(1024)} %get-tuple-element.991, f32[2048]{0:T(1024)} %bitcast.76, ...), kind=kOutput, calls=%fused_computation.23.clone.1 | convolution fusion | flops 826277888 | bytes 10524160 | tf_op jit(solution)/shard_map/while/body/eval_jaxpr/dot_general | solution.py:133
  282.1 8.5 %convolution_dynamic-update-slice_fusion.2 = f32[2048,1024]{1,0:T(8,128)} fusion(f32[2048,1024]{1,0:T(8,128)} %get-tuple-element.1063, s32[]{:T(128)S(6)} %select_n.198, bf16[1024,128]{1,0:T(8,128)(2,1)} %get-tuple-element.1087, f32[2048,1024]{1,0:T(8,128)} %fusion.104, f32[2048]{0:T(1024)} %get-tuple-element.991, f32[2048]{0:T(1024)} %bitcast.76, ...), kind=kOutput, calls=%fused_computation.23.clone.1 | convolution fusion | flops 826277888 | bytes 10524160 | tf_op jit(solution)/shard_map/while/body/eval_jaxpr/dot_general | solution.py:133
  298.0 8.5 %convolution_dynamic-update-slice_fusion.2 = f32[2048,1024]{1,0:T(8,128)} fusion(f32[2048,1024]{1,0:T(8,128)} %get-tuple-element.1063, s32[]{:T(128)S(6)} %select_n.198, bf16[1024,128]{1,0:T(8,128)(2,1)} %get-tuple-element.1087, f32[2048,1024]{1,0:T(8,128)} %fusion.104, f32[2048]{0:T(1024)} %get-tuple-element.991, f32[2048]{0:T(1024)} %bitcast.76, ...), kind=kOutput, calls=%fused_computation.23.clone.1 | convolution fusion | flops 826277888 | bytes 10524160 | tf_op jit(solution)/shard_map/while/body/eval_jaxpr/dot_general | solution.py:133
  308.5 5.5 fusion.104
  314.0 8.5 %convolution_dynamic-update-slice_fusion.2 = f32[2048,1024]{1,0:T(8,128)} fusion(f32[2048,1024]{1,0:T(8,128)} %get-tuple-element.1063, s32[]{:T(128)S(6)} %select_n.198, bf16[1024,128]{1,0:T(8,128)(2,1)} %get-tuple-element.1087, f32[2048,1024]{1,0:T(8,128)} %fusion.104, f32[2048]{0:T(1024)} %get-tuple-element.991, f32[2048]{0:T(1024)} %bitcast.76, ...), kind=kOutput, calls=%fused_computation.23.clone.1 | convolution fusion | flops 826277888 | bytes 10524160 | tf_op jit(solution)/shard_map/while/body/eval_jaxpr/dot_general | solution.py:133
  324.4 5.5 fusion.104
  330.0 8.5 %convolution_dynamic-update-slice_fusion.2 = f32[2048,1024]{1,0:T(8,128)} fusion(f32[2048,1024]{1,0:T(8,128)} %get-tuple-element.1063, s32[]{:T(128)S(6)} %select_n.198, bf16[1024,128]{1,0:T(8,128)(2,1)} %get-tuple-element.1087, f32[2048,1024]{1,0:T(8,128)} %fusion.104, f32[2048]{0:T(1024)} %get-tuple-element.991, f32[2048]{0:T(1024)} %bitcast.76, ...), kind=kOutput, calls=%fused_computation.23.clone.1 | convolution fusion | flops 826277888 | bytes 10524160 | tf_op jit(solution)/shard_map/while/body/eval_jaxpr/dot_general | solution.py:133
  338.4 105.3 %all-reduce.1 = bf16[2048,1024]{1,0:T(8,128)(2,1)} all-reduce(f32[2048,1024]{1,0:T(8,128)} %get-tuple-element.573), channel_id=1, replica_groups=mesh['qrow'=8,'kcol'=16] {'kcol'}, use_global_device_ids=true, to_apply=%region_8.9 | all-reduce | flops 2097152 | bytes 12582912 | tf_op jit(solution)/shard_map/psum | solution.py:139
  447.9 114.2 %while.50 = (s32[]{:T(128)}, f32[2048,512]{0,1:T(8,128)}, f32[1024,512]{0,1:T(8,128)}, bf16[2048,1024]{1,0:T(8,128)(2,1)}, bf16[1024,128]{1,0:T(8,128)(2,1)S(1)}...) while((s32[]{:T(128)}, f32[2048,512]{0,1:T(8,128)}, ...), condition=%wide.region_10.11_spmd.clone.clone, body=%wide.region_9.10_spmd.clone.clone.sunk | while | flops 1908618240 | bytes 51228120 | solution.py:161
  451.8 6.3 fusion.120
  466.0 6.3 fusion.120
  480.3 6.3 fusion.120
  494.6 6.3 fusion.120
  508.9 6.3 fusion.120
  523.2 6.3 fusion.120
  537.5 6.3 fusion.120
  551.7 6.2 fusion.120
  572.4 28.5 %all_to_all.16 = f32[8,128,512]{1,2,0:T(8,128)S(1)} all-to-all(f32[8,128,512]{1,2,0:T(8,128)} %copy.19), channel_id=1, replica_groups=mesh['qrow'=8,'kcol'=16] {'qrow'}, dimensions={0} | all-to-all | bytes 4194304 | tf_op jit(solution)/shard_map/all_to_all | solution.py:41
  601.9 45.2 %reduce-scatter.2.cloned.1.call-done = f32[128,512]{1,0:T(8,128)} async-done(((f32[2048,512]{1,0:T(8,128)}), f32[128,512]{1,0:T(8,128)}) %reduce-scatter.2.cloned.1.call-update) | async-done | bytes 262160 | tf_op jit(solution)/shard_map/reduce_scatter | solution.py:162
  (191 shorter events, 171.1 us)
Async XLA Ops:
  7.2 45.6 %all-gather.5.cloned.1.call-start = ((), (), s32[]{:S(2)}) async-start(), calls=%async_computation.5 | async-start | bytes 1769472 | tf_op jit(solution)/shard_map/all_gather | solution.py:14
  8.9 109.5 %all-gather.3.cloned.1.call-start = ((), (), s32[]{:S(2)}) async-start(), calls=%async_computation.4 | async-start | bytes 6684672 | tf_op jit(solution)/shard_map/all_gather | solution.py:14
  182.9 22.3 %all-to-all-start.1 = ((f32[16,2048,8]{1,2,0:T(8,128)}), f32[16,2048,8]{1,2,0:T(8,128)}, u32[]{:S(2)}, u32[]{:S(2)}) async-start(f32[16,2048,8]{1,2,0:T(8,128)} %broadcast_in_dim.83), calls=%async_computation.1 | async-start | bytes 2097152 | tf_op jit(solution)/shard_map/all_to_all | solution.py:20
  187.3 23.5 %slice-start = ((bf16[2048,1536]{1,0:T(8,128)(2,1)}), bf16[2048,512]{1,0:T(8,128)(2,1)S(1)}, s32[]{:S(2)}) async-start(bf16[2048,1536]{1,0:T(8,128)(2,1)} %all-gather.3.cloned.1.call-done), calls=%async_computation.7 | async-start | bytes 4194304 | tf_op jit(solution)/shard_map/split | solution.py:15
  187.3 23.5 %slice-start.1 = ((bf16[1024,768]{1,0:T(8,128)(2,1)}), bf16[1024,512]{1,0:T(8,128)(2,1)S(1)}, s32[]{:S(2)}) async-start(bf16[1024,768]{1,0:T(8,128)(2,1)} %all-gather.5.cloned.1.call-done), calls=%async_computation.8 | async-start | bytes 2097152 | tf_op jit(solution)/shard_map/split | solution.py:15
  187.3 459.8 %reduce-scatter.2.cloned.1.call-start = ((), (), s32[]{:S(2)}) async-start(), calls=%async_computation.6 | async-start | bytes 4456448 | tf_op jit(solution)/shard_map/reduce_scatter | solution.py:162
  450.4 1.4 copy-start.1
  464.7 1.4 copy-start.1
  479.0 1.4 copy-start.1
  493.3 1.3 copy-start.1
  507.6 1.4 copy-start.1
  521.8 1.4 copy-start.1
  536.1 1.4 copy-start.1
  550.4 1.4 copy-start.1
  562.1 5.5 copy-start
Sparse Core Ops, SparseCore 0:
  10.2 42.5 all-gather.4
  55.2 63.0 all-gather.2
  567.7 79.3 reduce-scatter.1
where the time goes:
time: 656 us; the launch traced here: 654 us
  matrix products  243 us (37%)
  waiting for transfers between devices  167 us (25%)
  blocking collectives  150 us (23%)
  other arithmetic  38.7 us (6%)
  local copies, waits for them, and re-layouts  36.1 us (6%)
  between operations  13.9 us (2%)
    dot_general x40, matrix products, contract_last(): lax.dot_general(left, right, (((1,), (1,)), ((), ())), preferred_element_...  142 us
    psum x1, blocking collectives, per_device(): mixed_b = lax.psum(mixed, 'kcol').astype(jnp.bfloat16)  105 us
    all_gather x2, waiting for transfers between devices, in_one_piece(): whole = lax.all_gather(both, axis, axis=dim, tiled=True)  104 us
    dot_general x8, matrix products, mixing_head(): jnp.dot(error.astype(jnp.bfloat16), v_tile, preferred_element_type=jnp.fl...  67.8 us
    reduce_scatter x1, waiting for transfers between devices, per_device(): lax.psum_scatter(q_grads, 'kcol', scatter_dimension=0, tiled=True)  45.2 us
    all_to_all x1, blocking collectives, sum_at_owner(): lax.all_to_all(parts, axis, split_axis=0, concat_axis=0, tiled=True)  28.5 us
    reduce_sum x8, other arithmetic, local_stats(): jnp.sum(jnp.where(allowed, jnp.exp(scores - highest[:, None]), 0.0), axis=1)  19.3 us
    dot_general x8, matrix products, grad_head(): q_part = -jnp.dot(weights, kf_head, preferred_element_type=jnp.float32)  18.2 us
  transfers between devices with their start and end apart: 4, of which 4 were waited for; matrix products, arithmetic and copies ran while one was open for 2% of the time, Pallas kernels for 0%

commit v1 on v0

v1 whole, which is shorter than its diff:
```python
import math

import jax
import jax.numpy as jnp
from jax import lax
from jax.experimental import pallas as pl
from jax.experimental.pallas import tpu as pltpu
from jax.sharding import Mesh, PartitionSpec as P

FLOOR = -1e30
LOW = -1e29
F32 = jnp.float32
BF16 = jnp.bfloat16
HEADS = ("zl", "y")
COLS = ("zh", "x")
BLK = 128
GROUPS = 8
COLUMNS = 8
HD = 128
FD = 64
TR = 2 * BLK
TK = COLUMNS * BLK
VROWS = 208
KEY_SCALE = 1.0 / math.sqrt(HD)
FEAT_SCALE = 1.0 / math.sqrt(FD)
SCORE = KEY_SCALE * math.log2(math.e)


def nn(a, b):
    return lax.dot_general(a, b, (((1,), (0,)), ((), ())), preferred_element_type=F32)


def nt(a, b):
    return lax.dot_general(a, b, (((1,), (1,)), ((), ())), preferred_element_type=F32)


def tn(a, b):
    return lax.dot_general(a, b, (((0,), (0,)), ((), ())), preferred_element_type=F32)


def split(a):
    high = a.astype(BF16)
    return high, (a - high.astype(F32)).astype(BF16)


def iota(shape, dim):
    return lax.broadcasted_iota(jnp.int32, shape, dim)


def row_positions(rows_at, k):
    lane = iota((1, TR), 1)
    first = rows_at[2 * k] * BLK
    second = rows_at[2 * k + 1] * BLK - BLK
    return lane + jnp.where(lane < BLK, first, second)


def tile_mask(rows_at, keys_at, k):
    pos_rows = row_positions(rows_at, k)
    step = iota((BLK, 1), 0)
    parts = [pos_rows >= step + keys_at[COLUMNS * k + j] * BLK for j in range(COLUMNS)]
    return jnp.concatenate(parts, axis=0)


def load_rows(core, own, other, q_buf, qf_buf):
    for ref, slot in ((own, core[0]), (other, 1 - core[0])):
        at = pl.ds(pl.multiple_of(slot * BLK, BLK), BLK)
        for k in range(GROUPS):
            q_buf[k, at, :] = ref[k * BLK : (k + 1) * BLK, :]
            base = GROUPS * BLK + (k % 4) * BLK
            lanes = slice(0, FD) if k < 4 else slice(FD, 2 * FD)
            qf_buf[k, at, :] = ref[base : base + BLK, lanes]


def key_feats(slab, k):
    base = 2 * GROUPS * BLK + (k % 4) * BLK
    lanes = slice(0, FD) if k < 4 else slice(FD, 2 * FD)
    return slab[base : base + BLK, lanes]


def forward_kernel(rows_at, keys_at, core, own, other, *rest):
    slabs = rest[:COLUMNS]
    pack, okf, states, k_buf, kf_buf, vft, q_buf, qf_buf, acc, state = rest[COLUMNS:]
    load_rows(core, own, other, q_buf, qf_buf)
    for k in range(GROUPS):
        for j, slab in enumerate(slabs):
            at = slice(j * BLK, (j + 1) * BLK)
            feats = key_feats(slab, k)
            k_buf[k, at, :] = slab[k * BLK : (k + 1) * BLK, :]
            kf_buf[k, at, :] = feats
            v_at = GROUPS * BLK + k * BLK
            vft[k, :HD, at] = slab[v_at : v_at + BLK, :].T
            vft[k, HD : HD + FD, at] = feats.T
        tail = iota((VROWS - HD - FD, TK), 0)
        vft[k, HD + FD :, :] = jnp.where(tail == 0, 1.0, 0.0).astype(BF16)
    state[...] = jnp.zeros_like(state)

    def group(k, carry):
        acc[...] = jnp.zeros_like(acc)

        def add(kp, t, m):
            m_new = jnp.maximum(m, jnp.max(t, axis=0, keepdims=True))
            p = jnp.exp2(t - m_new).astype(BF16)
            acc[...] = acc[...] * jnp.exp2(m - m_new) + nn(vft[kp], p)
            return m_new

        def full(kp, m):
            return add(kp, nt(k_buf[kp], q_buf[k]) * SCORE, m)

        m = lax.fori_loop(0, k, full, jnp.full((1, TR), LOW, F32))
        mask = tile_mask(rows_at, keys_at, k)
        m = add(k, jnp.where(mask, nt(k_buf[k], q_buf[k]) * SCORE, FLOOR), m)
        inv_n = FEAT_SCALE / (row_positions(rows_at, k) + 1).astype(F32)
        student = jnp.where(mask, nt(kf_buf[k], qf_buf[k]) * inv_n, 0.0).astype(BF16)
        high, low = split(state[:HD, :])
        linear = nn(vft[k, :HD, :], student) + (nt(high, qf_buf[k]) + nt(low, qf_buf[k])) * inv_n
        pack[k, :HD, :] = acc[:HD, :]
        pack[k, HD : 2 * HD, :] = linear
        pack[k, 2 * HD :, :] = jnp.where(iota((8, TR), 0) == 0, acc[HD + FD : HD + FD + 1, :], m)
        okf[k] = acc[HD : HD + FD, :]
        states[k] = state[...]
        state[...] += nn(vft[k, : HD + FD, :], kf_buf[k])
        return carry

    lax.fori_loop(0, GROUPS, group, 0)


def backward_kernel(rows_at, keys_at, core, own, other, *rest):
    slabs = rest[:COLUMNS]
    mine, theirs, okf, states, dk_out, dq_out = rest[COLUMNS : COLUMNS + 6]
    k_buf, v_buf, kf_buf, kft, q_buf, qf_buf, r_buf, bias, acc, w_state, u_state = rest[COLUMNS + 6 :]
    load_rows(core, own, other, q_buf, qf_buf)
    for k in range(GROUPS):
        for j, slab in enumerate(slabs):
            at = slice(j * BLK, (j + 1) * BLK)
            feats = key_feats(slab, k)
            k_buf[k, at, :] = slab[k * BLK : (k + 1) * BLK, :]
            v_at = GROUPS * BLK + k * BLK
            v_buf[k, at, :] = slab[v_at : v_at + BLK, :]
            kf_buf[k, at, :] = feats
            kft[k, :, at] = feats.T

    def merge(k, carry):
        l0, m0 = mine[k, 2 * HD : 2 * HD + 1, :], mine[k, 2 * HD + 1 : 2 * HD + 2, :]
        l1, m1 = theirs[k, 2 * HD : 2 * HD + 1, :], theirs[k, 2 * HD + 1 : 2 * HD + 2, :]
        top = jnp.maximum(m0, m1)
        w0, w1 = jnp.exp2(m0 - top), jnp.exp2(m1 - top)
        total = l0 * w0 + l1 * w1
        w0, w1 = w0 / total, w1 / total
        mixed = (mine[k, :HD, :] * w0 + theirs[k, :HD, :] * w1) - (
            mine[k, HD : 2 * HD, :] + theirs[k, HD : 2 * HD, :]
        )
        r_buf[k] = mixed.astype(BF16)
        n = (row_positions(rows_at, k) + 1).astype(F32)
        bias[k] = 0.5 * jnp.log2(n) - (top + jnp.log2(total))
        dq_out[k] = okf[k] * (w0 * jnp.sqrt(n))
        return carry

    lax.fori_loop(0, GROUPS, merge, 0)
    w_state[...] = jnp.zeros_like(w_state)
    u_state[...] = jnp.zeros_like(u_state)

    def group(step, carry):
        kp = GROUPS - 1 - step
        w_high, w_low = split(w_state[...])
        u_high, u_low = split(u_state[...])
        v_tile, kf_tile = v_buf[kp], kf_buf[kp]
        acc[...] = (nn(v_tile, w_high) + nn(v_tile, w_low)) - (nn(kf_tile, u_high) + nn(kf_tile, u_low))

        def full(k, c):
            p = jnp.exp2(nt(k_buf[kp], q_buf[k]) * SCORE + bias[k]).astype(BF16)
            acc[...] += nn(p, qf_buf[k])
            return c

        lax.fori_loop(kp + 1, GROUPS, full, 0)
        mask = tile_mask(rows_at, keys_at, kp)
        n = (row_positions(rows_at, kp) + 1).astype(F32)
        weight = FEAT_SCALE / jnp.sqrt(n)
        r_tile, qf_tile = r_buf[kp], qf_buf[kp]
        teacher = jnp.where(mask, nt(k_buf[kp], q_buf[kp]) * SCORE + bias[kp], FLOOR)
        linear = nn(v_tile, r_tile) * KEY_SCALE - nt(kf_tile, qf_tile) * weight
        linear = jnp.where(mask, linear, 0.0)
        g = (jnp.exp2(teacher) + linear).astype(BF16)
        acc[...] += nn(g, qf_tile)
        s_high, s_low = split(states[kp])
        query = tn(s_high[:HD], r_tile) + tn(s_low[:HD], r_tile)
        student = nt(s_high[HD:], qf_tile) + nt(s_low[HD:], qf_tile)
        query = query * KEY_SCALE - student * weight + nn(kft[kp], linear.astype(BF16))
        dq_out[kp] = -(dq_out[kp] + query)
        w_state[...] += nn(r_tile, qf_tile) * KEY_SCALE
        f_high, f_low = split(qf_tile.astype(F32).T * weight)
        u_state[...] += nn(f_high, qf_tile) + nn(f_low, qf_tile)
        result = -acc[...]
        half = kp // 4
        row = pl.ds(pl.multiple_of((kp % 4) * BLK, BLK), BLK)

        @pl.when(half == 0)
        def _():
            for j in range(COLUMNS):
                dk_out[j, row, :FD] = result[j * BLK : (j + 1) * BLK, :]

        @pl.when(half == 1)
        def _():
            for j in range(COLUMNS):
                dk_out[j, row, FD:] = result[j * BLK : (j + 1) * BLK, :]

        return carry

    lax.fori_loop(0, GROUPS, group, 0)


def on_chip(count_smem, count_vmem):
    smem = [pl.BlockSpec(memory_space=pltpu.SMEM)] * count_smem
    return smem + [pl.BlockSpec(memory_space=pltpu.VMEM)] * count_vmem


def forward(rows_at, keys_at, core, own, other, slabs):
    return pl.pallas_call(
        forward_kernel,
        out_shape=(
            jax.ShapeDtypeStruct((GROUPS, 2 * HD + 8, TR), F32),
            jax.ShapeDtypeStruct((GROUPS, FD, TR), F32),
            jax.ShapeDtypeStruct((GROUPS, HD + FD, FD), F32),
        ),
        in_specs=on_chip(3, 2 + COLUMNS),
        out_specs=[pl.BlockSpec(memory_space=pltpu.VMEM)] * 3,
        scratch_shapes=[
            pltpu.VMEM((GROUPS, TK, HD), BF16),
            pltpu.VMEM((GROUPS, TK, FD), BF16),
            pltpu.VMEM((GROUPS, VROWS, TK), BF16),
            pltpu.VMEM((GROUPS, TR, HD), BF16),
            pltpu.VMEM((GROUPS, TR, FD), BF16),
            pltpu.VMEM((VROWS, TR), F32),
            pltpu.VMEM((HD + FD, FD), F32),
        ],
        name="forward",
    )(rows_at, keys_at, core, own, other, *slabs)


def backward(rows_at, keys_at, core, own, other, slabs, mine, theirs, okf, states):
    return pl.pallas_call(
        backward_kernel,
        out_shape=(
            jax.ShapeDtypeStruct((COLUMNS, 4 * BLK, 2 * FD), F32),
            jax.ShapeDtypeStruct((GROUPS, FD, TR), F32),
        ),
        in_specs=on_chip(3, 6 + COLUMNS),
        out_specs=[pl.BlockSpec(memory_space=pltpu.VMEM)] * 2,
        scratch_shapes=[
            pltpu.VMEM((GROUPS, TK, HD), BF16),
            pltpu.VMEM((GROUPS, TK, HD), BF16),
            pltpu.VMEM((GROUPS, TK, FD), BF16),
            pltpu.VMEM((GROUPS, FD, TK), BF16),
            pltpu.VMEM((GROUPS, TR, HD), BF16),
            pltpu.VMEM((GROUPS, TR, FD), BF16),
            pltpu.VMEM((GROUPS, HD, TR), BF16),
            pltpu.VMEM((GROUPS, 1, TR), F32),
            pltpu.VMEM((TK, FD), F32),
            pltpu.VMEM((HD, FD), F32),
            pltpu.VMEM((FD, FD), F32),
        ],
        name="backward",
    )(rows_at, keys_at, core, own, other, *slabs, mine, theirs, okf, states)


def shifted(a, step):
    return lax.ppermute(a, "x", [(i, (i + step) % 4) for i in range(4)])


def across(a, axis):
    return lax.ppermute(a, axis, [(0, 1), (1, 0)])


def pair_up(a):
    return jnp.concatenate([a[:4], a[4:]], axis=-1).reshape(4 * BLK, 2 * FD)


def per_device(queries, keys, values, query_feats, key_feats_in, block_pos):
    q_heads = queries.reshape(BLK, GROUPS, HD).transpose(1, 0, 2)
    feats = jnp.concatenate(
        [key_feats_in.reshape(BLK, GROUPS, FD), query_feats.reshape(BLK, GROUPS, FD)], axis=-1
    ).transpose(1, 0, 2)
    shared = jnp.broadcast_to(jnp.concatenate([keys, values], axis=0)[None], (GROUPS, 2 * BLK, HD))
    sent = jnp.concatenate([q_heads, shared, feats], axis=1)
    got = lax.all_to_all(sent, HEADS, 0, 0, tiled=True)
    own = jnp.concatenate([got[:, :BLK].reshape(-1, HD), pair_up(got[:, 3 * BLK :, FD:])], axis=0)
    slab = jnp.concatenate(
        [
            got[:, BLK : 2 * BLK].reshape(-1, HD),
            got[:, 2 * BLK : 3 * BLK].reshape(-1, HD),
            pair_up(got[:, 3 * BLK :, :FD]),
        ],
        axis=0,
    )
    other = across(own, "c")
    far = across(slab, "zh")
    left, right = shifted(slab, 1), shifted(slab, 3)
    far_left, far_right = shifted(far, 1), shifted(far, 3)
    half = slab.shape[0] // 2
    behind = jnp.concatenate([shifted(left[:half], 1), shifted(right[half:], 3)], axis=0)
    far_behind = jnp.concatenate([shifted(far_left[:half], 1), shifted(far_right[half:], 3)], axis=0)
    slabs = (slab, far, left, right, far_left, far_right, behind, far_behind)

    zh, x, c = lax.axis_index("zh"), lax.axis_index("x"), lax.axis_index("c")
    grid = block_pos.reshape(GROUPS, 2, 4, 2)
    fz = 1 - zh
    xl, xr, xb = (x + 3) % 4, (x + 1) % 4, (x + 2) % 4
    z_at = jnp.stack([zh, fz, zh, zh, fz, fz, zh, fz])
    x_at = jnp.stack([x, x, xl, xr, xl, xr, xb, xb])
    flat = grid.reshape(GROUPS, 16)
    keys_at = jnp.take(flat, z_at * 8 + x_at * 2 + c, axis=1).reshape(-1)
    rows_at = lax.dynamic_slice_in_dim(flat, zh * 8 + x * 2, 2, 1).reshape(-1)
    core = c.reshape(1).astype(jnp.int32)

    mine, okf, states = forward(rows_at, keys_at, core, own, other, slabs)
    theirs = across(mine, "c")
    dk, dq = backward(rows_at, keys_at, core, own, other, slabs, mine, theirs, okf, states)

    order = z_at * 4 + x_at
    dk = jnp.take(dk, jnp.argsort(order), axis=0)
    dk = lax.all_to_all(dk, COLS, 0, 0, tiled=True).sum(axis=0)
    dk = dk.reshape(4, BLK, 2, FD).transpose(2, 0, 1, 3).reshape(GROUPS, BLK, FD)
    dq = dq.reshape(GROUPS, FD, 2, BLK)
    keep = lax.dynamic_slice_in_dim(dq, c, 1, 2)
    give = lax.dynamic_slice_in_dim(dq, 1 - c, 1, 2)
    dq = (keep + across(give, "c"))[:, :, 0].transpose(0, 2, 1)
    final = lax.all_to_all(jnp.concatenate([dq, dk], axis=-1), HEADS, 0, 0, tiled=True)
    final = final.transpose(1, 0, 2)
    return final[:, :, :FD].reshape(BLK, -1), final[:, :, FD:].reshape(BLK, -1)


def solution(mesh):
    split_mesh = Mesh(mesh.devices.reshape(2, 4, 2, 4, 2), ("zl", "y", "zh", "x", "c"))
    spec = P(("zl", "y", "zh", "x", "c"), None)
    return jax.shard_map(
        per_device,
        mesh=split_mesh,
        in_specs=(spec,) * 5 + (P(),),
        out_specs=(spec, spec),
        check_vma=False,
    )
```

time: 656 us -> 223 us (0.34)
  matrix products: 243 us -> 0 us
  blocking collectives: 150 us -> 12.7 us
  waiting for transfers between devices: 167 us -> 77.2 us
  Pallas kernels: 0 us -> 81.2 us
  other arithmetic: 38.7 us -> 6.89 us
  starting transfers between devices: 4.46 us -> 28.5 us
  local copies, waits for them, and re-layouts: 36.1 us -> 15.2 us
  between operations: 13.9 us -> 1.03 us
    dot_general x64 -> x0, matrix products: 243 us -> none  [the longest x40 142 us: contract_last(): lax.dot_general(left, right, (((1,), (1,)), ((), ())), preferred_element_...]
    psum x1 -> x0, blocking collectives: 105 us -> none  [per_device(): mixed_b = lax.psum(mixed, 'kcol').astype(jnp.bfloat16)]
    all_gather x2 -> x0, waiting for transfers between devices: 104 us -> none  [in_one_piece(): whole = lax.all_gather(both, axis, axis=dim, tiled=True)]
    pallas_call x0 -> x2, Pallas kernels: none -> 81.2 us  [the longest x1 43.6 us: forward(): pl.pallas_call(forward_kernel, out_shape=(jax.ShapeDtypeStruct((GROUPS, 2...]
    reduce_scatter x1 -> x0, waiting for transfers between devices: 45.2 us -> none  [per_device(): lax.psum_scatter(q_grads, 'kcol', scatter_dimension=0, tiled=True)]
    ppermute x0 -> x12, waiting for transfers between devices: none -> 35.4 us  [the longest x8 19.9 us: shifted(): return lax.ppermute(a, 'x', [(i, (i + step) % 4) for i in range(4)])]
    all_to_all x2 -> x1, blocking collectives: 44.3 us -> 12.7 us  [per_device(): lax.all_to_all(jnp.concatenate([dq, dk], axis=-1), HEADS, 0, 0, tiled=True)]
    all_to_all x1 -> x2, waiting for transfers between devices: 17.9 us -> 41.7 us  [the longest x1 26.2 us: per_device(): dk = lax.all_to_all(dk, COLS, 0, 0, tiled=True).sum(axis=0)]
  transfers between devices with their start and end apart: 4 -> 14, of which waited for: 4 -> 9; matrix products, arithmetic and copies ran while one was open for 2% -> 4% of each run, Pallas kernels for 0% -> 0%
where the time goes in v1:
time: 223 us
  Pallas kernels  81.2 us (36%)
  waiting for transfers between devices  77.2 us (35%)
  starting transfers between devices  28.5 us (13%)
  local copies, waits for them, and re-layouts  15.2 us (7%)
  blocking collectives  12.7 us (6%)
  other arithmetic  6.89 us (3%)
    pallas_call x1, Pallas kernels, forward(): pl.pallas_call(forward_kernel, out_shape=(jax.ShapeDtypeStruct((GROUPS, 2...  43.6 us
    pallas_call x1, Pallas kernels, backward(): pl.pallas_call(backward_kernel, out_shape=(jax.ShapeDtypeStruct((COLUMNS,...  37.6 us
    all_to_all x1, waiting for transfers between devices, per_device(): dk = lax.all_to_all(dk, COLS, 0, 0, tiled=True).sum(axis=0)  26.2 us
    ppermute x8, waiting for transfers between devices, shifted(): return lax.ppermute(a, 'x', [(i, (i + step) % 4) for i in range(4)])  19.9 us
    all_to_all x1, waiting for transfers between devices, per_device(): got = lax.all_to_all(sent, HEADS, 0, 0, tiled=True)  15.5 us
    ppermute x4, waiting for transfers between devices, across(): return lax.ppermute(a, axis, [(0, 1), (1, 0)])  15.5 us
    all_to_all x1, blocking collectives, per_device(): lax.all_to_all(jnp.concatenate([dq, dk], axis=-1), HEADS, 0, 0, tiled=True)  12.7 us
    ppermute x8, starting transfers between devices, shifted(): return lax.ppermute(a, 'x', [(i, (i + step) % 4) for i in range(4)])  11.9 us
  transfers between devices with their start and end apart: 14, of which 9 were waited for; matrix products, arithmetic and copies ran while one was open for 4% of the time, Pallas kernels for 0%

profile of v1, /device:TPU:0, one launch (start us, length us, event | category | flops | bytes accessed | tf_op | source)
XLA Modules:
  0.0 222.7 jit_solution(10687612804518907208)
XLA Ops:
  0.7 1.1 copy.39
  1.7 1.0 copy.40
  3.2 1.1 pad_maximum_fusion
  4.2 5.9 %all-to-all-start = ((bf16[8,512,128]{2,1,0:T(8,128)(2,1)}), bf16[8,512,128]{2,1,0:T(8,128)(2,1)S(1)}, u32[]{:S(2)}, u32[]{:S(2)}) async-start(bf16[8,512,128]{2,1,0:T(8,128)(2,1)} %pad_maximum_fusion), calls=%async_computation | async-start | bytes 2097152 | tf_op jit(solution)/shard_map/all_to_all | solution.py:284
  10.3 15.5 %all-to-all-done = bf16[8,512,128]{2,1,0:T(8,128)(2,1)S(1)} async-done(((bf16[8,512,128]{2,1,0:T(8,128)(2,1)}), bf16[8,512,128]{2,1,0:T(8,128)(2,1)S(1)}, u32[]{:S(2)}, u32[]{:S(2)}) %all-to-all-start) | async-done | bytes 1048608 | tf_op jit(solution)/shard_map/all_to_all | solution.py:284
  27.6 3.7 %collective-permute-start.1 = (bf16[2560,128]{1,0:T(8,128)(2,1)S(1)}, bf16[2560,128]{1,0:T(8,128)(2,1)}, u32[]{:S(2)}, u32[]{:S(2)}) collective-permute-start(bf16[2560,128]{1,0:T(8,128)(2,1)S(1)} %pad_maximum_fusion.1.rest_0_), channel_id=1, source_target_pairs={{0,8},{8,0},{1,9},{9,1},{2,10},{10,2},{3,11},{11,3},{4,12},{12,4},... | collective-permute-start | bytes 1966088 | tf_op jit(solution)/shard_map/ppermute | solution.py:270
  31.3 1.0 sort.17
  32.2 1.5 collective-permute-start.2
  34.6 1.8 collective-permute-start.3
  36.4 9.6 %collective-permute-done.1.rest_1_ = bf16[2560,128]{1,0:T(8,128)(2,1)} collective-permute-done((bf16[2560,128]{1,0:T(8,128)(2,1)S(1)}, bf16[2560,128]{1,0:T(8,128)(2,1)}, u32[]{:S(2)}, u32[]{:S(2)}) %collective-permute-start.1) | collective-permute-done | bytes 655392 | tf_op jit(solution)/shard_map/ppermute | solution.py:270
  46.0 1.5 collective-permute-start.4
  48.1 1.8 collective-permute-start.5
  53.1 3.0 %collective-permute-start.7 = (bf16[1280,128]{1,0:T(8,128)(2,1)S(1)}, bf16[1280,128]{1,0:T(8,128)(2,1)S(1)}, u32[]{:S(2)}, u32[]{:S(2)}) collective-permute-start(bf16[1280,128]{1,0:T(8,128)(2,1)S(1)} %slice.70), channel_id=1, source_target_pairs={{0,6},{2,0},{4,2},{6,4},{1,7},{3,1},{5,3},{7,5},{8,14},{10,8},{12,... | collective-permute-start | bytes 983048 | tf_op jit(solution)/shard_map/ppermute | solution.py:266
  56.1 1.0 pad_maximum_fusion.3.own
  57.3 7.7 %collective-permute-done.4.rest_4_ = bf16[2560,128]{1,0:T(8,128)(2,1)S(1)} collective-permute-done((bf16[2560,128]{1,0:T(8,128)(2,1)}, bf16[2560,128]{1,0:T(8,128)(2,1)S(1)}, u32[]{:S(2)}, u32[]{:S(2)}) %collective-permute-start.4) | collective-permute-done | bytes 655392 | tf_op jit(solution)/shard_map/ppermute | solution.py:266
  65.4 6.7 %collective-permute-done.6 = bf16[1280,128]{1,0:T(8,128)(2,1)} collective-permute-done((bf16[1280,128]{1,0:T(8,128)(2,1)}, bf16[1280,128]{1,0:T(8,128)(2,1)}, u32[]{:S(2)}, u32[]{:S(2)}) %collective-permute-start.6) | collective-permute-done | bytes 327712 | tf_op jit(solution)/shard_map/ppermute | solution.py:266
  72.2 1.0 constant_dynamic-update-slice_fusion.1
  73.2 1.6 collective-permute-start.9
  74.9 2.7 %collective-permute-done.8 = bf16[1280,128]{1,0:T(8,128)(2,1)S(1)} collective-permute-done((bf16[1280,128]{1,0:T(8,128)(2,1)S(1)}, bf16[1280,128]{1,0:T(8,128)(2,1)S(1)}, u32[]{:S(2)}, u32[]{:S(2)}) %collective-permute-start.8) | collective-permute-done | bytes 327712 | tf_op jit(solution)/shard_map/ppermute | solution.py:266
  77.7 2.7 %collective-permute-done.9 = bf16[1280,128]{1,0:T(8,128)(2,1)S(1)} collective-permute-done((bf16[1280,128]{1,0:T(8,128)(2,1)S(1)}, bf16[1280,128]{1,0:T(8,128)(2,1)S(1)}, u32[]{:S(2)}, u32[]{:S(2)}) %collective-permute-start.9) | collective-permute-done | bytes 327712 | tf_op jit(solution)/shard_map/ppermute | solution.py:266
  81.4 43.6 %forward.1 = (f32[8,264,256]{2,1,0:T(8,128)}, f32[8,64,256]{2,1,0:T(8,128)}, f32[8,192,64]{2,1,0:T(8,128)}) custom-call(s32[16]{0:T(128)} %reshape.373.rows_at, s32[64]{0:T(128)} %select_n.63.keys_at, s32[1]{0:T(128)} %bitcast.14.core, bf16[1536,128]{1,0:T(8,128)(2,1)} %copy-done.8, bf16[1536,128]{1,0:T(8,128)(2,1)} %copy-done.10, ...), custom_call_target="tpu_custom_call" | custom-call | tf_op jit(solution)/shard_map/forward/pallas_call | solution.py:217
  125.0 4.4 %collective-permute-done.10.rest_9_ = f32[8,264,256]{2,1,0:T(8,128)S(1)} collective-permute-done((f32[8,264,256]{2,1,0:T(8,128)}, f32[8,264,256]{2,1,0:T(8,128)S(1)}, u32[]{:S(2)}, u32[]{:S(2)}) %collective-permute-start.10) | collective-permute-done | bytes 2162720 | tf_op jit(solution)/shard_map/ppermute | solution.py:270
  129.5 1.3 copy-done.9
  130.8 37.6 %backward.1 = (f32[8,512,128]{2,1,0:T(8,128)}, f32[8,64,256]{2,1,0:T(8,128)}) custom-call(s32[16]{0:T(128)} %reshape.373.rows_at, s32[64]{0:T(128)} %select_n.63.keys_at, s32[1]{0:T(128)} %bitcast.14.core, bf16[1536,128]{1,0:T(8,128)(2,1)} %copy-done.8, bf16[1536,128]{1,0:T(8,128)(2,1)} %copy-done.10, bf16[2560,128]{1,0:T(8,128)(2,1)} %copy-done.1, ...), custom_call_target="tpu_custom_call" | custom-call | tf_op jit(solution)/shard_map/backward/pallas_call | solution.py:240
  168.4 2.3 %gather_fusion.1 = f32[8,512,128]{2,1,0:T(8,128)S(1)} fusion(f32[8,512,128]{2,1,0:T(8,128)} %get-tuple-element.13, s32[1024]{0:T(1024)S(1)} %pad_clamp_fusion), kind=kCustom, calls=%fused_computation.1 | custom fusion | bytes 4194336 | tf_op jit(solution)/shard_map/jit(_take)/gather | solution.py:319
  170.7 1.6 broadcast_select_fusion
  172.3 6.8 %all-to-all-start.1 = ((f32[8,512,128]{2,1,0:T(8,128)}), f32[8,512,128]{2,1,0:T(8,128)S(1)}, u32[]{:S(2)}, u32[]{:S(2)}) async-start(f32[8,512,128]{2,1,0:T(8,128)} %broadcast_select_fusion), calls=%async_computation.1 | async-start | bytes 4194304 | tf_op jit(solution)/shard_map/all_to_all | solution.py:320
  180.1 1.5 collective-permute-done.11
  181.6 26.2 %all-to-all-done.1 = f32[8,512,128]{2,1,0:T(8,128)S(1)} async-done(((f32[8,512,128]{2,1,0:T(8,128)}), f32[8,512,128]{2,1,0:T(8,128)S(1)}, u32[]{:S(2)}, u32[]{:S(2)}) %all-to-all-start.1) | async-done | bytes 2097184 | tf_op jit(solution)/shard_map/all_to_all | solution.py:320
  208.3 12.7 %all_to_all.15 = f32[8,128,128]{1,2,0:T(8,128)S(1)} all-to-all(f32[8,128,128]{1,2,0:T(8,128)S(1)} %pad_maximum_fusion.2), channel_id=1, replica_groups=mesh['zl'=2,'y'=4,'zh'=2,'x'=4,'c'=2] {'zl','y'}, dimensions={0} | all-to-all | bytes 1048576 | tf_op jit(solution)/shard_map/all_to_all | solution.py:326
  221.0 0.8 copy.46
  221.8 0.8 copy.47
  (87 shorter events, 9.9 us)
Async XLA Ops:
  0.6 2.3 %copy-start = (bf16[128,1024]{1,0:T(8,128)(2,1)S(1)}, bf16[128,1024]{1,0:T(8,128)(2,1)}, u32[]{:S(2)}) copy-start(bf16[128,1024]{1,0:T(8,128)(2,1)} %param.6) | copy-start | bytes 786436
  0.6 2.4 %copy-start.13 = (bf16[128,128]{1,0:T(8,128)(2,1)S(1)}, bf16[128,128]{1,0:T(8,128)(2,1)}, u32[]{:S(2)}) copy-start(bf16[128,128]{1,0:T(8,128)(2,1)} %param.7) | copy-start | bytes 98308
  0.7 2.4 %copy-start.12 = (bf16[128,128]{1,0:T(8,128)(2,1)S(1)}, bf16[128,128]{1,0:T(8,128)(2,1)}, u32[]{:S(2)}) copy-start(bf16[128,128]{1,0:T(8,128)(2,1)} %param.8) | copy-start | bytes 98308
  4.2 21.6 %all-to-all-start = ((bf16[8,512,128]{2,1,0:T(8,128)(2,1)}), bf16[8,512,128]{2,1,0:T(8,128)(2,1)S(1)}, u32[]{:S(2)}, u32[]{:S(2)}) async-start(bf16[8,512,128]{2,1,0:T(8,128)(2,1)} %pad_maximum_fusion), calls=%async_computation | async-start | bytes 2097152 | tf_op jit(solution)/shard_map/all_to_all | solution.py:284
  26.0 8.3 %copy-start.14 = (s32[128]{0:T(128)S(1)}, s32[128]{0:T(128)}, u32[]{:S(2)}) copy-start(s32[128]{0:T(128)} %param.11) | copy-start | bytes 1540
  27.6 45.6 %copy-start.1 = (bf16[2560,128]{1,0:T(8,128)(2,1)}, bf16[2560,128]{1,0:T(8,128)(2,1)S(1)}, u32[]{:S(2)}) copy-start(bf16[2560,128]{1,0:T(8,128)(2,1)S(1)} %pad_maximum_fusion.1.rest_0_) | copy-start | bytes 1966084
  27.6 18.4 %collective-permute-start.1 = (bf16[2560,128]{1,0:T(8,128)(2,1)S(1)}, bf16[2560,128]{1,0:T(8,128)(2,1)}, u32[]{:S(2)}, u32[]{:S(2)}) collective-permute-start(bf16[2560,128]{1,0:T(8,128)(2,1)S(1)} %pad_maximum_fusion.1.rest_0_), channel_id=1, source_target_pairs={{0,8},{8,0},{1,9},{9,1},{2,10},{10,2},{3,11},{11,3},{4,12},{12,4},... | collective-permute-start | bytes 1966088 | tf_op jit(solution)/shard_map/ppermute | solution.py:270
  32.2 2.4 %copy-start.15 = (s32[8]{0:T(128)}, s32[8]{0:T(128)S(1)}, u32[]{:S(2)}) copy-start(s32[8]{0:T(128)S(1)} %get-tuple-element.12) | copy-start | bytes 100
  32.2 19.0 %collective-permute-start.2 = (bf16[2560,128]{1,0:T(8,128)(2,1)S(1)}, bf16[2560,128]{1,0:T(8,128)(2,1)S(1)}, u32[]{:S(2)}, u32[]{:S(2)}) collective-permute-start(bf16[2560,128]{1,0:T(8,128)(2,1)S(1)} %pad_maximum_fusion.1.rest_0_), channel_id=1, source_target_pairs={{0,2},{2,4},{4,6},{6,0},{1,3},{3,5},{5,7},{7,1},{8,10},{10,12},{12... | collective-permute-start | bytes 1966088 | tf_op jit(solution)/shard_map/ppermute | solution.py:266
  34.6 18.5 %collective-permute-start.3 = (bf16[2560,128]{1,0:T(8,128)(2,1)S(1)}, bf16[2560,128]{1,0:T(8,128)(2,1)S(1)}, u32[]{:S(2)}, u32[]{:S(2)}) collective-permute-start(bf16[2560,128]{1,0:T(8,128)(2,1)S(1)} %pad_maximum_fusion.1.rest_0_), channel_id=1, source_target_pairs={{0,6},{2,0},{4,2},{6,4},{1,7},{3,1},{5,3},{7,5},{8,14},{10,8},{12,... | collective-permute-start | bytes 1966088 | tf_op jit(solution)/shard_map/ppermute | solution.py:266
  46.0 19.0 %collective-permute-start.4 = (bf16[2560,128]{1,0:T(8,128)(2,1)}, bf16[2560,128]{1,0:T(8,128)(2,1)S(1)}, u32[]{:S(2)}, u32[]{:S(2)}) collective-permute-start(bf16[2560,128]{1,0:T(8,128)(2,1)} %collective-permute-done.1.rest_1_), channel_id=1, source_target_pairs={{0,2},{2,4},{4,6},{6,0},{1,3},{3,5},{5,7},{7,1},{8,10},{10,12},{12... | collective-permute-start | bytes 1966088 | tf_op jit(solution)/shard_map/ppermute | solution.py:266
  48.1 25.1 %collective-permute-start.5 = (bf16[2560,128]{1,0:T(8,128)(2,1)}, bf16[2560,128]{1,0:T(8,128)(2,1)S(1)}, u32[]{:S(2)}, u32[]{:S(2)}) collective-permute-start(bf16[2560,128]{1,0:T(8,128)(2,1)} %collective-permute-done.1.rest_1_), channel_id=1, source_target_pairs={{0,6},{2,0},{4,2},{6,4},{1,7},{3,1},{5,3},{7,5},{8,14},{10,8},{12,... | collective-permute-start | bytes 1966088 | tf_op jit(solution)/shard_map/ppermute | solution.py:266
  51.2 23.7 %copy-start.2 = (bf16[2560,128]{1,0:T(8,128)(2,1)}, bf16[2560,128]{1,0:T(8,128)(2,1)S(1)}, u32[]{:S(2)}) copy-start(bf16[2560,128]{1,0:T(8,128)(2,1)S(1)} %collective-permute-done.2.rest_2_) | copy-start | bytes 1966084
  52.1 20.1 %collective-permute-start.6 = (bf16[1280,128]{1,0:T(8,128)(2,1)}, bf16[1280,128]{1,0:T(8,128)(2,1)}, u32[]{:S(2)}, u32[]{:S(2)}) collective-permute-start(bf16[1280,128]{1,0:T(8,128)(2,1)} %slice.69), channel_id=1, source_target_pairs={{0,2},{2,4},{4,6},{6,0},{1,3},{3,5},{5,7},{7,1},{8,10},{10,12},{12... | collective-permute-start | bytes 983048 | tf_op jit(solution)/shard_map/ppermute | solution.py:266
  53.1 24.6 %copy-start.3 = (bf16[2560,128]{1,0:T(8,128)(2,1)}, bf16[2560,128]{1,0:T(8,128)(2,1)S(1)}, u32[]{:S(2)}) copy-start(bf16[2560,128]{1,0:T(8,128)(2,1)S(1)} %collective-permute-done.3.rest_3_) | copy-start | bytes 1966084
  53.1 21.7 %collective-permute-start.7 = (bf16[1280,128]{1,0:T(8,128)(2,1)S(1)}, bf16[1280,128]{1,0:T(8,128)(2,1)S(1)}, u32[]{:S(2)}, u32[]{:S(2)}) collective-permute-start(bf16[1280,128]{1,0:T(8,128)(2,1)S(1)} %slice.70), channel_id=1, source_target_pairs={{0,6},{2,0},{4,2},{6,4},{1,7},{3,1},{5,3},{7,5},{8,14},{10,8},{12,... | collective-permute-start | bytes 983048 | tf_op jit(solution)/shard_map/ppermute | solution.py:266
  57.2 23.2 %copy-start.8 = (bf16[1536,128]{1,0:T(8,128)(2,1)}, bf16[1536,128]{1,0:T(8,128)(2,1)S(1)}, u32[]{:S(2)}) copy-start(bf16[1536,128]{1,0:T(8,128)(2,1)S(1)} %pad_maximum_fusion.3.own) | copy-start | bytes 1179652
  57.2 23.2 %collective-permute-start = (bf16[1536,128]{1,0:T(8,128)(2,1)S(1)}, bf16[1536,128]{1,0:T(8,128)(2,1)S(1)}, u32[]{:S(2)}, u32[]{:S(2)}) collective-permute-start(bf16[1536,128]{1,0:T(8,128)(2,1)S(1)} %pad_maximum_fusion.3.own), channel_id=1, source_target_pairs={{0,1},{1,0},{2,3},{3,2},{4,5},{5,4},{6,7},{7,6},{8,9},{9,8},{10,11... | collective-permute-start | bytes 1179656 | tf_op jit(solution)/shard_map/ppermute | solution.py:270
  65.0 16.2 %copy-start.4 = (bf16[2560,128]{1,0:T(8,128)(2,1)}, bf16[2560,128]{1,0:T(8,128)(2,1)S(1)}, u32[]{:S(2)}) copy-start(bf16[2560,128]{1,0:T(8,128)(2,1)S(1)} %collective-permute-done.4.rest_4_) | copy-start | bytes 1966084
  65.1 12.6 %collective-permute-start.8 = (bf16[1280,128]{1,0:T(8,128)(2,1)S(1)}, bf16[1280,128]{1,0:T(8,128)(2,1)S(1)}, u32[]{:S(2)}, u32[]{:S(2)}) collective-permute-start(bf16[1280,128]{1,0:T(8,128)(2,1)S(1)} %slice.71), channel_id=1, source_target_pairs={{0,2},{2,4},{4,6},{6,0},{1,3},{3,5},{5,7},{7,1},{8,10},{10,12},{12... | collective-permute-start | bytes 983048 | tf_op jit(solution)/shard_map/ppermute | solution.py:266
  73.2 8.1 %copy-start.5 = (bf16[2560,128]{1,0:T(8,128)(2,1)}, bf16[2560,128]{1,0:T(8,128)(2,1)S(1)}, u32[]{:S(2)}) copy-start(bf16[2560,128]{1,0:T(8,128)(2,1)S(1)} %collective-permute-done.5.rest_5_) | copy-start | bytes 1966084
  73.2 7.1 %collective-permute-start.9 = (bf16[1280,128]{1,0:T(8,128)(2,1)S(1)}, bf16[1280,128]{1,0:T(8,128)(2,1)S(1)}, u32[]{:S(2)}, u32[]{:S(2)}) collective-permute-start(bf16[1280,128]{1,0:T(8,128)(2,1)S(1)} %slice.72), channel_id=1, source_target_pairs={{0,6},{2,0},{4,2},{6,4},{1,7},{3,1},{5,3},{7,5},{8,14},{10,8},{12,... | collective-permute-start | bytes 983048 | tf_op jit(solution)/shard_map/ppermute | solution.py:266
  74.9 5.5 %copy-start.6 = (bf16[2560,128]{1,0:T(8,128)(2,1)}, bf16[2560,128]{1,0:T(8,128)(2,1)S(1)}, u32[]{:S(2)}) copy-start(bf16[2560,128]{1,0:T(8,128)(2,1)S(1)} %constant_dynamic-update-slice_fusion.rest_6_) | copy-start | bytes 1966084
  80.4 1.0 copy-start.7
  80.5 0.8 copy-start.10
  81.4 43.6 %copy-start.16 = (s32[8]{0:T(128)S(1)}, s32[8]{0:T(128)}, u32[]{:S(2)}) copy-start(s32[8]{0:T(128)} %copy-done.15) | copy-start | bytes 100
  125.0 4.5 %collective-permute-start.10 = (f32[8,264,256]{2,1,0:T(8,128)}, f32[8,264,256]{2,1,0:T(8,128)S(1)}, u32[]{:S(2)}, u32[]{:S(2)}) collective-permute-start(f32[8,264,256]{2,1,0:T(8,128)} %get-tuple-element.8.rest_8_), channel_id=1, source_target_pairs={{0,1},{1,0},{2,3},{3,2},{4,5},{5,4},{6,7},{7,6},{8,9},{9,8},{10,11... | collective-permute-start | bytes 6488072 | tf_op jit(solution)/shard_map/ppermute | solution.py:270
  129.5 1.4 copy-start.9
  172.3 6.8 %copy-start.11 = (f32[8,64,256]{2,1,0:T(8,128)S(1)}, f32[8,64,256]{2,1,0:T(8,128)}, u32[]{:S(2)}) copy-start(f32[8,64,256]{2,1,0:T(8,128)} %get-tuple-element.11) | copy-start | bytes 1572868
  172.3 35.6 %all-to-all-start.1 = ((f32[8,512,128]{2,1,0:T(8,128)}), f32[8,512,128]{2,1,0:T(8,128)S(1)}, u32[]{:S(2)}, u32[]{:S(2)}) async-start(f32[8,512,128]{2,1,0:T(8,128)} %broadcast_select_fusion), calls=%async_computation.1 | async-start | bytes 4194304 | tf_op jit(solution)/shard_map/all_to_all | solution.py:320
  180.0 1.6 collective-permute-start.11

commit v2 on v1

v2 whole, which is shorter than its diff:
```python
import functools
import math

import jax
import jax.numpy as jnp
from jax import lax
from jax.experimental import pallas as pl
from jax.experimental.pallas import tpu as pltpu
from jax.sharding import Mesh, PartitionSpec as P

FLOOR = -1e30
LOW = -1e29
F32 = jnp.float32
BF16 = jnp.bfloat16
HEADS = ("zl", "y")
COLS = ("zh", "x")
BLK = 128
GROUPS = 8
COLUMNS = 8
HD = 128
FD = 64
TR = 2 * BLK
TK = COLUMNS * BLK
PAIRS = GROUPS // 2
VROWS = 208
ROW_L = VROWS
ROW_M = VROWS + HD
CARRY = ROW_M + 8
PACK = 2 * HD + 8
PLACES = ((0, 0), (1, 0), (0, 3), (0, 1), (1, 3), (1, 1), (0, 2), (1, 2))
KEY_SCALE = 1.0 / math.sqrt(HD)
FEAT_SCALE = 1.0 / math.sqrt(FD)
SCORE = KEY_SCALE * math.log2(math.e)


def nn(a, b):
    return lax.dot_general(a, b, (((1,), (0,)), ((), ())), preferred_element_type=F32)


def nt(a, b):
    return lax.dot_general(a, b, (((1,), (1,)), ((), ())), preferred_element_type=F32)


def tn(a, b):
    return lax.dot_general(a, b, (((0,), (0,)), ((), ())), preferred_element_type=F32)


def split(a):
    high = a.astype(BF16)
    return high, (a - high.astype(F32)).astype(BF16)


def iota(shape, dim):
    return lax.broadcasted_iota(jnp.int32, shape, dim)


def column(where, j):
    zh, x = PLACES[j]
    return (where[0] + zh) % 2, (where[1] + x) % 4


def row_positions(blocks, where, k):
    lane = iota((1, TR), 1)
    at = k * 16 + where[0] * 8 + where[1] * 2
    first = blocks[at] * BLK
    second = blocks[at + 1] * BLK - BLK
    return lane + jnp.where(lane < BLK, first, second)


def tile_mask(blocks, where, k, columns):
    pos_rows = row_positions(blocks, where, k)
    step = iota((BLK, 1), 0)
    parts = []
    for j in columns:
        zh, x = column(where, j)
        parts.append(pos_rows >= step + blocks[k * 16 + zh * 8 + x * 2 + where[2]] * BLK)
    return jnp.concatenate(parts, axis=0)


def block_at(base, k):
    return pl.ds(pl.multiple_of(base + k * BLK, BLK), BLK)


def load_rows(where, own, other, q_buf, qf_buf):
    for ref, slot in ((own, where[2]), (other, 1 - where[2])):
        at = pl.ds(pl.multiple_of(slot * BLK, BLK), BLK)
        for k in range(GROUPS):
            q_buf[k, at, :] = ref[k * BLK : (k + 1) * BLK, :]
            base = (GROUPS + k // 2) * BLK
            lanes = slice((k % 2) * FD, (k % 2 + 1) * FD)
            qf_buf[k, at, :] = ref[base : base + BLK, lanes]


def forward_kernel(columns, first, last, *refs):
    width = len(columns)
    keys_n = width * BLK
    blocks, where, own, other = refs[:4]
    slabs = refs[4 : 4 + width]
    refs = refs[4 + width :]
    if not first:
        carry_in, sums_in = refs[:2]
        refs = refs[2:]
    if last:
        pack, okf, states = refs[:3]
        carry, sums = refs[3:5]
        refs = refs[5:]
    else:
        carry, sums = refs[:2]
        refs = refs[2:]
    k_buf, kf_buf, vft, q_buf, qf_buf = refs
    load_rows(where, own, other, q_buf, qf_buf)
    if first:
        carry[...] = jnp.zeros_like(carry)
        for k in range(GROUPS):
            carry[k, ROW_M : ROW_M + 1, :] = jnp.full((1, TR), LOW, F32)
        sums[...] = jnp.zeros_like(sums)
    else:
        carry[...] = carry_in[...]
        sums[...] = sums_in[...]
    tail_rows = jnp.where(iota((VROWS - HD - FD, keys_n), 0) == 0, 1.0, 0.0).astype(BF16)
    for k in range(GROUPS):
        vft[k, HD + FD :, :] = tail_rows

    def update(rows, plans):
        olds = [carry[k, :VROWS, :] for k in rows]
        tops = [carry[k, ROW_M : ROW_M + 1, :] for k in rows]
        scores = []
        for k, plan in zip(rows, plans):
            found = []
            for g, mask in plan:
                s = nt(k_buf[g], q_buf[k])
                found.append(s if mask is None else jnp.where(mask, s, FLOOR))
            scores.append(found)
        results = []
        for old, top, found, plan in zip(olds, tops, scores, plans):
            new = top
            for s in found:
                new = jnp.maximum(new, jnp.max(s, axis=0, keepdims=True))
            total = old * jnp.exp2((top - new) * SCORE)
            for s, (g, _) in zip(found, plan):
                total = total + nn(vft[g], jnp.exp2((s - new) * SCORE).astype(BF16))
            results.append((total, new))
        for k, (total, new) in zip(rows, results):
            carry[k, :VROWS, :] = total
            carry[k, ROW_M : ROW_M + 1, :] = new

    def pair(i, c):
        a, b = 2 * i, 2 * i + 1
        step = 4 // width

        def full(u, c2):
            groups = [step * u + e for e in range(step)]
            update((a, b), [[(g, None) for g in groups]] * 2)
            return c2

        lax.fori_loop(0, i * 2 // step, full, 0)
        for j, slab in enumerate(slabs):
            at = slice(j * BLK, (j + 1) * BLK)
            feats = slab[block_at(2 * GROUPS * BLK, i), :]
            for e, k in enumerate((a, b)):
                part = feats[:, e * FD : (e + 1) * FD]
                k_buf[k, at, :] = slab[block_at(0, k), :]
                kf_buf[k, at, :] = part
                vft[k, :HD, at] = slab[block_at(GROUPS * BLK, k), :].T
                vft[k, HD : HD + FD, at] = part.T
        masks = [tile_mask(blocks, where, k, columns) for k in (a, b)]
        update((a, b), [[(a, masks[0])], [(a, None), (b, masks[1])]])
        for k, mask in zip((a, b), masks):
            inv_n = FEAT_SCALE / (row_positions(blocks, where, k) + 1).astype(F32)
            student = jnp.where(mask, nt(kf_buf[k], qf_buf[k]) * inv_n, 0.0).astype(BF16)
            carry[k, ROW_L:ROW_M, :] += nn(vft[k, :HD, :], student)
            sums[k] += nn(vft[k, : HD + FD, :], kf_buf[k])
        return c

    lax.fori_loop(0, PAIRS, pair, 0)
    if not last:
        return

    def finish(k, state):
        inv_n = FEAT_SCALE / (row_positions(blocks, where, k) + 1).astype(F32)
        high, low = split(state[:HD])
        linear = (nt(high, qf_buf[k]) + nt(low, qf_buf[k])) * inv_n
        pack[k, :HD, :] = carry[k, :HD, :]
        pack[k, HD : 2 * HD, :] = carry[k, ROW_L:ROW_M, :] + linear
        norm = carry[k, HD + FD : HD + FD + 1, :]
        top = carry[k, ROW_M : ROW_M + 1, :]
        pack[k, 2 * HD :, :] = jnp.where(iota((8, TR), 0) == 0, norm, top)
        okf[k] = carry[k, HD : HD + FD, :]
        states[k] = state
        return state + sums[k]

    state = jnp.zeros((HD + FD, FD), F32)
    for k in range(GROUPS):
        state = finish(k, state)


def backward_kernel(blocks, where, own, other, *rest):
    slabs = rest[:COLUMNS]
    mine, theirs, okf, states, dk_out, dq_out = rest[COLUMNS : COLUMNS + 6]
    k_buf, v_buf, kf_buf, kft, q_buf, qf_buf, r_buf, bias, acc, w_state, u_state = rest[COLUMNS + 6 :]
    load_rows(where, own, other, q_buf, qf_buf)

    for k in range(GROUPS):
        l0, m0 = mine[k, 2 * HD : 2 * HD + 1, :], mine[k, 2 * HD + 1 : 2 * HD + 2, :]
        l1, m1 = theirs[k, 2 * HD : 2 * HD + 1, :], theirs[k, 2 * HD + 1 : 2 * HD + 2, :]
        top = jnp.maximum(m0, m1)
        w0, w1 = jnp.exp2((m0 - top) * SCORE), jnp.exp2((m1 - top) * SCORE)
        total = l0 * w0 + l1 * w1
        w0, w1 = w0 / total, w1 / total
        mixed = (mine[k, :HD, :] * w0 + theirs[k, :HD, :] * w1) - (
            mine[k, HD : 2 * HD, :] + theirs[k, HD : 2 * HD, :]
        )
        r_buf[k] = mixed.astype(BF16)
        n = (row_positions(blocks, where, k) + 1).astype(F32)
        bias[k] = (0.5 * jnp.log2(n) - jnp.log2(total)) - top * SCORE
        dq_out[k] = okf[k] * (w0 * jnp.sqrt(n))
    w_state[...] = jnp.zeros_like(w_state)
    u_state[...] = jnp.zeros_like(u_state)

    def teach(g, k):
        return nt(k_buf[g], q_buf[k]) * SCORE + bias[k]

    def pair(step, c):
        i = PAIRS - 1 - step
        a, b = 2 * i, 2 * i + 1
        for j, slab in enumerate(slabs):
            at = slice(j * BLK, (j + 1) * BLK)
            feats = slab[block_at(2 * GROUPS * BLK, i), :]
            for e, g in enumerate((a, b)):
                part = feats[:, e * FD : (e + 1) * FD]
                k_buf[g, at, :] = slab[block_at(0, g), :]
                v_buf[g, at, :] = slab[block_at(GROUPS * BLK, g), :]
                kf_buf[g, at, :] = part
                kft[g, :, at] = part.T

        def diagonal(g, e):
            mask = tile_mask(blocks, where, g, range(COLUMNS))
            n = (row_positions(blocks, where, g) + 1).astype(F32)
            weight = FEAT_SCALE / jnp.sqrt(n)
            r_tile, qf_tile, v_tile, kf_tile = r_buf[g], qf_buf[g], v_buf[g], kf_buf[g]
            w_high, w_low = split(w_state[...])
            u_high, u_low = split(u_state[...])
            total = (nn(v_tile, w_high) + nn(v_tile, w_low)) - (nn(kf_tile, u_high) + nn(kf_tile, u_low))
            linear = nn(v_tile, r_tile) * KEY_SCALE - nt(kf_tile, qf_tile) * weight
            linear = jnp.where(mask, linear, 0.0)
            p = jnp.exp2(jnp.where(mask, teach(g, g), FLOOR))
            total = total + nn((p + linear).astype(BF16), qf_tile)
            if e == 0:
                p = jnp.exp2(teach(a, b)).astype(BF16)
                total = total + nn(p, qf_buf[b])
            acc[e] = total
            s_high, s_low = split(states[g])
            query = tn(s_high[:HD], r_tile) + tn(s_low[:HD], r_tile)
            student = nt(s_high[HD:], qf_tile) + nt(s_low[HD:], qf_tile)
            query = query * KEY_SCALE - student * weight + nn(kft[g], linear.astype(BF16))
            dq_out[g] = -(dq_out[g] + query)
            w_state[...] += nn(r_tile, qf_tile) * KEY_SCALE
            f_high, f_low = split(qf_tile.astype(F32).T * weight)
            u_state[...] += nn(f_high, qf_tile) + nn(f_low, qf_tile)

        diagonal(b, 1)
        diagonal(a, 0)

        def full(t, c2):
            olds = [acc[e] for e in range(2)]
            for e, g in enumerate((a, b)):
                for k in (2 * t, 2 * t + 1):
                    p = jnp.exp2(teach(g, k)).astype(BF16)
                    olds[e] = olds[e] + nn(p, qf_buf[k])
            for e in range(2):
                acc[e] = olds[e]
            return c2

        lax.fori_loop(i + 1, PAIRS, full, 0)
        for e in range(2):
            result = (-acc[e]).astype(dk_out.dtype)
            for j in range(COLUMNS):
                zh, x = column(where, j)
                dk_out[zh * 4 + x, block_at(0, i), e * FD : (e + 1) * FD] = result[j * BLK : (j + 1) * BLK, :]
        return c

    lax.fori_loop(0, PAIRS, pair, 0)


def on_chip(count_smem, count_vmem):
    smem = [pl.BlockSpec(memory_space=pltpu.SMEM)] * count_smem
    return smem + [pl.BlockSpec(memory_space=pltpu.VMEM)] * count_vmem


def forward(columns, blocks, where, own, other, slabs, carried, last):
    width = len(columns)
    carry = ((GROUPS, CARRY, TR), F32)
    sums = ((GROUPS, HD + FD, FD), F32)
    if last:
        outs = [((GROUPS, PACK, TR), F32), ((GROUPS, FD, TR), F32), sums]
        scratch = [pltpu.VMEM(*carry), pltpu.VMEM(*sums)]
    else:
        outs, scratch = [carry, sums], []
    scratch += [
        pltpu.VMEM((GROUPS, width * BLK, HD), BF16),
        pltpu.VMEM((GROUPS, width * BLK, FD), BF16),
        pltpu.VMEM((GROUPS, VROWS, width * BLK), BF16),
        pltpu.VMEM((GROUPS, TR, HD), BF16),
        pltpu.VMEM((GROUPS, TR, FD), BF16),
    ]
    return pl.pallas_call(
        functools.partial(forward_kernel, columns, not carried, last),
        out_shape=tuple(jax.ShapeDtypeStruct(*o) for o in outs),
        in_specs=on_chip(2, 2 + width + len(carried)),
        out_specs=[pl.BlockSpec(memory_space=pltpu.VMEM)] * len(outs),
        scratch_shapes=scratch,
        name="forward" + str(columns[0]),
    )(blocks, where, own, other, *[slabs[j] for j in columns], *carried)


def backward(blocks, where, own, other, slabs, mine, theirs, okf, states):
    return pl.pallas_call(
        backward_kernel,
        out_shape=(
            jax.ShapeDtypeStruct((COLUMNS, PAIRS * BLK, 2 * FD), BF16),
            jax.ShapeDtypeStruct((GROUPS, FD, TR), F32),
        ),
        in_specs=on_chip(2, 6 + COLUMNS),
        out_specs=[pl.BlockSpec(memory_space=pltpu.VMEM)] * 2,
        scratch_shapes=[
            pltpu.VMEM((GROUPS, TK, HD), BF16),
            pltpu.VMEM((GROUPS, TK, HD), BF16),
            pltpu.VMEM((GROUPS, TK, FD), BF16),
            pltpu.VMEM((GROUPS, FD, TK), BF16),
            pltpu.VMEM((GROUPS, TR, HD), BF16),
            pltpu.VMEM((GROUPS, TR, FD), BF16),
            pltpu.VMEM((GROUPS, HD, TR), BF16),
            pltpu.VMEM((GROUPS, 1, TR), F32),
            pltpu.VMEM((2, TK, FD), F32),
            pltpu.VMEM((HD, FD), F32),
            pltpu.VMEM((FD, FD), F32),
        ],
        name="backward",
    )(blocks, where, own, other, *slabs, mine, theirs, okf, states)


def shifted(a, step):
    return lax.ppermute(a, "x", [(i, (i + step) % 4) for i in range(4)])


def across(a, axis):
    return lax.ppermute(a, axis, [(0, 1), (1, 0)])


def pair_up(a):
    return a.reshape(PAIRS, 2, BLK, FD).transpose(0, 2, 1, 3).reshape(PAIRS * BLK, 2 * FD)


def per_device(queries, keys, values, query_feats, key_feats, block_pos):
    q_heads = queries.reshape(BLK, GROUPS, HD).transpose(1, 0, 2)
    feats = jnp.concatenate(
        [key_feats.reshape(BLK, GROUPS, FD), query_feats.reshape(BLK, GROUPS, FD)], axis=-1
    ).transpose(1, 0, 2)
    shared = jnp.broadcast_to(jnp.concatenate([keys, values], axis=0)[None], (GROUPS, 2 * BLK, HD))
    sent = jnp.concatenate([q_heads, shared, feats], axis=1)
    got = lax.all_to_all(sent, HEADS, 0, 0, tiled=True)
    slab = jnp.concatenate(
        [
            got[:, BLK : 2 * BLK].reshape(-1, HD),
            got[:, 2 * BLK : 3 * BLK].reshape(-1, HD),
            pair_up(got[:, 3 * BLK :, :FD]),
        ],
        axis=0,
    )
    own = jnp.concatenate([got[:, :BLK].reshape(-1, HD), pair_up(got[:, 3 * BLK :, FD:])], axis=0)
    far = across(slab, "zh")
    left, right = shifted(slab, 1), shifted(slab, 3)
    other = across(own, "c")
    far_left, far_right = shifted(far, 1), shifted(far, 3)
    half = slab.shape[0] // 2
    behind = jnp.concatenate([shifted(left[:half], 1), shifted(right[half:], 3)], axis=0)
    far_behind = jnp.concatenate([shifted(far_left[:half], 1), shifted(far_right[half:], 3)], axis=0)
    slabs = (slab, far, left, right, far_left, far_right, behind, far_behind)
    c = lax.axis_index("c")
    where = jnp.stack([lax.axis_index("zh"), lax.axis_index("x"), c]).astype(jnp.int32)

    carried = forward((0, 1), block_pos, where, own, other, slabs, (), False)
    carried = forward((2, 3, 4, 5), block_pos, where, own, other, slabs, carried, False)
    mine, okf, states = forward((6, 7), block_pos, where, own, other, slabs, carried, True)
    theirs = across(mine, "c")
    dk, dq = backward(block_pos, where, own, other, slabs, mine, theirs, okf, states)

    dk = lax.all_to_all(dk, COLS, 0, 0, tiled=True).astype(F32).sum(axis=0)
    dk = dk.reshape(PAIRS, BLK, 2, FD).transpose(0, 2, 1, 3).reshape(GROUPS, BLK, FD)
    dq = dq.reshape(GROUPS, FD, 2, BLK)
    keep = lax.dynamic_slice_in_dim(dq, c, 1, 2)
    give = lax.dynamic_slice_in_dim(dq, 1 - c, 1, 2)
    dq = (keep + across(give, "c"))[:, :, 0].transpose(0, 2, 1)
    final = lax.all_to_all(jnp.concatenate([dq, dk], axis=-1), HEADS, 0, 0, tiled=True)
    final = final.transpose(1, 0, 2)
    return final[:, :, :FD].reshape(BLK, -1), final[:, :, FD:].reshape(BLK, -1)


def solution(mesh):
    split_mesh = Mesh(mesh.devices.reshape(2, 4, 2, 4, 2), ("zl", "y", "zh", "x", "c"))
    spec = P(("zl", "y", "zh", "x", "c"), None)
    return jax.shard_map(
        per_device,
        mesh=split_mesh,
        in_specs=(spec,) * 5 + (P(),),
        out_specs=(spec, spec),
        check_vma=False,
    )
```

time: 223 us -> 178 us (0.80)
  waiting for transfers between devices: 77.2 us -> 32.9 us
  blocking collectives: 12.7 us -> 34.1 us
  Pallas kernels: 81.2 us -> 72.2 us
  starting transfers between devices: 28.5 us -> 20.4 us
  other arithmetic: 6.89 us -> 1.82 us
    all_to_all x2 -> x1, waiting for transfers between devices: 41.7 us -> 15 us  [per_device(): dk = lax.all_to_all(dk, COLS, 0, 0, tiled=True).astype(F32).sum(axis=0)]
    all_to_all x0 -> x1, blocking collectives: none -> 21.4 us  [per_device(): got = lax.all_to_all(sent, HEADS, 0, 0, tiled=True)]
    ppermute x8, waiting for transfers between devices: 19.9 us -> 1.46 us  [shifted(): return lax.ppermute(a, 'x', [(i, (i + step) % 4) for i in range(4)])]
    pallas_call x1, Pallas kernels: 37.6 us -> 27 us  [backward(): pl.pallas_call(backward_kernel, out_shape=(jax.ShapeDtypeStruct((COLUMNS,...]
    all_to_all x2 -> x1, starting transfers between devices: 12.8 us -> 4.67 us  [per_device(): dk = lax.all_to_all(dk, COLS, 0, 0, tiled=True).astype(F32).sum(axis=0)]
    gather x2 -> x0, local copies, waits for them, and re-layouts: 2.82 us -> none  [the longest x1 2.27 us: per_device(): dk = jnp.take(dk, jnp.argsort(order), axis=0)]
    select_n x4 -> x0, other arithmetic: 2.26 us -> none  [the longest x2 1.59 us: per_device(): dk = jnp.take(dk, jnp.argsort(order), axis=0)]
    unnamed x40 -> x28, local copies, waits for them, and re-layouts: 7.13 us -> 8.91 us
  transfers between devices with their start and end apart: 14 -> 13, of which waited for: 9 -> 5; matrix products, arithmetic and copies ran while one was open for 4% -> 4% of each run, Pallas kernels for 0% -> 18%
where the time goes in v2:
time: 178 us
  Pallas kernels  72.2 us (41%)
  blocking collectives  34.1 us (19%)
  waiting for transfers between devices  32.9 us (18%)
  starting transfers between devices  20.4 us (11%)
  local copies, waits for them, and re-layouts  15.2 us (9%)
  other arithmetic  1.82 us (1%)
    pallas_call x3, Pallas kernels, forward(): pl.pallas_call(functools.partial(forward_kernel, columns, not carried, la...  45.3 us
    pallas_call x1, Pallas kernels, backward(): pl.pallas_call(backward_kernel, out_shape=(jax.ShapeDtypeStruct((COLUMNS,...  27 us
    all_to_all x1, blocking collectives, per_device(): got = lax.all_to_all(sent, HEADS, 0, 0, tiled=True)  21.4 us
    ppermute x4, waiting for transfers between devices, across(): return lax.ppermute(a, axis, [(0, 1), (1, 0)])  16.5 us
    all_to_all x1, waiting for transfers between devices, per_device(): dk = lax.all_to_all(dk, COLS, 0, 0, tiled=True).astype(F32).sum(axis=0)  15 us
    all_to_all x1, blocking collectives, per_device(): lax.all_to_all(jnp.concatenate([dq, dk], axis=-1), HEADS, 0, 0, tiled=True)  12.7 us
    ppermute x8, starting transfers between devices, shifted(): return lax.ppermute(a, 'x', [(i, (i + step) % 4) for i in range(4)])  11.9 us
    unnamed x28, local copies, waits for them, and re-layouts  8.91 us
  transfers between devices with their start and end apart: 13, of which 5 were waited for; matrix products, arithmetic and copies ran while one was open for 4% of the time, Pallas kernels for 18%

profile of v2, /device:TPU:0, one launch (start us, length us, event | category | flops | bytes accessed | tf_op | source)
XLA Modules:
  0.0 177.7 jit_solution(11176048022775952163)
XLA Ops:
  0.6 0.8 pad_maximum_fusion.4
  1.5 1.0 copy.47
  2.6 1.0 copy.48
  3.6 1.1 copy.45
  4.9 21.4 %all_to_all.15 = bf16[8,512,128]{1,2,0:T(8,128)(2,1)S(1)} all-to-all(bf16[8,512,128]{1,2,0:T(8,128)(2,1)S(1)} %pad_maximum_fusion), channel_id=1, replica_groups=mesh['zl'=2,'y'=4,'zh'=2,'x'=4,'c'=2] {'zl','y'}, dimensions={0} | all-to-all | bytes 2097152 | tf_op jit(solution)/shard_map/all_to_all | solution.py:361
  27.4 3.7 %collective-permute-start.1 = (bf16[2560,128]{1,0:T(8,128)(2,1)S(1)}, bf16[2560,128]{1,0:T(8,128)(2,1)}, u32[]{:S(2)}, u32[]{:S(2)}) collective-permute-start(bf16[2560,128]{1,0:T(8,128)(2,1)S(1)} %pad_maximum_fusion.1.refs_4_.rest_0_), channel_id=1, source_target_pairs={{0,8},{8,0},{1,9},{9,1},{2,10},{10,2},{3,11},{11,3},{4,12},{12,4},... | collective-permute-start | bytes 1966088 | tf_op jit(solution)/shard_map/ppermute | solution.py:347
  31.0 1.5 collective-permute-start.2
  32.5 1.7 collective-permute-start.3
  34.3 10.5 %collective-permute-done.1.refs_5_.rest_1_ = bf16[2560,128]{1,0:T(8,128)(2,1)} collective-permute-done((bf16[2560,128]{1,0:T(8,128)(2,1)S(1)}, bf16[2560,128]{1,0:T(8,128)(2,1)}, u32[]{:S(2)}, u32[]{:S(2)}) %collective-permute-start.1) | collective-permute-done | bytes 655392 | tf_op jit(solution)/shard_map/ppermute | solution.py:347
  44.8 1.5 collective-permute-start.4
  46.7 1.8 %collective-permute-start.5 = (bf16[2560,128]{1,0:T(8,128)(2,1)}, bf16[2560,128]{1,0:T(8,128)(2,1)}, u32[]{:S(2)}, u32[]{:S(2)}) collective-permute-start(bf16[2560,128]{1,0:T(8,128)(2,1)} %collective-permute-done.1.refs_5_.rest_1_), channel_id=1, source_target_pairs={{0,6},{2,0},{4,2},{6,4},{1,7},{3,1},{5,3},{7,5},{8,14},{10,8},{12,... | collective-permute-start | bytes 1966088 | tf_op jit(solution)/shard_map/ppermute | solution.py:343
  48.7 0.9 slice.49
  49.8 0.8 slice.50
  50.6 3.0 %collective-permute-start.7 = (bf16[1280,128]{1,0:T(8,128)(2,1)}, bf16[1280,128]{1,0:T(8,128)(2,1)}, u32[]{:S(2)}, u32[]{:S(2)}) collective-permute-start(bf16[1280,128]{1,0:T(8,128)(2,1)} %slice.50), channel_id=1, source_target_pairs={{0,6},{2,0},{4,2},{6,4},{1,7},{3,1},{5,3},{7,5},{8,14},{10,8},{12,... | collective-permute-start | bytes 983048 | tf_op jit(solution)/shard_map/ppermute | solution.py:343
  54.9 12.0 %forward0.1 = (f32[8,344,256]{2,1,0:T(8,128)}, f32[8,192,64]{2,1,0:T(8,128)}) custom-call(s32[128]{0:T(128)} %blocks.1, s32[3]{0:T(128)} %pad_add_fusion.refs_1_.where, bf16[1536,128]{1,0:T(8,128)(2,1)} %copy-done, bf16[1536,128]{1,0:T(8,128)(2,1)} %copy-done.1, bf16[2560,128]{1,0:T(8,128)(2,1)} %copy-done.2, ...), custom_call_target="tpu_custom_call" | custom-call | tf_op jit(solution)/shard_map/forward0/pallas_call | solution.py:306
  67.0 1.4 collective-permute-done.6
  68.5 1.0 constant_dynamic-update-slice_fusion.1
  69.5 1.0 slice.52
  70.5 2.0 %collective-permute-start.9 = (bf16[1280,128]{1,0:T(8,128)(2,1)S(1)}, bf16[1280,128]{1,0:T(8,128)(2,1)S(1)}, u32[]{:S(2)}, u32[]{:S(2)}) collective-permute-start(bf16[1280,128]{1,0:T(8,128)(2,1)S(1)} %slice.52), channel_id=1, source_target_pairs={{0,6},{2,0},{4,2},{6,4},{1,7},{3,1},{5,3},{7,5},{8,14},{10,8},{12,... | collective-permute-start | bytes 983048 | tf_op jit(solution)/shard_map/ppermute | solution.py:343
  72.5 1.0 constant_dynamic-update-slice_fusion.refs_4_.rest_6_
  73.6 19.8 %forward2.1 = (f32[8,344,256]{2,1,0:T(8,128)}, f32[8,192,64]{2,1,0:T(8,128)}) custom-call(s32[128]{0:T(128)} %blocks.1, s32[3]{0:T(128)} %pad_add_fusion.refs_1_.where, bf16[1536,128]{1,0:T(8,128)(2,1)} %copy-done, bf16[1536,128]{1,0:T(8,128)(2,1)} %copy-done.1, bf16[2560,128]{1,0:T(8,128)(2,1)} %copy-done.3, bf16[2560,128]{1,0:T(8,128)(2,1)} %copy-done.4, ...), custom_call_target="tpu_custom_call" | custom-call | tf_op jit(solution)/shard_map/forward2/pallas_call | solution.py:306
  93.6 0.9 copy-done.7
  94.5 13.4 %forward6.1 = (f32[8,264,256]{2,1,0:T(8,128)}, f32[8,64,256]{2,1,0:T(8,128)}, f32[8,192,64]{2,1,0:T(8,128)}) custom-call(s32[128]{0:T(128)} %blocks.1, s32[3]{0:T(128)} %pad_add_fusion.refs_1_.where, bf16[1536,128]{1,0:T(8,128)(2,1)} %copy-done, bf16[1536,128]{1,0:T(8,128)(2,1)} %copy-done.1, bf16[2560,128]{1,0:T(8,128)(2,1)} %copy-done.6, ...), custom_call_target="tpu_custom_call" | custom-call | tf_op jit(solution)/shard_map/forward6/pallas_call | solution.py:306
  107.9 4.5 %collective-permute-done.10.rest_9_ = f32[8,264,256]{2,1,0:T(8,128)S(1)} collective-permute-done((f32[8,264,256]{2,1,0:T(8,128)}, f32[8,264,256]{2,1,0:T(8,128)S(1)}, u32[]{:S(2)}, u32[]{:S(2)}) %collective-permute-start.10) | collective-permute-done | bytes 2162720 | tf_op jit(solution)/shard_map/ppermute | solution.py:347
  112.4 1.3 copy-done.8
  113.7 27.0 %backward.1 = (bf16[8,512,128]{2,1,0:T(8,128)(2,1)}, f32[8,64,256]{2,1,0:T(8,128)}) custom-call(s32[128]{0:T(128)} %blocks.1, s32[3]{0:T(128)} %pad_add_fusion.refs_1_.where, bf16[1536,128]{1,0:T(8,128)(2,1)} %copy-done, bf16[1536,128]{1,0:T(8,128)(2,1)} %copy-done.1, bf16[2560,128]{1,0:T(8,128)(2,1)} %copy-done.2, ...), custom_call_target="tpu_custom_call" | custom-call | tf_op jit(solution)/shard_map/backward/pallas_call | solution.py:317
  140.7 4.7 %all-to-all-start.1 = ((bf16[8,512,128]{2,1,0:T(8,128)(2,1)}), bf16[8,512,128]{2,1,0:T(8,128)(2,1)S(1)}, u32[]{:S(2)}, u32[]{:S(2)}) async-start(bf16[8,512,128]{2,1,0:T(8,128)(2,1)} %get-tuple-element.19), calls=%async_computation.1 | async-start | bytes 2097152 | tf_op jit(solution)/shard_map/all_to_all | solution.py:388
  146.3 1.5 collective-permute-done.11
  147.9 15.0 %all-to-all-done.1 = bf16[8,512,128]{2,1,0:T(8,128)(2,1)S(1)} async-done(((bf16[8,512,128]{2,1,0:T(8,128)(2,1)}), bf16[8,512,128]{2,1,0:T(8,128)(2,1)S(1)}, u32[]{:S(2)}, u32[]{:S(2)}) %all-to-all-start.1) | async-done | bytes 1048608 | tf_op jit(solution)/shard_map/all_to_all | solution.py:388
  163.3 12.7 %all_to_all.16 = f32[8,128,128]{1,2,0:T(8,128)S(1)} all-to-all(f32[8,128,128]{1,2,0:T(8,128)S(1)} %pad_maximum_fusion.2), channel_id=1, replica_groups=mesh['zl'=2,'y'=4,'zh'=2,'x'=4,'c'=2] {'zl','y'}, dimensions={0} | all-to-all | bytes 1048576 | tf_op jit(solution)/shard_map/all_to_all | solution.py:394
  176.0 0.8 copy.60
  176.8 0.8 copy.61
  (60 shorter events, 5.1 us)
Async XLA Ops:
  27.4 26.8 %copy-start.2 = (bf16[2560,128]{1,0:T(8,128)(2,1)}, bf16[2560,128]{1,0:T(8,128)(2,1)S(1)}, u32[]{:S(2)}) copy-start(bf16[2560,128]{1,0:T(8,128)(2,1)S(1)} %pad_maximum_fusion.1.refs_4_.rest_0_) | copy-start | bytes 1966084
  27.4 17.4 %collective-permute-start.1 = (bf16[2560,128]{1,0:T(8,128)(2,1)S(1)}, bf16[2560,128]{1,0:T(8,128)(2,1)}, u32[]{:S(2)}, u32[]{:S(2)}) collective-permute-start(bf16[2560,128]{1,0:T(8,128)(2,1)S(1)} %pad_maximum_fusion.1.refs_4_.rest_0_), channel_id=1, source_target_pairs={{0,8},{8,0},{1,9},{9,1},{2,10},{10,2},{3,11},{11,3},{4,12},{12,4},... | collective-permute-start | bytes 1966088 | tf_op jit(solution)/shard_map/ppermute | solution.py:347
  31.0 17.6 %collective-permute-start.2 = (bf16[2560,128]{1,0:T(8,128)(2,1)S(1)}, bf16[2560,128]{1,0:T(8,128)(2,1)S(1)}, u32[]{:S(2)}, u32[]{:S(2)}) collective-permute-start(bf16[2560,128]{1,0:T(8,128)(2,1)S(1)} %pad_maximum_fusion.1.refs_4_.rest_0_), channel_id=1, source_target_pairs={{0,2},{2,4},{4,6},{6,0},{1,3},{3,5},{5,7},{7,1},{8,10},{10,12},{12... | collective-permute-start | bytes 1966088 | tf_op jit(solution)/shard_map/ppermute | solution.py:343
  32.5 17.3 %collective-permute-start.3 = (bf16[2560,128]{1,0:T(8,128)(2,1)S(1)}, bf16[2560,128]{1,0:T(8,128)(2,1)S(1)}, u32[]{:S(2)}, u32[]{:S(2)}) collective-permute-start(bf16[2560,128]{1,0:T(8,128)(2,1)S(1)} %pad_maximum_fusion.1.refs_4_.rest_0_), channel_id=1, source_target_pairs={{0,6},{2,0},{4,2},{6,4},{1,7},{3,1},{5,3},{7,5},{8,14},{10,8},{12,... | collective-permute-start | bytes 1966088 | tf_op jit(solution)/shard_map/ppermute | solution.py:343
  44.8 22.2 %collective-permute-start.4 = (bf16[2560,128]{1,0:T(8,128)(2,1)}, bf16[2560,128]{1,0:T(8,128)(2,1)S(1)}, u32[]{:S(2)}, u32[]{:S(2)}) collective-permute-start(bf16[2560,128]{1,0:T(8,128)(2,1)} %collective-permute-done.1.refs_5_.rest_1_), channel_id=1, source_target_pairs={{0,2},{2,4},{4,6},{6,0},{1,3},{3,5},{5,7},{7,1},{8,10},{10,12},{12... | collective-permute-start | bytes 1966088 | tf_op jit(solution)/shard_map/ppermute | solution.py:343
  46.7 22.8 %collective-permute-start.5 = (bf16[2560,128]{1,0:T(8,128)(2,1)}, bf16[2560,128]{1,0:T(8,128)(2,1)}, u32[]{:S(2)}, u32[]{:S(2)}) collective-permute-start(bf16[2560,128]{1,0:T(8,128)(2,1)} %collective-permute-done.1.refs_5_.rest_1_), channel_id=1, source_target_pairs={{0,6},{2,0},{4,2},{6,4},{1,7},{3,1},{5,3},{7,5},{8,14},{10,8},{12,... | collective-permute-start | bytes 1966088 | tf_op jit(solution)/shard_map/ppermute | solution.py:343
  48.5 5.6 %copy-start = (bf16[1536,128]{1,0:T(8,128)(2,1)}, bf16[1536,128]{1,0:T(8,128)(2,1)S(1)}, u32[]{:S(2)}) copy-start(bf16[1536,128]{1,0:T(8,128)(2,1)S(1)} %pad_maximum_fusion.3.refs_2_.own) | copy-start | bytes 1179652
  48.5 5.6 %collective-permute-start = (bf16[1536,128]{1,0:T(8,128)(2,1)S(1)}, bf16[1536,128]{1,0:T(8,128)(2,1)S(1)}, u32[]{:S(2)}, u32[]{:S(2)}) collective-permute-start(bf16[1536,128]{1,0:T(8,128)(2,1)S(1)} %pad_maximum_fusion.3.refs_2_.own), channel_id=1, source_target_pairs={{0,1},{1,0},{2,3},{3,2},{4,5},{5,4},{6,7},{7,6},{8,9},{9,8},{10,11... | collective-permute-start | bytes 1179656 | tf_op jit(solution)/shard_map/ppermute | solution.py:347
  48.6 20.8 %copy-start.3 = (bf16[2560,128]{1,0:T(8,128)(2,1)}, bf16[2560,128]{1,0:T(8,128)(2,1)S(1)}, u32[]{:S(2)}) copy-start(bf16[2560,128]{1,0:T(8,128)(2,1)S(1)} %collective-permute-done.2.refs_4_.rest_2_) | copy-start | bytes 1966084
  49.5 19.0 %collective-permute-start.6 = (bf16[1280,128]{1,0:T(8,128)(2,1)}, bf16[1280,128]{1,0:T(8,128)(2,1)}, u32[]{:S(2)}, u32[]{:S(2)}) collective-permute-start(bf16[1280,128]{1,0:T(8,128)(2,1)} %slice.49), channel_id=1, source_target_pairs={{0,2},{2,4},{4,6},{6,0},{1,3},{3,5},{5,7},{7,1},{8,10},{10,12},{12... | collective-permute-start | bytes 983048 | tf_op jit(solution)/shard_map/ppermute | solution.py:343
  49.8 23.8 %copy-start.4 = (bf16[2560,128]{1,0:T(8,128)(2,1)}, bf16[2560,128]{1,0:T(8,128)(2,1)S(1)}, u32[]{:S(2)}) copy-start(bf16[2560,128]{1,0:T(8,128)(2,1)S(1)} %collective-permute-done.3.refs_5_.rest_3_) | copy-start | bytes 1966084
  50.6 22.0 %collective-permute-start.7 = (bf16[1280,128]{1,0:T(8,128)(2,1)}, bf16[1280,128]{1,0:T(8,128)(2,1)}, u32[]{:S(2)}, u32[]{:S(2)}) collective-permute-start(bf16[1280,128]{1,0:T(8,128)(2,1)} %slice.50), channel_id=1, source_target_pairs={{0,6},{2,0},{4,2},{6,4},{1,7},{3,1},{5,3},{7,5},{8,14},{10,8},{12,... | collective-permute-start | bytes 983048 | tf_op jit(solution)/shard_map/ppermute | solution.py:343
  54.2 0.8 copy-start.1
  66.9 6.7 %copy-start.5 = (bf16[2560,128]{1,0:T(8,128)(2,1)}, bf16[2560,128]{1,0:T(8,128)(2,1)S(1)}, u32[]{:S(2)}) copy-start(bf16[2560,128]{1,0:T(8,128)(2,1)S(1)} %collective-permute-done.4.refs_6_.rest_4_) | copy-start | bytes 1966084
  67.0 26.5 %collective-permute-start.8 = (bf16[1280,128]{1,0:T(8,128)(2,1)S(1)}, bf16[1280,128]{1,0:T(8,128)(2,1)S(1)}, u32[]{:S(2)}, u32[]{:S(2)}) collective-permute-start(bf16[1280,128]{1,0:T(8,128)(2,1)S(1)} %slice.51), channel_id=1, source_target_pairs={{0,2},{2,4},{4,6},{6,0},{1,3},{3,5},{5,7},{7,1},{8,10},{10,12},{12... | collective-permute-start | bytes 983048 | tf_op jit(solution)/shard_map/ppermute | solution.py:343
  70.5 23.0 %collective-permute-start.9 = (bf16[1280,128]{1,0:T(8,128)(2,1)S(1)}, bf16[1280,128]{1,0:T(8,128)(2,1)S(1)}, u32[]{:S(2)}, u32[]{:S(2)}) collective-permute-start(bf16[1280,128]{1,0:T(8,128)(2,1)S(1)} %slice.52), channel_id=1, source_target_pairs={{0,6},{2,0},{4,2},{6,4},{1,7},{3,1},{5,3},{7,5},{8,14},{10,8},{12,... | collective-permute-start | bytes 983048 | tf_op jit(solution)/shard_map/ppermute | solution.py:343
  73.6 19.9 %copy-start.6 = (bf16[2560,128]{1,0:T(8,128)(2,1)}, bf16[2560,128]{1,0:T(8,128)(2,1)S(1)}, u32[]{:S(2)}) copy-start(bf16[2560,128]{1,0:T(8,128)(2,1)S(1)} %constant_dynamic-update-slice_fusion.refs_4_.rest_6_) | copy-start | bytes 1966084
  93.5 0.9 copy-start.7
  107.9 4.5 %collective-permute-start.10 = (f32[8,264,256]{2,1,0:T(8,128)}, f32[8,264,256]{2,1,0:T(8,128)S(1)}, u32[]{:S(2)}, u32[]{:S(2)}) collective-permute-start(f32[8,264,256]{2,1,0:T(8,128)} %get-tuple-element.15.rest_8_), channel_id=1, source_target_pairs={{0,1},{1,0},{2,3},{3,2},{4,5},{5,4},{6,7},{7,6},{8,9},{9,8},{10,11... | collective-permute-start | bytes 6488072 | tf_op jit(solution)/shard_map/ppermute | solution.py:347
  112.3 1.3 copy-start.8
  140.7 4.7 %copy-start.9 = (f32[8,64,256]{2,1,0:T(8,128)S(1)}, f32[8,64,256]{2,1,0:T(8,128)}, u32[]{:S(2)}) copy-start(f32[8,64,256]{2,1,0:T(8,128)} %get-tuple-element.18) | copy-start | bytes 1572868
  140.7 22.2 %all-to-all-start.1 = ((bf16[8,512,128]{2,1,0:T(8,128)(2,1)}), bf16[8,512,128]{2,1,0:T(8,128)(2,1)S(1)}, u32[]{:S(2)}, u32[]{:S(2)}) async-start(bf16[8,512,128]{2,1,0:T(8,128)(2,1)} %get-tuple-element.19), calls=%async_computation.1 | async-start | bytes 2097152 | tf_op jit(solution)/shard_map/all_to_all | solution.py:388
  146.2 1.6 collective-permute-start.11

commit v3 on v2

v3 whole, which is shorter than its diff:
```python
import functools
import math

import jax
import jax.numpy as jnp
from jax import lax
from jax.experimental import pallas as pl
from jax.experimental.pallas import tpu as pltpu
from jax.sharding import Mesh, PartitionSpec as P

FLOOR = -1e30
LOW = -1e29
F32 = jnp.float32
BF16 = jnp.bfloat16
HEADS = ("zl", "y")
COLS = ("zh", "x")
BLK = 128
GROUPS = 8
COLUMNS = 8
HD = 128
FD = 64
TR = 2 * BLK
TK = COLUMNS * BLK
PAIRS = GROUPS // 2
HALF = BLK // 2
WIDTH = 2
KEYS = WIDTH * BLK
SLAB = 2 * BLK + HALF
ROWS = BLK + HALF
VROWS = 208
ROW_L = VROWS
ROW_M = VROWS + HD
CARRY = ROW_M + 8
PACK = 2 * HD + 8
PLACES = ((0, 0), (1, 0), (0, 3), (0, 1), (1, 3), (1, 1), (0, 2), (1, 2))
KEY_SCALE = 1.0 / math.sqrt(HD)
FEAT_SCALE = 1.0 / math.sqrt(FD)
SCORE = KEY_SCALE * math.log2(math.e)


def nn(a, b):
    return lax.dot_general(a, b, (((1,), (0,)), ((), ())), preferred_element_type=F32)


def nt(a, b):
    return lax.dot_general(a, b, (((1,), (1,)), ((), ())), preferred_element_type=F32)


def tn(a, b):
    return lax.dot_general(a, b, (((0,), (0,)), ((), ())), preferred_element_type=F32)


def split(a):
    high = a.astype(BF16)
    return high, (a - high.astype(F32)).astype(BF16)


def iota(shape, dim):
    return lax.broadcasted_iota(jnp.int32, shape, dim)


def column(where, j):
    zh, x = PLACES[j]
    return (where[0] + zh) % 2, (where[1] + x) % 4


def row_positions(blocks, where, k):
    lane = iota((1, TR), 1)
    at = k * 16 + where[0] * 8 + where[1] * 2
    first = blocks[at] * BLK
    second = blocks[at + 1] * BLK - BLK
    return lane + jnp.where(lane < BLK, first, second)


def tile_mask(blocks, where, k, columns):
    pos_rows = row_positions(blocks, where, k)
    step = iota((BLK, 1), 0)
    parts = []
    for j in columns:
        zh, x = column(where, j)
        parts.append(pos_rows >= step + blocks[k * 16 + zh * 8 + x * 2 + where[2]] * BLK)
    return jnp.concatenate(parts, axis=0)


def feats_of(ref, e, at):
    packed = ref[e, at : at + HALF, :]
    return packed[:, :FD], packed[:, FD:]


def core_slices(where):
    for mine, slot in ((True, where[2]), (False, 1 - where[2])):
        yield mine, pl.ds(pl.multiple_of(slot * BLK, BLK), BLK)


def forward_kernel(columns, first, last, *refs):
    blocks, where, own, other = refs[:4]
    slabs = refs[4 : 4 + WIDTH]
    refs = refs[4 + WIDTH :]
    if not first:
        carry_in, sums_in = refs[:2]
        refs = refs[2:]
    if last:
        pack, okf, states = refs[:3]
        carry, sums, prefix = refs[3:6]
        refs = refs[6:]
    else:
        carry, sums = refs[:2]
        refs = refs[2:]
    k_buf, kf_buf, vft, q_buf, qf_buf = refs
    i = pl.program_id(0)
    a, b = 2 * i, 2 * i + 1
    if last:

        @pl.when(i == 0)
        def _():
            prefix[...] = jnp.zeros_like(prefix)

    if first:
        carry[...] = jnp.zeros_like(carry)
        for e in range(2):
            carry[e, ROW_M : ROW_M + 1, :] = jnp.full((1, TR), LOW, F32)
        sums[...] = jnp.zeros_like(sums)
    else:
        carry[...] = carry_in[...]
        sums[...] = sums_in[...]
    for mine, at in core_slices(where):
        ref = own if mine else other
        for e in range(2):
            q_buf[e, at, :] = ref[e, :BLK, :]
            qf_buf[e, at, :] = jnp.concatenate(feats_of(ref, e, BLK), axis=0)

    def update(plans):
        olds = [carry[e, :VROWS, :] for e in range(2)]
        tops = [carry[e, ROW_M : ROW_M + 1, :] for e in range(2)]
        scores = []
        for e, plan in enumerate(plans):
            found = []
            for g, mask in plan:
                s = nt(k_buf[g], q_buf[e])
                found.append(s if mask is None else jnp.where(mask, s, FLOOR))
            scores.append(found)
        results = []
        for old, top, found, plan in zip(olds, tops, scores, plans):
            new = top
            for s in found:
                new = jnp.maximum(new, jnp.max(s, axis=0, keepdims=True))
            total = old * jnp.exp2((top - new) * SCORE)
            for s, (g, _) in zip(found, plan):
                total = total + nn(vft[g], jnp.exp2((s - new) * SCORE).astype(BF16))
            results.append((total, new))
        for e, (total, new) in enumerate(results):
            carry[e, :VROWS, :] = total
            carry[e, ROW_M : ROW_M + 1, :] = new

    def full(u, c):
        update([[(2 * u, None), (2 * u + 1, None)]] * 2)
        return c

    lax.fori_loop(0, i, full, 0)
    tail_rows = jnp.where(iota((VROWS - HD - FD, KEYS), 0) == 0, 1.0, 0.0).astype(BF16)
    for e, g in enumerate((a, b)):
        for j, slab in enumerate(slabs):
            at = slice(j * BLK, (j + 1) * BLK)
            feats = jnp.concatenate(feats_of(slab, e, 2 * BLK), axis=0)
            k_buf[g, at, :] = slab[e, :BLK, :]
            kf_buf[g, at, :] = feats
            vft[g, :HD, at] = slab[e, BLK : 2 * BLK, :].T
            vft[g, HD : HD + FD, at] = feats.T
        vft[g, HD + FD :, :] = tail_rows
    masks = [tile_mask(blocks, where, g, columns) for g in (a, b)]
    update([[(a, masks[0])], [(a, None), (b, masks[1])]])
    for e, (g, mask) in enumerate(zip((a, b), masks)):
        inv_n = FEAT_SCALE / (row_positions(blocks, where, g) + 1).astype(F32)
        student = jnp.where(mask, nt(kf_buf[g], qf_buf[e]) * inv_n, 0.0).astype(BF16)
        carry[e, ROW_L:ROW_M, :] += nn(vft[g, :HD, :], student)
        sums[e] += nn(vft[g, : HD + FD, :], kf_buf[g])
        if last:
            state = prefix[...]
            high, low = split(state[:HD])
            linear = (nt(high, qf_buf[e]) + nt(low, qf_buf[e])) * inv_n
            pack[e, :HD, :] = carry[e, :HD, :]
            pack[e, HD : 2 * HD, :] = carry[e, ROW_L:ROW_M, :] + linear
            norm = carry[e, HD + FD : HD + FD + 1, :]
            top = carry[e, ROW_M : ROW_M + 1, :]
            pack[e, 2 * HD :, :] = jnp.where(iota((8, TR), 0) == 0, norm, top)
            okf[e] = carry[e, HD : HD + FD, :]
            states[e] = state
            prefix[...] = state + sums[e]


def backward_kernel(blocks, where, own, other, *rest):
    slabs = rest[:COLUMNS]
    mine, theirs, okf, states, dk_out, dq_out = rest[COLUMNS : COLUMNS + 6]
    k_buf, v_buf, kf_buf, kft, q_buf, qf_buf, r_buf, bias, acc, w_state, u_state = rest[COLUMNS + 6 :]
    step = pl.program_id(0)
    i = PAIRS - 1 - step
    a, b = 2 * i, 2 * i + 1

    @pl.when(step == 0)
    def _():
        w_state[...] = jnp.zeros_like(w_state)
        u_state[...] = jnp.zeros_like(u_state)

    for here, at in core_slices(where):
        ref = own if here else other
        for e, k in enumerate((a, b)):
            q_buf[k, at, :] = ref[e, :BLK, :]
            qf_buf[k, :, at] = jnp.concatenate([part.T for part in feats_of(ref, e, BLK)], axis=1)
    for e, k in enumerate((a, b)):
        l0, m0 = mine[e, 2 * HD : 2 * HD + 1, :], mine[e, 2 * HD + 1 : 2 * HD + 2, :]
        l1, m1 = theirs[e, 2 * HD : 2 * HD + 1, :], theirs[e, 2 * HD + 1 : 2 * HD + 2, :]
        top = jnp.maximum(m0, m1)
        w0, w1 = jnp.exp2((m0 - top) * SCORE), jnp.exp2((m1 - top) * SCORE)
        total = l0 * w0 + l1 * w1
        w0, w1 = w0 / total, w1 / total
        mixed = (mine[e, :HD, :] * w0 + theirs[e, :HD, :] * w1) - (
            mine[e, HD : 2 * HD, :] + theirs[e, HD : 2 * HD, :]
        )
        r_buf[e] = mixed.astype(BF16)
        n = (row_positions(blocks, where, k) + 1).astype(F32)
        bias[k] = (0.5 * jnp.log2(n) - jnp.log2(total)) - top * SCORE
        dq_out[e] = okf[e] * (w0 * jnp.sqrt(n))
        for j, slab in enumerate(slabs):
            at = slice(j * BLK, (j + 1) * BLK)
            feats = jnp.concatenate(feats_of(slab, e, 2 * BLK), axis=0)
            k_buf[e, at, :] = slab[e, :BLK, :]
            v_buf[e, at, :] = slab[e, BLK : 2 * BLK, :]
            kf_buf[e, at, :] = feats
            kft[e, :, at] = feats.T

    def teach(e, k):
        return nt(k_buf[e], q_buf[k]) * SCORE + bias[k]

    def diagonal(g, e):
        mask = tile_mask(blocks, where, g, range(COLUMNS))
        n = (row_positions(blocks, where, g) + 1).astype(F32)
        weight = FEAT_SCALE / jnp.sqrt(n)
        r_tile, qf_tile, v_tile, kf_tile = r_buf[e], qf_buf[g], v_buf[e], kf_buf[e]
        w_high, w_low = split(w_state[...])
        u_high, u_low = split(u_state[...])
        total = (nt(w_high, v_tile) + nt(w_low, v_tile)) - (nt(u_high, kf_tile) + nt(u_low, kf_tile))
        linear = nn(v_tile, r_tile) * KEY_SCALE - nn(kf_tile, qf_tile) * weight
        linear = jnp.where(mask, linear, 0.0)
        p = jnp.exp2(jnp.where(mask, teach(e, g), FLOOR))
        total = total + nt(qf_tile, (p + linear).astype(BF16))
        if e == 0:
            p = jnp.exp2(teach(e, b)).astype(BF16)
            total = total + nt(qf_buf[b], p)
        acc[e] = total
        s_high, s_low = split(states[e])
        query = tn(s_high[:HD], r_tile) + tn(s_low[:HD], r_tile)
        student = nn(s_high[HD:], qf_tile) + nn(s_low[HD:], qf_tile)
        query = query * KEY_SCALE - student * weight + nn(kft[e], linear.astype(BF16))
        dq_out[e] = -(dq_out[e] + query)
        w_state[...] += nt(qf_tile, r_tile) * KEY_SCALE
        f_high, f_low = split(qf_tile.astype(F32) * weight)
        u_state[...] += nt(f_high, qf_tile) + nt(f_low, qf_tile)

    diagonal(b, 1)
    diagonal(a, 0)

    def full(t, c):
        olds = [acc[e] for e in range(2)]
        for e in range(2):
            p = [jnp.exp2(score).astype(BF16) for score in [teach(e, 2 * t), teach(e, 2 * t + 1)]]
            olds[e] = olds[e] + (nt(qf_buf[2 * t], p[0]) + nt(qf_buf[2 * t + 1], p[1]))
        for e in range(2):
            acc[e] = olds[e]
        return c

    lax.fori_loop(i + 1, PAIRS, full, 0)
    result = -jnp.concatenate([acc[0], acc[1]], axis=0).astype(dk_out.dtype)
    for j in range(COLUMNS):
        zh, x = column(where, j)
        dk_out[zh * 4 + x] = result[:, j * BLK : (j + 1) * BLK]


def smem(count):
    return [pl.BlockSpec(memory_space=pltpu.SMEM)] * count


def by_pair(rows, lanes, down=False):
    return pl.BlockSpec((2, rows, lanes), lambda s: (PAIRS - 1 - s if down else s, 0, 0))


def forward(columns, blocks, where, own, other, slabs, carried, last):
    carry = ((GROUPS, CARRY, TR), F32)
    sums = ((GROUPS, HD + FD, FD), F32)
    carry_specs = [by_pair(CARRY, TR), by_pair(HD + FD, FD)]
    if last:
        outs = [((GROUPS, PACK, TR), F32), ((GROUPS, FD, TR), F32), sums]
        out_specs = [by_pair(PACK, TR), by_pair(FD, TR), by_pair(HD + FD, FD)]
        scratch = [pltpu.VMEM((2, CARRY, TR), F32), pltpu.VMEM((2, HD + FD, FD), F32)]
        scratch += [pltpu.VMEM((HD + FD, FD), F32)]
    else:
        outs, out_specs, scratch = [carry, sums], carry_specs, []
    scratch += [
        pltpu.VMEM((GROUPS, KEYS, HD), BF16),
        pltpu.VMEM((GROUPS, KEYS, FD), BF16),
        pltpu.VMEM((GROUPS, VROWS, KEYS), BF16),
        pltpu.VMEM((2, TR, HD), BF16),
        pltpu.VMEM((2, TR, FD), BF16),
    ]
    in_specs = smem(2) + [by_pair(ROWS, HD)] * 2 + [by_pair(SLAB, HD)] * WIDTH
    return pl.pallas_call(
        functools.partial(forward_kernel, columns, not carried, last),
        grid=(PAIRS,),
        out_shape=tuple(jax.ShapeDtypeStruct(*o) for o in outs),
        in_specs=in_specs + (carry_specs if carried else []),
        out_specs=out_specs,
        scratch_shapes=scratch,
        cost_estimate=pl.CostEstimate(flops=6_000_000_000, transcendentals=2_400_000, bytes_accessed=8_000_000),
        name="forward" + str(columns[0]),
    )(blocks, where, own, other, *[slabs[j] for j in columns], *carried)


def backward(blocks, where, own, other, slabs, mine, theirs, okf, states):
    in_specs = smem(2) + [by_pair(ROWS, HD, True)] * 2 + [by_pair(SLAB, HD, True)] * COLUMNS
    in_specs += [by_pair(PACK, TR, True)] * 2 + [by_pair(FD, TR, True), by_pair(HD + FD, FD, True)]
    return pl.pallas_call(
        backward_kernel,
        grid=(PAIRS,),
        out_shape=(
            jax.ShapeDtypeStruct((COLUMNS, PAIRS * BLK, BLK), BF16),
            jax.ShapeDtypeStruct((GROUPS, FD, TR), F32),
        ),
        in_specs=in_specs,
        out_specs=[
            pl.BlockSpec((COLUMNS, BLK, BLK), lambda s: (0, PAIRS - 1 - s, 0)),
            by_pair(FD, TR, True),
        ],
        scratch_shapes=[
            pltpu.VMEM((2, TK, HD), BF16),
            pltpu.VMEM((2, TK, HD), BF16),
            pltpu.VMEM((2, TK, FD), BF16),
            pltpu.VMEM((2, FD, TK), BF16),
            pltpu.VMEM((GROUPS, TR, HD), BF16),
            pltpu.VMEM((GROUPS, FD, TR), BF16),
            pltpu.VMEM((2, HD, TR), BF16),
            pltpu.VMEM((GROUPS, 1, TR), F32),
            pltpu.VMEM((2, FD, TK), F32),
            pltpu.VMEM((FD, HD), F32),
            pltpu.VMEM((FD, FD), F32),
        ],
        cost_estimate=pl.CostEstimate(flops=20_000_000_000, transcendentals=9_400_000, bytes_accessed=16_000_000),
        name="backward",
    )(blocks, where, own, other, *slabs, mine, theirs, okf, states)


def shifted(a, step):
    return lax.ppermute(a, "x", [(i, (i + step) % 4) for i in range(4)])


def across(a, axis):
    return lax.ppermute(a, axis, [(0, 1), (1, 0)])


def by_head(feats):
    return feats.reshape(2, HALF, GROUPS, FD).transpose(2, 1, 0, 3).reshape(GROUPS, HALF, 2 * FD)


def per_device(queries, keys, values, query_feats, key_feats, block_pos):
    shared = jnp.broadcast_to(jnp.concatenate([keys, values], axis=0)[None], (GROUPS, 2 * BLK, HD))
    slab = lax.all_to_all(jnp.concatenate([shared, by_head(key_feats)], axis=1), HEADS, 0, 0, tiled=True)
    far = across(slab, "zh")
    left, right = shifted(slab, 1), shifted(slab, 3)
    q_heads = queries.reshape(BLK, GROUPS, HD).transpose(1, 0, 2)
    rows = jnp.concatenate([q_heads, by_head(query_feats)], axis=1)
    own = lax.all_to_all(rows, HEADS, 0, 0, tiled=True)
    other = across(own, "c")
    far_left, far_right = shifted(far, 1), shifted(far, 3)
    behind = jnp.concatenate([shifted(left[:4], 1), shifted(right[4:], 3)], axis=0)
    far_behind = jnp.concatenate([shifted(far_left[:4], 1), shifted(far_right[4:], 3)], axis=0)
    slabs = (slab, far, left, right, far_left, far_right, behind, far_behind)
    c = lax.axis_index("c")
    where = jnp.stack([lax.axis_index("zh"), lax.axis_index("x"), c]).astype(jnp.int32)

    carried = ()
    for first in range(0, COLUMNS, WIDTH):
        columns = tuple(range(first, first + WIDTH))
        carried = forward(columns, block_pos, where, own, other, slabs, carried, first + WIDTH == COLUMNS)
    mine, okf, states = carried
    theirs = across(mine, "c")
    dk, dq = backward(block_pos, where, own, other, slabs, mine, theirs, okf, states)

    dk = lax.all_to_all(dk, COLS, 0, 0, tiled=True).astype(F32).sum(axis=0)
    dk = dk.reshape(GROUPS, FD, BLK)
    dq = dq.reshape(GROUPS, FD, 2, BLK)
    keep = lax.dynamic_slice_in_dim(dq, c, 1, 2)
    give = lax.dynamic_slice_in_dim(dq, 1 - c, 1, 2)
    dq = (keep + across(give, "c"))[:, :, 0]
    final = lax.all_to_all(jnp.concatenate([dq, dk], axis=1), HEADS, 0, 0, tiled=True)
    dq, dk = final[:, :FD].reshape(-1, BLK), final[:, FD:].reshape(-1, BLK)
    return dq.T, dk.T


def solution(mesh):
    split_mesh = Mesh(mesh.devices.reshape(2, 4, 2, 4, 2), ("zl", "y", "zh", "x", "c"))
    spec = P(("zl", "y", "zh", "x", "c"), None)
    return jax.shard_map(
        per_device,
        mesh=split_mesh,
        in_specs=(spec,) * 5 + (P(),),
        out_specs=(spec, spec),
        check_vma=False,
    )
```

time: 178 us -> 171 us (0.961)
  blocking collectives: 34.1 us -> 13.9 us
  starting transfers between devices: 20.4 us -> 30.4 us
  waiting for transfers between devices: 32.9 us -> 42.5 us
  Pallas kernels: 72.2 us -> 67.5 us
  local copies, waits for them, and re-layouts: 15.2 us -> 11.5 us
    all_to_all x2 -> x1, blocking collectives: 34.1 us -> 13.9 us  [per_device(): lax.all_to_all(jnp.concatenate([dq, dk], axis=1), HEADS, 0, 0, tiled=True)]
    all_to_all x0 -> x2, waiting for transfers between devices: none -> 11.6 us  [the longest x1 9.7 us: per_device(): lax.all_to_all(jnp.concatenate([shared, by_head(key_feats)], axis=1), HEA...]
    all_to_all x0 -> x2, starting transfers between devices: none -> 9.39 us  [the longest x1 5.94 us: per_device(): lax.all_to_all(jnp.concatenate([shared, by_head(key_feats)], axis=1), HEA...]
    ppermute x4, waiting for transfers between devices: 16.5 us -> 7.49 us  [across(): return lax.ppermute(a, axis, [(0, 1), (1, 0)])]
    ppermute x8, waiting for transfers between devices: 1.46 us -> 8.22 us  [shifted(): return lax.ppermute(a, 'x', [(i, (i + step) % 4) for i in range(4)])]
    unnamed x28 -> x25, local copies, waits for them, and re-layouts: 8.91 us -> 4.9 us
    pallas_call x1, Pallas kernels: 27 us -> 24.1 us  [backward(): pl.pallas_call(backward_kernel, grid=(PAIRS,), out_shape=(jax.ShapeDtypeS...]
    pallas_call x3 -> x4, Pallas kernels: 45.3 us -> 43.4 us  [forward(): pl.pallas_call(functools.partial(forward_kernel, columns, not carried, la...]
  transfers between devices with their start and end apart: 13 -> 15, of which waited for: 5 -> 7; matrix products, arithmetic and copies ran while one was open for 4% -> 4% of each run, Pallas kernels for 18% -> 19%
where the time goes in v3:
time: 171 us; the launch traced here: 170 us
  Pallas kernels  67.5 us (39%)
  waiting for transfers between devices  42.5 us (25%)
  starting transfers between devices  30.4 us (18%)
  blocking collectives  13.9 us (8%)
  local copies, waits for them, and re-layouts  11.5 us (7%)
  other arithmetic  3.33 us (2%)
    pallas_call x4, Pallas kernels, forward(): pl.pallas_call(functools.partial(forward_kernel, columns, not carried, la...  43.4 us
    pallas_call x1, Pallas kernels, backward(): pl.pallas_call(backward_kernel, grid=(PAIRS,), out_shape=(jax.ShapeDtypeS...  24.1 us
    all_to_all x1, waiting for transfers between devices, per_device(): dk = lax.all_to_all(dk, COLS, 0, 0, tiled=True).astype(F32).sum(axis=0)  15.2 us
    all_to_all x1, blocking collectives, per_device(): lax.all_to_all(jnp.concatenate([dq, dk], axis=1), HEADS, 0, 0, tiled=True)  13.9 us
    ppermute x8, starting transfers between devices, shifted(): return lax.ppermute(a, 'x', [(i, (i + step) % 4) for i in range(4)])  13.3 us
    all_to_all x1, waiting for transfers between devices, per_device(): lax.all_to_all(jnp.concatenate([shared, by_head(key_feats)], axis=1), HEA...  9.7 us
    ppermute x8, waiting for transfers between devices, shifted(): return lax.ppermute(a, 'x', [(i, (i + step) % 4) for i in range(4)])  8.22 us
    ppermute x4, waiting for transfers between devices, across(): return lax.ppermute(a, axis, [(0, 1), (1, 0)])  7.49 us
  transfers between devices with their start and end apart: 15, of which 7 were waited for; matrix products, arithmetic and copies ran while one was open for 4% of the time, Pallas kernels for 19%

profile of v3, /device:TPU:0, one launch (start us, length us, event | category | flops | bytes accessed | tf_op | source)
XLA Modules:
  0.0 170.1 jit_solution(10544040505664786983)
XLA Ops:
  0.6 1.1 reshape.35
  3.0 0.9 pad_maximum_fusion
  3.9 5.9 %all-to-all-start.1 = ((bf16[8,320,128]{2,1,0:T(8,128)(2,1)}), bf16[8,320,128]{2,1,0:T(8,128)(2,1)S(1)}, u32[]{:S(2)}, u32[]{:S(2)}) async-start(bf16[8,320,128]{2,1,0:T(8,128)(2,1)} %pad_maximum_fusion), calls=%async_computation.1 | async-start | bytes 1310720 | tf_op jit(solution)/shard_map/all_to_all | solution.py:364
  11.6 9.7 %all-to-all-done.1.refs_4_.rest_0_ = bf16[8,320,128]{2,1,0:T(8,128)(2,1)S(1)} async-done(((bf16[8,320,128]{2,1,0:T(8,128)(2,1)}), bf16[8,320,128]{2,1,0:T(8,128)(2,1)S(1)}, u32[]{:S(2)}, u32[]{:S(2)}) %all-to-all-start.1) | async-done | bytes 655392 | tf_op jit(solution)/shard_map/all_to_all | solution.py:364
  21.3 3.5 %all-to-all-start = ((bf16[8,192,128]{2,1,0:T(8,128)(2,1)}), bf16[8,192,128]{2,1,0:T(8,128)(2,1)S(1)}, u32[]{:S(2)}, u32[]{:S(2)}) async-start(bf16[8,192,128]{2,1,0:T(8,128)(2,1)} %pad_maximum_fusion.2), calls=%async_computation | async-start | bytes 786432 | tf_op jit(solution)/shard_map/all_to_all | solution.py:369
  24.8 1.6 collective-permute-start.2
  26.4 1.7 %collective-permute-start.3 = (bf16[8,320,128]{2,1,0:T(8,128)(2,1)S(1)}, bf16[8,320,128]{2,1,0:T(8,128)(2,1)}, u32[]{:S(2)}, u32[]{:S(2)}) collective-permute-start(bf16[8,320,128]{2,1,0:T(8,128)(2,1)S(1)} %all-to-all-done.1.refs_4_.rest_0_), channel_id=1, source_target_pairs={{0,6},{2,0},{4,2},{6,4},{1,7},{3,1},{5,3},{7,5},{8,14},{10,8},{12,... | collective-permute-start | bytes 1966088 | tf_op jit(solution)/shard_map/ppermute | solution.py:351
  28.1 3.6 %collective-permute-start.1 = (bf16[8,320,128]{2,1,0:T(8,128)(2,1)S(1)}, bf16[8,320,128]{2,1,0:T(8,128)(2,1)}, u32[]{:S(2)}, u32[]{:S(2)}) collective-permute-start(bf16[8,320,128]{2,1,0:T(8,128)(2,1)S(1)} %all-to-all-done.1.refs_4_.rest_0_), channel_id=1, source_target_pairs={{0,8},{8,0},{1,9},{9,1},{2,10},{10,2},{3,11},{11,3},{4,12},{12,4},... | collective-permute-start | bytes 1966088 | tf_op jit(solution)/shard_map/ppermute | solution.py:355
  31.7 1.9 %all-to-all-done.refs_2_.own = bf16[8,192,128]{2,1,0:T(8,128)(2,1)S(1)} async-done(((bf16[8,192,128]{2,1,0:T(8,128)(2,1)}), bf16[8,192,128]{2,1,0:T(8,128)(2,1)S(1)}, u32[]{:S(2)}, u32[]{:S(2)}) %all-to-all-start) | async-done | bytes 393248 | tf_op jit(solution)/shard_map/all_to_all | solution.py:369
  34.2 8.2 %collective-permute-done.2.refs_4_.rest_2_ = bf16[8,320,128]{2,1,0:T(8,128)(2,1)S(1)} collective-permute-done((bf16[8,320,128]{2,1,0:T(8,128)(2,1)S(1)}, bf16[8,320,128]{2,1,0:T(8,128)(2,1)S(1)}, u32[]{:S(2)}, u32[]{:S(2)}) %collective-permute-start.2) | collective-permute-done | bytes 655392 | tf_op jit(solution)/shard_map/ppermute | solution.py:351
  42.8 1.0 slice.25
  43.8 3.0 %collective-permute-start.7 = (bf16[4,320,128]{2,1,0:T(8,128)(2,1)S(1)}, bf16[4,320,128]{2,1,0:T(8,128)(2,1)S(1)}, u32[]{:S(2)}, u32[]{:S(2)}) collective-permute-start(bf16[4,320,128]{2,1,0:T(8,128)(2,1)S(1)} %slice.25), channel_id=1, source_target_pairs={{0,6},{2,0},{4,2},{6,4},{1,7},{3,1},{5,3},{7,5},{8,14},{10,8},{12,... | collective-permute-start | bytes 983048 | tf_op jit(solution)/shard_map/ppermute | solution.py:351
  46.9 1.6 collective-permute-done.1.refs_5_.rest_1_
  48.5 1.0 collective-permute-start.4
  49.5 2.3 %collective-permute-start.5 = (bf16[8,320,128]{2,1,0:T(8,128)(2,1)}, bf16[8,320,128]{2,1,0:T(8,128)(2,1)}, u32[]{:S(2)}, u32[]{:S(2)}) collective-permute-start(bf16[8,320,128]{2,1,0:T(8,128)(2,1)} %collective-permute-done.1.refs_5_.rest_1_), channel_id=1, source_target_pairs={{0,6},{2,0},{4,2},{6,4},{1,7},{3,1},{5,3},{7,5},{8,14},{10,8},{12,... | collective-permute-start | bytes 1966088 | tf_op jit(solution)/shard_map/ppermute | solution.py:351
  52.5 10.6 %forward0.1 = (f32[8,344,256]{2,1,0:T(8,128)}, f32[8,192,64]{2,1,0:T(8,128)}) custom-call(s32[128]{0:T(128)} %blocks.1, s32[3]{0:T(128)} %pad_add_fusion.refs_1_.where, bf16[8,192,128]{2,1,0:T(8,128)(2,1)} %copy-done.2, bf16[8,192,128]{2,1,0:T(8,128)(2,1)} %copy-done.9, bf16[8,320,128]{2,1,0:T(8,128)(2,1)} %copy-done, ...), custom_call_target="tpu_custom_call" | custom-call | flops 6000000000 | bytes 8000000 | tf_op jit(solution)/shard_map/forward0/pallas_call | solution.py:305
  63.1 11.0 %forward2.1 = (f32[8,344,256]{2,1,0:T(8,128)}, f32[8,192,64]{2,1,0:T(8,128)}) custom-call(s32[128]{0:T(128)} %blocks.1, s32[3]{0:T(128)} %pad_add_fusion.refs_1_.where, bf16[8,192,128]{2,1,0:T(8,128)(2,1)} %copy-done.2, bf16[8,192,128]{2,1,0:T(8,128)(2,1)} %copy-done.9, bf16[8,320,128]{2,1,0:T(8,128)(2,1)} %copy-done.4, ...), custom_call_target="tpu_custom_call" | custom-call | flops 6000000000 | bytes 8000000 | tf_op jit(solution)/shard_map/forward2/pallas_call | solution.py:305
  74.2 1.2 slice.26
  75.6 1.0 slice.27
  76.6 3.3 %collective-permute-start.9 = (bf16[4,320,128]{2,1,0:T(8,128)(2,1)S(1)}, bf16[4,320,128]{2,1,0:T(8,128)(2,1)S(1)}, u32[]{:S(2)}, u32[]{:S(2)}) collective-permute-start(bf16[4,320,128]{2,1,0:T(8,128)(2,1)S(1)} %slice.27), channel_id=1, source_target_pairs={{0,6},{2,0},{4,2},{6,4},{1,7},{3,1},{5,3},{7,5},{8,14},{10,8},{12,... | collective-permute-start | bytes 983048 | tf_op jit(solution)/shard_map/ppermute | solution.py:351
  79.8 10.9 %forward4.1 = (f32[8,344,256]{2,1,0:T(8,128)}, f32[8,192,64]{2,1,0:T(8,128)}) custom-call(s32[128]{0:T(128)} %blocks.1, s32[3]{0:T(128)} %pad_add_fusion.refs_1_.where, bf16[8,192,128]{2,1,0:T(8,128)(2,1)} %copy-done.2, bf16[8,192,128]{2,1,0:T(8,128)(2,1)} %copy-done.9, bf16[8,320,128]{2,1,0:T(8,128)(2,1)} %collective-permute-done.4.refs_4_.rest_4_, ...), custom_call_target="tpu_custom_call" | custom-call | flops 6000000000 | bytes 8000000 | tf_op jit(solution)/shard_map/forward4/pallas_call | solution.py:305
  90.9 0.9 copy-done.6
  91.8 10.9 %forward6.1 = (f32[8,264,256]{2,1,0:T(8,128)}, f32[8,64,256]{2,1,0:T(8,128)}, f32[8,192,64]{2,1,0:T(8,128)}) custom-call(s32[128]{0:T(128)} %blocks.1, s32[3]{0:T(128)} %pad_add_fusion.refs_1_.where, bf16[8,192,128]{2,1,0:T(8,128)(2,1)} %copy-done.2, bf16[8,192,128]{2,1,0:T(8,128)(2,1)} %copy-done.9, bf16[8,320,128]{2,1,0:T(8,128)(2,1)} %copy-done.5, ...), custom_call_target="tpu_custom_call" | custom-call | flops 6000000000 | bytes 8000000 | tf_op jit(solution)/shard_map/forward6/pallas_call | solution.py:305
  103.0 4.5 %collective-permute-done.10.rest_9_ = f32[8,264,256]{2,1,0:T(8,128)S(1)} collective-permute-done((f32[8,264,256]{2,1,0:T(8,128)}, f32[8,264,256]{2,1,0:T(8,128)S(1)}, u32[]{:S(2)}, u32[]{:S(2)}) %collective-permute-start.10) | collective-permute-done | bytes 2162720 | tf_op jit(solution)/shard_map/ppermute | solution.py:355
  107.4 1.3 copy-done.8
  108.8 24.1 %backward.1 = (bf16[8,512,128]{2,1,0:T(8,128)(2,1)}, f32[8,64,256]{2,1,0:T(8,128)}) custom-call(s32[128]{0:T(128)} %blocks.1, s32[3]{0:T(128)} %pad_add_fusion.refs_1_.where, bf16[8,192,128]{2,1,0:T(8,128)(2,1)} %copy-done.2, bf16[8,192,128]{2,1,0:T(8,128)(2,1)} %copy-done.9, bf16[8,320,128]{2,1,0:T(8,128)(2,1)} %copy-done, ...), custom_call_target="tpu_custom_call" | custom-call | flops 20000000000 | bytes 16000000 | tf_op jit(solution)/shard_map/backward/pallas_call | solution.py:320
  132.8 3.7 %all-to-all-start.2 = ((bf16[8,512,128]{2,1,0:T(8,128)(2,1)}), bf16[8,512,128]{2,1,0:T(8,128)(2,1)S(1)}, u32[]{:S(2)}, u32[]{:S(2)}) async-start(bf16[8,512,128]{2,1,0:T(8,128)(2,1)} %get-tuple-element.23), calls=%async_computation.2 | async-start | bytes 2097152 | tf_op jit(solution)/shard_map/all_to_all | solution.py:386
  137.7 1.4 collective-permute-done.11
  139.1 15.2 %all-to-all-done.2 = bf16[8,512,128]{2,1,0:T(8,128)(2,1)S(1)} async-done(((bf16[8,512,128]{2,1,0:T(8,128)(2,1)}), bf16[8,512,128]{2,1,0:T(8,128)(2,1)S(1)}, u32[]{:S(2)}, u32[]{:S(2)}) %all-to-all-start.2) | async-done | bytes 1048608 | tf_op jit(solution)/shard_map/all_to_all | solution.py:386
  154.5 13.9 %all_to_all.20 = f32[8,128,128]{2,1,0:T(8,128)S(1)} all-to-all(f32[8,128,128]{2,1,0:T(8,128)S(1)} %pad_maximum_fusion.1), channel_id=1, replica_groups=mesh['zl'=2,'y'=4,'zh'=2,'x'=4,'c'=2] {'zl','y'}, dimensions={0} | all-to-all | bytes 1048576 | tf_op jit(solution)/shard_map/all_to_all | solution.py:392
  168.4 0.8 copy.18
  169.2 0.8 copy.19
  (53 shorter events, 6.6 us)
Async XLA Ops:
  1.7 8.1 %copy-start.7 = (bf16[128,512]{1,0:T(8,128)(2,1)S(1)}, bf16[128,512]{1,0:T(8,128)(2,1)}, u32[]{:S(2)}) copy-start(bf16[128,512]{1,0:T(8,128)(2,1)} %param.9) | copy-start | bytes 393220
  3.0 7.5 %copy-start.3 = (bf16[128,1024]{1,0:T(8,128)(2,1)S(1)}, bf16[128,1024]{1,0:T(8,128)(2,1)}, u32[]{:S(2)}) copy-start(bf16[128,1024]{1,0:T(8,128)(2,1)} %param.6) | copy-start | bytes 786436
  3.9 17.4 %all-to-all-start.1 = ((bf16[8,320,128]{2,1,0:T(8,128)(2,1)}), bf16[8,320,128]{2,1,0:T(8,128)(2,1)S(1)}, u32[]{:S(2)}, u32[]{:S(2)}) async-start(bf16[8,320,128]{2,1,0:T(8,128)(2,1)} %pad_maximum_fusion), calls=%async_computation.1 | async-start | bytes 1310720 | tf_op jit(solution)/shard_map/all_to_all | solution.py:364
  21.3 30.4 %copy-start = (bf16[8,320,128]{2,1,0:T(8,128)(2,1)}, bf16[8,320,128]{2,1,0:T(8,128)(2,1)S(1)}, u32[]{:S(2)}) copy-start(bf16[8,320,128]{2,1,0:T(8,128)(2,1)S(1)} %all-to-all-done.1.refs_4_.rest_0_) | copy-start | bytes 1966084
  21.3 12.2 %all-to-all-start = ((bf16[8,192,128]{2,1,0:T(8,128)(2,1)}), bf16[8,192,128]{2,1,0:T(8,128)(2,1)S(1)}, u32[]{:S(2)}, u32[]{:S(2)}) async-start(bf16[8,192,128]{2,1,0:T(8,128)(2,1)} %pad_maximum_fusion.2), calls=%async_computation | async-start | bytes 786432 | tf_op jit(solution)/shard_map/all_to_all | solution.py:369
  24.8 17.6 %collective-permute-start.2 = (bf16[8,320,128]{2,1,0:T(8,128)(2,1)S(1)}, bf16[8,320,128]{2,1,0:T(8,128)(2,1)S(1)}, u32[]{:S(2)}, u32[]{:S(2)}) collective-permute-start(bf16[8,320,128]{2,1,0:T(8,128)(2,1)S(1)} %all-to-all-done.1.refs_4_.rest_0_), channel_id=1, source_target_pairs={{0,2},{2,4},{4,6},{6,0},{1,3},{3,5},{5,7},{7,1},{8,10},{10,12},{12... | collective-permute-start | bytes 1966088 | tf_op jit(solution)/shard_map/ppermute | solution.py:351
  26.4 16.5 %collective-permute-start.3 = (bf16[8,320,128]{2,1,0:T(8,128)(2,1)S(1)}, bf16[8,320,128]{2,1,0:T(8,128)(2,1)}, u32[]{:S(2)}, u32[]{:S(2)}) collective-permute-start(bf16[8,320,128]{2,1,0:T(8,128)(2,1)S(1)} %all-to-all-done.1.refs_4_.rest_0_), channel_id=1, source_target_pairs={{0,6},{2,0},{4,2},{6,4},{1,7},{3,1},{5,3},{7,5},{8,14},{10,8},{12,... | collective-permute-start | bytes 1966088 | tf_op jit(solution)/shard_map/ppermute | solution.py:351
  28.1 20.4 %collective-permute-start.1 = (bf16[8,320,128]{2,1,0:T(8,128)(2,1)S(1)}, bf16[8,320,128]{2,1,0:T(8,128)(2,1)}, u32[]{:S(2)}, u32[]{:S(2)}) collective-permute-start(bf16[8,320,128]{2,1,0:T(8,128)(2,1)S(1)} %all-to-all-done.1.refs_4_.rest_0_), channel_id=1, source_target_pairs={{0,8},{8,0},{1,9},{9,1},{2,10},{10,2},{3,11},{11,3},{4,12},{12,4},... | collective-permute-start | bytes 1966088 | tf_op jit(solution)/shard_map/ppermute | solution.py:355
  33.6 18.1 %copy-start.2 = (bf16[8,192,128]{2,1,0:T(8,128)(2,1)}, bf16[8,192,128]{2,1,0:T(8,128)(2,1)S(1)}, u32[]{:S(2)}) copy-start(bf16[8,192,128]{2,1,0:T(8,128)(2,1)S(1)} %all-to-all-done.refs_2_.own) | copy-start | bytes 1179652
  33.6 18.1 %collective-permute-start = (bf16[8,192,128]{2,1,0:T(8,128)(2,1)S(1)}, bf16[8,192,128]{2,1,0:T(8,128)(2,1)S(1)}, u32[]{:S(2)}, u32[]{:S(2)}) collective-permute-start(bf16[8,192,128]{2,1,0:T(8,128)(2,1)S(1)} %all-to-all-done.refs_2_.own), channel_id=1, source_target_pairs={{0,1},{1,0},{2,3},{3,2},{4,5},{5,4},{6,7},{7,6},{8,9},{9,8},{10,11... | collective-permute-start | bytes 1179656 | tf_op jit(solution)/shard_map/ppermute | solution.py:355
  42.4 20.6 %copy-start.4 = (bf16[8,320,128]{2,1,0:T(8,128)(2,1)}, bf16[8,320,128]{2,1,0:T(8,128)(2,1)S(1)}, u32[]{:S(2)}) copy-start(bf16[8,320,128]{2,1,0:T(8,128)(2,1)S(1)} %collective-permute-done.2.refs_4_.rest_2_) | copy-start | bytes 1966084
  42.5 31.6 %collective-permute-start.6 = (bf16[4,320,128]{2,1,0:T(8,128)(2,1)S(1)}, bf16[4,320,128]{2,1,0:T(8,128)(2,1)S(1)}, u32[]{:S(2)}, u32[]{:S(2)}) collective-permute-start(bf16[4,320,128]{2,1,0:T(8,128)(2,1)S(1)} %slice.24), channel_id=1, source_target_pairs={{0,2},{2,4},{4,6},{6,0},{1,3},{3,5},{5,7},{7,1},{8,10},{10,12},{12... | collective-permute-start | bytes 983048 | tf_op jit(solution)/shard_map/ppermute | solution.py:351
  43.8 30.3 %collective-permute-start.7 = (bf16[4,320,128]{2,1,0:T(8,128)(2,1)S(1)}, bf16[4,320,128]{2,1,0:T(8,128)(2,1)S(1)}, u32[]{:S(2)}, u32[]{:S(2)}) collective-permute-start(bf16[4,320,128]{2,1,0:T(8,128)(2,1)S(1)} %slice.25), channel_id=1, source_target_pairs={{0,6},{2,0},{4,2},{6,4},{1,7},{3,1},{5,3},{7,5},{8,14},{10,8},{12,... | collective-permute-start | bytes 983048 | tf_op jit(solution)/shard_map/ppermute | solution.py:351
  48.5 25.7 %collective-permute-start.4 = (bf16[8,320,128]{2,1,0:T(8,128)(2,1)}, bf16[8,320,128]{2,1,0:T(8,128)(2,1)}, u32[]{:S(2)}, u32[]{:S(2)}) collective-permute-start(bf16[8,320,128]{2,1,0:T(8,128)(2,1)} %collective-permute-done.1.refs_5_.rest_1_), channel_id=1, source_target_pairs={{0,2},{2,4},{4,6},{6,0},{1,3},{3,5},{5,7},{7,1},{8,10},{10,12},{12... | collective-permute-start | bytes 1966088 | tf_op jit(solution)/shard_map/ppermute | solution.py:351
  49.5 26.1 %collective-permute-start.5 = (bf16[8,320,128]{2,1,0:T(8,128)(2,1)}, bf16[8,320,128]{2,1,0:T(8,128)(2,1)}, u32[]{:S(2)}, u32[]{:S(2)}) collective-permute-start(bf16[8,320,128]{2,1,0:T(8,128)(2,1)} %collective-permute-done.1.refs_5_.rest_1_), channel_id=1, source_target_pairs={{0,6},{2,0},{4,2},{6,4},{1,7},{3,1},{5,3},{7,5},{8,14},{10,8},{12,... | collective-permute-start | bytes 1966088 | tf_op jit(solution)/shard_map/ppermute | solution.py:351
  51.7 0.8 copy-start.9
  74.2 16.6 %copy-start.5 = (bf16[8,320,128]{2,1,0:T(8,128)(2,1)}, bf16[8,320,128]{2,1,0:T(8,128)(2,1)S(1)}, u32[]{:S(2)}) copy-start(bf16[8,320,128]{2,1,0:T(8,128)(2,1)S(1)} %constant_dynamic-update-slice_fusion.refs_4_.rest_6_) | copy-start | bytes 1966084
  75.5 15.3 %collective-permute-start.8 = (bf16[4,320,128]{2,1,0:T(8,128)(2,1)S(1)}, bf16[4,320,128]{2,1,0:T(8,128)(2,1)S(1)}, u32[]{:S(2)}, u32[]{:S(2)}) collective-permute-start(bf16[4,320,128]{2,1,0:T(8,128)(2,1)S(1)} %slice.26), channel_id=1, source_target_pairs={{0,2},{2,4},{4,6},{6,0},{1,3},{3,5},{5,7},{7,1},{8,10},{10,12},{12... | collective-permute-start | bytes 983048 | tf_op jit(solution)/shard_map/ppermute | solution.py:351
  76.6 14.3 %collective-permute-start.9 = (bf16[4,320,128]{2,1,0:T(8,128)(2,1)S(1)}, bf16[4,320,128]{2,1,0:T(8,128)(2,1)S(1)}, u32[]{:S(2)}, u32[]{:S(2)}) collective-permute-start(bf16[4,320,128]{2,1,0:T(8,128)(2,1)S(1)} %slice.27), channel_id=1, source_target_pairs={{0,6},{2,0},{4,2},{6,4},{1,7},{3,1},{5,3},{7,5},{8,14},{10,8},{12,... | collective-permute-start | bytes 983048 | tf_op jit(solution)/shard_map/ppermute | solution.py:351
  90.9 0.9 copy-start.6
  102.7 4.7 %collective-permute-start.10 = (f32[8,264,256]{2,1,0:T(8,128)}, f32[8,264,256]{2,1,0:T(8,128)S(1)}, u32[]{:S(2)}, u32[]{:S(2)}) collective-permute-start(f32[8,264,256]{2,1,0:T(8,128)} %get-tuple-element.19.rest_8_), channel_id=1, source_target_pairs={{0,1},{1,0},{2,3},{3,2},{4,5},{5,4},{6,7},{7,6},{8,9},{9,8},{10,11... | collective-permute-start | bytes 6488072 | tf_op jit(solution)/shard_map/ppermute | solution.py:355
  107.4 1.3 copy-start.8
  132.8 3.7 %copy-start.1 = (f32[8,64,256]{2,1,0:T(8,128)S(1)}, f32[8,64,256]{2,1,0:T(8,128)}, u32[]{:S(2)}) copy-start(f32[8,64,256]{2,1,0:T(8,128)} %get-tuple-element.22) | copy-start | bytes 1572868
  132.8 21.4 %all-to-all-start.2 = ((bf16[8,512,128]{2,1,0:T(8,128)(2,1)}), bf16[8,512,128]{2,1,0:T(8,128)(2,1)S(1)}, u32[]{:S(2)}, u32[]{:S(2)}) async-start(bf16[8,512,128]{2,1,0:T(8,128)(2,1)} %get-tuple-element.23), calls=%async_computation.2 | async-start | bytes 2097152 | tf_op jit(solution)/shard_map/all_to_all | solution.py:386
  137.4 1.6 collective-permute-start.11

commit v4 on v3

--- a/solution.py
+++ b/solution.py
@@ -23,8 +23,9 @@
 TK = COLUMNS * BLK
 PAIRS = GROUPS // 2
 HALF = BLK // 2
-WIDTH = 2
+WIDTH = 4
 KEYS = WIDTH * BLK
+STEP = 4 // WIDTH
 SLAB = 2 * BLK + HALF
 ROWS = BLK + HALF
 VROWS = 208
@@ -53,6 +54,14 @@
 def split(a):
     high = a.astype(BF16)
     return high, (a - high.astype(F32)).astype(BF16)
+
+
+def stacked(a):
+    return jnp.concatenate(split(a), axis=0)
+
+
+def halves(a):
+    return a[: a.shape[0] // 2] + a[a.shape[0] // 2 :]
 
 
 def iota(shape, dim):
@@ -136,27 +145,30 @@
         for e, plan in enumerate(plans):
             found = []
             for g, mask in plan:
-                s = nt(k_buf[g], q_buf[e])
-                found.append(s if mask is None else jnp.where(mask, s, FLOOR))
+                for at in range(0, KEYS, TR):
+                    s = nt(k_buf[g, at : at + TR, :], q_buf[e])
+                    s = s if mask is None else jnp.where(mask[at : at + TR], s, FLOOR)
+                    found.append((s, g, at))
             scores.append(found)
         results = []
-        for old, top, found, plan in zip(olds, tops, scores, plans):
+        for old, top, found in zip(olds, tops, scores):
             new = top
-            for s in found:
+            for s, _, _ in found:
                 new = jnp.maximum(new, jnp.max(s, axis=0, keepdims=True))
             total = old * jnp.exp2((top - new) * SCORE)
-            for s, (g, _) in zip(found, plan):
-                total = total + nn(vft[g], jnp.exp2((s - new) * SCORE).astype(BF16))
+            probs = [jnp.exp2((s - new) * SCORE).astype(BF16) for s, _, _ in found]
+            for p, (_, g, at) in zip(probs, found):
+                total = total + nn(vft[g, :, at : at + TR], p)
             results.append((total, new))
         for e, (total, new) in enumerate(results):
             carry[e, :VROWS, :] = total
             carry[e, ROW_M : ROW_M + 1, :] = new
 
     def full(u, c):
-        update([[(2 * u, None), (2 * u + 1, None)]] * 2)
+        update([[(STEP * u + e, None) for e in range(STEP)]] * 2)
         return c
 
-    lax.fori_loop(0, i, full, 0)
+    lax.fori_loop(0, 2 * i // STEP, full, 0)
     tail_rows = jnp.where(iota((VROWS - HD - FD, KEYS), 0) == 0, 1.0, 0.0).astype(BF16)
     for e, g in enumerate((a, b)):
         for j, slab in enumerate(slabs):
@@ -184,22 +196,21 @@
             top = carry[e, ROW_M : ROW_M + 1, :]
             pack[e, 2 * HD :, :] = jnp.where(iota((8, TR), 0) == 0, norm, top)
             okf[e] = carry[e, HD : HD + FD, :]
-            states[e] = state
+            states[e] = state.T
             prefix[...] = state + sums[e]
 
 
 def backward_kernel(blocks, where, own, other, *rest):
     slabs = rest[:COLUMNS]
     mine, theirs, okf, states, dk_out, dq_out = rest[COLUMNS : COLUMNS + 6]
-    k_buf, v_buf, kf_buf, kft, q_buf, qf_buf, r_buf, bias, acc, w_state, u_state = rest[COLUMNS + 6 :]
+    k_buf, vk_buf, kft, q_buf, qf_buf, rk_buf, bias, acc, state = rest[COLUMNS + 6 :]
     step = pl.program_id(0)
     i = PAIRS - 1 - step
     a, b = 2 * i, 2 * i + 1
 
     @pl.when(step == 0)
     def _():
-        w_state[...] = jnp.zeros_like(w_state)
-        u_state[...] = jnp.zeros_like(u_state)
+        state[...] = jnp.zeros_like(state)
 
     for here, at in core_slices(where):
         ref = own if here else other
@@ -216,16 +227,16 @@
         mixed = (mine[e, :HD, :] * w0 + theirs[e, :HD, :] * w1) - (
             mine[e, HD : 2 * HD, :] + theirs[e, HD : 2 * HD, :]
         )
-        r_buf[e] = mixed.astype(BF16)
         n = (row_positions(blocks, where, k) + 1).astype(F32)
+        student = split(qf_buf[k].astype(F32) * (-FEAT_SCALE / (KEY_SCALE * jnp.sqrt(n))))
+        rk_buf[e] = jnp.concatenate([mixed.astype(BF16), *student], axis=0)
         bias[k] = (0.5 * jnp.log2(n) - jnp.log2(total)) - top * SCORE
         dq_out[e] = okf[e] * (w0 * jnp.sqrt(n))
         for j, slab in enumerate(slabs):
             at = slice(j * BLK, (j + 1) * BLK)
             feats = jnp.concatenate(feats_of(slab, e, 2 * BLK), axis=0)
             k_buf[e, at, :] = slab[e, :BLK, :]
-            v_buf[e, at, :] = slab[e, BLK : 2 * BLK, :]
-            kf_buf[e, at, :] = feats
+            vk_buf[e, at, :] = jnp.concatenate([slab[e, BLK : 2 * BLK, :], feats, feats], axis=1)
             kft[e, :, at] = feats.T
 
     def teach(e, k):
@@ -233,28 +244,20 @@
 
     def diagonal(g, e):
         mask = tile_mask(blocks, where, g, range(COLUMNS))
-        n = (row_positions(blocks, where, g) + 1).astype(F32)
-        weight = FEAT_SCALE / jnp.sqrt(n)
-        r_tile, qf_tile, v_tile, kf_tile = r_buf[e], qf_buf[g], v_buf[e], kf_buf[e]
-        w_high, w_low = split(w_state[...])
-        u_high, u_low = split(u_state[...])
-        total = (nt(w_high, v_tile) + nt(w_low, v_tile)) - (nt(u_high, kf_tile) + nt(u_low, kf_tile))
-        linear = nn(v_tile, r_tile) * KEY_SCALE - nn(kf_tile, qf_tile) * weight
-        linear = jnp.where(mask, linear, 0.0)
+        rk_tile, qf_tile, vk_tile = rk_buf[e], qf_buf[g], vk_buf[e]
+        linear = jnp.where(mask, nn(vk_tile, rk_tile) * KEY_SCALE, 0.0)
         p = jnp.exp2(jnp.where(mask, teach(e, g), FLOOR))
+        total = halves(nt(stacked(state[...]), vk_tile)) * KEY_SCALE
         total = total + nt(qf_tile, (p + linear).astype(BF16))
         if e == 0:
             p = jnp.exp2(teach(e, b)).astype(BF16)
             total = total + nt(qf_buf[b], p)
         acc[e] = total
-        s_high, s_low = split(states[e])
-        query = tn(s_high[:HD], r_tile) + tn(s_low[:HD], r_tile)
-        student = nn(s_high[HD:], qf_tile) + nn(s_low[HD:], qf_tile)
-        query = query * KEY_SCALE - student * weight + nn(kft[e], linear.astype(BF16))
+        past = states[e]
+        query = halves(nn(stacked(jnp.concatenate([past, past[:, HD:]], axis=1)), rk_tile)) * KEY_SCALE
+        query = query + nn(kft[e], linear.astype(BF16))
         dq_out[e] = -(dq_out[e] + query)
-        w_state[...] += nt(qf_tile, r_tile) * KEY_SCALE
-        f_high, f_low = split(qf_tile.astype(F32) * weight)
-        u_state[...] += nt(f_high, qf_tile) + nt(f_low, qf_tile)
+        state[...] += nt(qf_tile, rk_tile)
 
     diagonal(b, 1)
     diagonal(a, 0)
@@ -288,8 +291,8 @@
     sums = ((GROUPS, HD + FD, FD), F32)
     carry_specs = [by_pair(CARRY, TR), by_pair(HD + FD, FD)]
     if last:
-        outs = [((GROUPS, PACK, TR), F32), ((GROUPS, FD, TR), F32), sums]
-        out_specs = [by_pair(PACK, TR), by_pair(FD, TR), by_pair(HD + FD, FD)]
+        outs = [((GROUPS, PACK, TR), F32), ((GROUPS, FD, TR), F32), ((GROUPS, FD, HD + FD), F32)]
+        out_specs = [by_pair(PACK, TR), by_pair(FD, TR), by_pair(FD, HD + FD)]
         scratch = [pltpu.VMEM((2, CARRY, TR), F32), pltpu.VMEM((2, HD + FD, FD), F32)]
         scratch += [pltpu.VMEM((HD + FD, FD), F32)]
     else:
@@ -311,12 +314,12 @@
         scratch_shapes=scratch,
         cost_estimate=pl.CostEstimate(flops=6_000_000_000, transcendentals=2_400_000, bytes_accessed=8_000_000),
         name="forward" + str(columns[0]),
-    )(blocks, where, own, other, *[slabs[j] for j in columns], *carried)
+    )(blocks, where, own, other, *slabs, *carried)
 
 
 def backward(blocks, where, own, other, slabs, mine, theirs, okf, states):
     in_specs = smem(2) + [by_pair(ROWS, HD, True)] * 2 + [by_pair(SLAB, HD, True)] * COLUMNS
-    in_specs += [by_pair(PACK, TR, True)] * 2 + [by_pair(FD, TR, True), by_pair(HD + FD, FD, True)]
+    in_specs += [by_pair(PACK, TR, True)] * 2 + [by_pair(FD, TR, True), by_pair(FD, HD + FD, True)]
     return pl.pallas_call(
         backward_kernel,
         grid=(PAIRS,),
@@ -331,16 +334,14 @@
         ],
         scratch_shapes=[
             pltpu.VMEM((2, TK, HD), BF16),
-            pltpu.VMEM((2, TK, HD), BF16),
-            pltpu.VMEM((2, TK, FD), BF16),
+            pltpu.VMEM((2, TK, TR), BF16),
             pltpu.VMEM((2, FD, TK), BF16),
             pltpu.VMEM((GROUPS, TR, HD), BF16),
             pltpu.VMEM((GROUPS, FD, TR), BF16),
-            pltpu.VMEM((2, HD, TR), BF16),
+            pltpu.VMEM((2, TR, TR), BF16),
             pltpu.VMEM((GROUPS, 1, TR), F32),
             pltpu.VMEM((2, FD, TK), F32),
-            pltpu.VMEM((FD, HD), F32),
-            pltpu.VMEM((FD, FD), F32),
+            pltpu.VMEM((FD, TR), F32),
         ],
         cost_estimate=pl.CostEstimate(flops=20_000_000_000, transcendentals=9_400_000, bytes_accessed=16_000_000),
         name="backward",
@@ -370,28 +371,25 @@
     other = across(own, "c")
     far_left, far_right = shifted(far, 1), shifted(far, 3)
     behind = jnp.concatenate([shifted(left[:4], 1), shifted(right[4:], 3)], axis=0)
+    c = lax.axis_index("c")
+    where = jnp.stack([lax.axis_index("zh"), lax.axis_index("x"), c]).astype(jnp.int32)
+
+    carried = forward((0, 1, 2, 3), block_pos, where, own, other, (slab, far, left, right), (), False)
+    far_left, far_right, *carried = lax.optimization_barrier((far_left, far_right, *carried))
     far_behind = jnp.concatenate([shifted(far_left[:4], 1), shifted(far_right[4:], 3)], axis=0)
     slabs = (slab, far, left, right, far_left, far_right, behind, far_behind)
-    c = lax.axis_index("c")
-    where = jnp.stack([lax.axis_index("zh"), lax.axis_index("x"), c]).astype(jnp.int32)
-
-    carried = ()
-    for first in range(0, COLUMNS, WIDTH):
-        columns = tuple(range(first, first + WIDTH))
-        carried = forward(columns, block_pos, where, own, other, slabs, carried, first + WIDTH == COLUMNS)
-    mine, okf, states = carried
+    mine, okf, states = forward((4, 5, 6, 7), block_pos, where, own, other, slabs[4:], carried, True)
     theirs = across(mine, "c")
     dk, dq = backward(block_pos, where, own, other, slabs, mine, theirs, okf, states)
 
     dk = lax.all_to_all(dk, COLS, 0, 0, tiled=True).astype(F32).sum(axis=0)
-    dk = dk.reshape(GROUPS, FD, BLK)
     dq = dq.reshape(GROUPS, FD, 2, BLK)
     keep = lax.dynamic_slice_in_dim(dq, c, 1, 2)
     give = lax.dynamic_slice_in_dim(dq, 1 - c, 1, 2)
     dq = (keep + across(give, "c"))[:, :, 0]
-    final = lax.all_to_all(jnp.concatenate([dq, dk], axis=1), HEADS, 0, 0, tiled=True)
-    dq, dk = final[:, :FD].reshape(-1, BLK), final[:, FD:].reshape(-1, BLK)
-    return dq.T, dk.T
+    final = jnp.concatenate([dq, dk.reshape(GROUPS, FD, BLK)], axis=1)
+    final = lax.all_to_all(final, HEADS, 0, 0, tiled=True)
+    return final[:, :FD].reshape(-1, BLK).T, final[:, FD:].reshape(-1, BLK).T
 
 
 def solution(mesh):

time: 171 us -> 164 us (0.959)
  Pallas kernels: 67.5 us -> 53.8 us
  waiting for transfers between devices: 42.5 us -> 48.4 us
  starting transfers between devices: 30.4 us -> 32.6 us
    pallas_call x4 -> x2, Pallas kernels: 43.4 us -> 32.8 us  [forward(): pl.pallas_call(functools.partial(forward_kernel, columns, not carried, la...]
    all_to_all x1, waiting for transfers between devices: 1.89 us -> 11 us  [per_device(): own = lax.all_to_all(rows, HEADS, 0, 0, tiled=True)]
    pallas_call x1, Pallas kernels: 24.1 us -> 21 us  [backward(): pl.pallas_call(backward_kernel, grid=(PAIRS,), out_shape=(jax.ShapeDtypeS...]
    all_to_all x1, starting transfers between devices: 3.7 us -> 5.94 us  [per_device(): dk = lax.all_to_all(dk, COLS, 0, 0, tiled=True).astype(F32).sum(axis=0)]
    ppermute x8, waiting for transfers between devices: 8.22 us -> 6.06 us  [shifted(): return lax.ppermute(a, 'x', [(i, (i + step) % 4) for i in range(4)])]
  transfers between devices with their start and end apart: 15 -> 15, of which waited for: 7 -> 7; matrix products, arithmetic and copies ran while one was open for 4% -> 4% of each run, Pallas kernels for 19% -> 10%
where the time goes in v4:
time: 164 us; the launch traced here: 163 us
  Pallas kernels  53.8 us (33%)
  waiting for transfers between devices  48.4 us (30%)
  starting transfers between devices  32.6 us (20%)
  blocking collectives  13 us (8%)
  local copies, waits for them, and re-layouts  11.3 us (7%)
  other arithmetic  3.26 us (2%)
    pallas_call x2, Pallas kernels, forward(): pl.pallas_call(functools.partial(forward_kernel, columns, not carried, la...  32.8 us
    pallas_call x1, Pallas kernels, backward(): pl.pallas_call(backward_kernel, grid=(PAIRS,), out_shape=(jax.ShapeDtypeS...  21 us
    all_to_all x1, waiting for transfers between devices, per_device(): dk = lax.all_to_all(dk, COLS, 0, 0, tiled=True).astype(F32).sum(axis=0)  15 us
    ppermute x8, starting transfers between devices, shifted(): return lax.ppermute(a, 'x', [(i, (i + step) % 4) for i in range(4)])  13.3 us
    all_to_all x1, blocking collectives, per_device(): final = lax.all_to_all(final, HEADS, 0, 0, tiled=True)  13 us
    all_to_all x1, waiting for transfers between devices, per_device(): own = lax.all_to_all(rows, HEADS, 0, 0, tiled=True)  11 us
    all_to_all x1, waiting for transfers between devices, per_device(): lax.all_to_all(jnp.concatenate([shared, by_head(key_feats)], axis=1), HEA...  10.5 us
    ppermute x8, waiting for transfers between devices, shifted(): return lax.ppermute(a, 'x', [(i, (i + step) % 4) for i in range(4)])  6.06 us
  transfers between devices with their start and end apart: 15, of which 7 were waited for; matrix products, arithmetic and copies ran while one was open for 4% of the time, Pallas kernels for 10%

profile of v4, /device:TPU:0, one launch (start us, length us, event | category | flops | bytes accessed | tf_op | source)
XLA Modules:
  0.0 163.3 jit_solution(11459265696995265222)
XLA Ops:
  0.6 1.1 reshape.35
  2.2 0.8 pad_maximum_fusion.3
  3.0 0.9 pad_maximum_fusion
  3.9 5.9 %all-to-all-start.1 = ((bf16[8,320,128]{2,1,0:T(8,128)(2,1)}), bf16[8,320,128]{2,1,0:T(8,128)(2,1)S(1)}, u32[]{:S(2)}, u32[]{:S(2)}) async-start(bf16[8,320,128]{2,1,0:T(8,128)(2,1)} %pad_maximum_fusion), calls=%async_computation.1 | async-start | bytes 1310720 | tf_op jit(solution)/shard_map/all_to_all | solution.py:365
  10.9 10.5 %all-to-all-done.1.refs_4_.rest_0_ = bf16[8,320,128]{2,1,0:T(8,128)(2,1)S(1)} async-done(((bf16[8,320,128]{2,1,0:T(8,128)(2,1)}), bf16[8,320,128]{2,1,0:T(8,128)(2,1)S(1)}, u32[]{:S(2)}, u32[]{:S(2)}) %all-to-all-start.1) | async-done | bytes 655392 | tf_op jit(solution)/shard_map/all_to_all | solution.py:365
  21.4 3.6 %collective-permute-start.1 = (bf16[8,320,128]{2,1,0:T(8,128)(2,1)S(1)}, bf16[8,320,128]{2,1,0:T(8,128)(2,1)}, u32[]{:S(2)}, u32[]{:S(2)}) collective-permute-start(bf16[8,320,128]{2,1,0:T(8,128)(2,1)S(1)} %all-to-all-done.1.refs_4_.rest_0_), channel_id=1, source_target_pairs={{0,8},{8,0},{1,9},{9,1},{2,10},{10,2},{3,11},{11,3},{4,12},{12,4},... | collective-permute-start | bytes 1966088 | tf_op jit(solution)/shard_map/ppermute | solution.py:356
  24.9 0.8 pad_maximum_fusion.2
  25.7 3.5 %all-to-all-start = ((bf16[8,192,128]{2,1,0:T(8,128)(2,1)}), bf16[8,192,128]{2,1,0:T(8,128)(2,1)S(1)}, u32[]{:S(2)}, u32[]{:S(2)}) async-start(bf16[8,192,128]{2,1,0:T(8,128)(2,1)} %pad_maximum_fusion.2), calls=%async_computation | async-start | bytes 786432 | tf_op jit(solution)/shard_map/all_to_all | solution.py:370
  29.2 1.6 collective-permute-start.2
  30.7 1.7 %collective-permute-start.3 = (bf16[8,320,128]{2,1,0:T(8,128)(2,1)S(1)}, bf16[8,320,128]{2,1,0:T(8,128)(2,1)}, u32[]{:S(2)}, u32[]{:S(2)}) collective-permute-start(bf16[8,320,128]{2,1,0:T(8,128)(2,1)S(1)} %all-to-all-done.1.refs_4_.rest_0_), channel_id=1, source_target_pairs={{0,6},{2,0},{4,2},{6,4},{1,7},{3,1},{5,3},{7,5},{8,14},{10,8},{12,... | collective-permute-start | bytes 1966088 | tf_op jit(solution)/shard_map/ppermute | solution.py:352
  32.5 11.0 %all-to-all-done.refs_2_.own = bf16[8,192,128]{2,1,0:T(8,128)(2,1)S(1)} async-done(((bf16[8,192,128]{2,1,0:T(8,128)(2,1)}), bf16[8,192,128]{2,1,0:T(8,128)(2,1)S(1)}, u32[]{:S(2)}, u32[]{:S(2)}) %all-to-all-start) | async-done | bytes 393248 | tf_op jit(solution)/shard_map/all_to_all | solution.py:370
  43.5 1.6 collective-permute-start.4
  45.0 1.7 %collective-permute-start.5 = (bf16[8,320,128]{2,1,0:T(8,128)(2,1)}, bf16[8,320,128]{2,1,0:T(8,128)(2,1)}, u32[]{:S(2)}, u32[]{:S(2)}) collective-permute-start(bf16[8,320,128]{2,1,0:T(8,128)(2,1)} %collective-permute-done.1.refs_5_.rest_1_), channel_id=1, source_target_pairs={{0,6},{2,0},{4,2},{6,4},{1,7},{3,1},{5,3},{7,5},{8,14},{10,8},{12,... | collective-permute-start | bytes 1966088 | tf_op jit(solution)/shard_map/ppermute | solution.py:352
  47.7 1.0 slice.25
  48.7 3.0 %collective-permute-start.7 = (bf16[4,320,128]{2,1,0:T(8,128)(2,1)S(1)}, bf16[4,320,128]{2,1,0:T(8,128)(2,1)S(1)}, u32[]{:S(2)}, u32[]{:S(2)}) collective-permute-start(bf16[4,320,128]{2,1,0:T(8,128)(2,1)S(1)} %slice.25), channel_id=1, source_target_pairs={{0,6},{2,0},{4,2},{6,4},{1,7},{3,1},{5,3},{7,5},{8,14},{10,8},{12,... | collective-permute-start | bytes 983048 | tf_op jit(solution)/shard_map/ppermute | solution.py:352
  51.8 0.8 copy-done.9
  52.6 15.7 %forward0.1 = (f32[8,344,256]{2,1,0:T(8,128)}, f32[8,192,64]{2,1,0:T(8,128)}) custom-call(s32[128]{0:T(128)} %blocks.1, s32[3]{0:T(128)} %pad_add_fusion.refs_1_.where, bf16[8,192,128]{2,1,0:T(8,128)(2,1)} %copy-done.2, bf16[8,192,128]{2,1,0:T(8,128)(2,1)} %copy-done.9, bf16[8,320,128]{2,1,0:T(8,128)(2,1)} %copy-done, ...), custom_call_target="tpu_custom_call" | custom-call | flops 6000000000 | bytes 8000000 | tf_op jit(solution)/shard_map/forward0/pallas_call | solution.py:308
  68.3 1.0 slice.20
  69.4 1.0 slice.21
  70.4 3.3 %collective-permute-start.9 = (bf16[4,320,128]{2,1,0:T(8,128)(2,1)S(1)}, bf16[4,320,128]{2,1,0:T(8,128)(2,1)S(1)}, u32[]{:S(2)}, u32[]{:S(2)}) collective-permute-start(bf16[4,320,128]{2,1,0:T(8,128)(2,1)S(1)} %slice.21), channel_id=1, source_target_pairs={{0,6},{2,0},{4,2},{6,4},{1,7},{3,1},{5,3},{7,5},{8,14},{10,8},{12,... | collective-permute-start | bytes 983048 | tf_op jit(solution)/shard_map/ppermute | solution.py:352
  73.8 5.7 %collective-permute-done.8 = bf16[4,320,128]{2,1,0:T(8,128)(2,1)S(1)} collective-permute-done((bf16[4,320,128]{2,1,0:T(8,128)(2,1)S(1)}, bf16[4,320,128]{2,1,0:T(8,128)(2,1)S(1)}, u32[]{:S(2)}, u32[]{:S(2)}) %collective-permute-start.8) | collective-permute-done | bytes 327712 | tf_op jit(solution)/shard_map/ppermute | solution.py:352
  79.9 0.9 copy-done.6
  80.8 17.1 %forward4.1 = (f32[8,264,256]{2,1,0:T(8,128)}, f32[8,64,256]{2,1,0:T(8,128)}, f32[8,64,192]{2,1,0:T(8,128)}) custom-call(s32[128]{0:T(128)} %blocks.1, s32[3]{0:T(128)} %pad_add_fusion.refs_1_.where, bf16[8,192,128]{2,1,0:T(8,128)(2,1)} %copy-done.2, bf16[8,192,128]{2,1,0:T(8,128)(2,1)} %copy-done.9, ...), custom_call_target="tpu_custom_call" | custom-call | flops 6000000000 | bytes 8000000 | tf_op jit(solution)/shard_map/forward4/pallas_call | solution.py:308
  98.1 4.5 %collective-permute-done.10.rest_9_ = f32[8,264,256]{2,1,0:T(8,128)S(1)} collective-permute-done((f32[8,264,256]{2,1,0:T(8,128)}, f32[8,264,256]{2,1,0:T(8,128)S(1)}, u32[]{:S(2)}, u32[]{:S(2)}) %collective-permute-start.10) | collective-permute-done | bytes 2162720 | tf_op jit(solution)/shard_map/ppermute | solution.py:356
  102.6 1.3 copy-done.8
  103.9 21.0 %backward.1 = (bf16[8,512,128]{2,1,0:T(8,128)(2,1)}, f32[8,64,256]{2,1,0:T(8,128)}) custom-call(s32[128]{0:T(128)} %blocks.1, s32[3]{0:T(128)} %pad_add_fusion.refs_1_.where, bf16[8,192,128]{2,1,0:T(8,128)(2,1)} %copy-done.2, bf16[8,192,128]{2,1,0:T(8,128)(2,1)} %copy-done.9, bf16[8,320,128]{2,1,0:T(8,128)(2,1)} %copy-done, ...), custom_call_target="tpu_custom_call" | custom-call | flops 20000000000 | bytes 16000000 | tf_op jit(solution)/shard_map/backward/pallas_call | solution.py:323
  125.0 5.9 %all-to-all-start.2 = ((bf16[8,512,128]{2,1,0:T(8,128)(2,1)}), bf16[8,512,128]{2,1,0:T(8,128)(2,1)S(1)}, u32[]{:S(2)}, u32[]{:S(2)}) async-start(bf16[8,512,128]{2,1,0:T(8,128)(2,1)} %get-tuple-element.23), calls=%async_computation.2 | async-start | bytes 2097152 | tf_op jit(solution)/shard_map/all_to_all | solution.py:385
  131.9 1.5 collective-permute-done.11
  133.5 15.0 %all-to-all-done.2 = bf16[8,512,128]{2,1,0:T(8,128)(2,1)S(1)} async-done(((bf16[8,512,128]{2,1,0:T(8,128)(2,1)}), bf16[8,512,128]{2,1,0:T(8,128)(2,1)S(1)}, u32[]{:S(2)}, u32[]{:S(2)}) %all-to-all-start.2) | async-done | bytes 1048608 | tf_op jit(solution)/shard_map/all_to_all | solution.py:385
  148.6 13.0 %all_to_all.20 = f32[8,128,128]{2,1,0:T(8,128)S(1)} all-to-all(f32[8,128,128]{2,1,0:T(8,128)S(1)} %pad_maximum_fusion.1), channel_id=1, replica_groups=mesh['zl'=2,'y'=4,'zh'=2,'x'=4,'c'=2] {'zl','y'}, dimensions={0} | all-to-all | bytes 1048576 | tf_op jit(solution)/shard_map/all_to_all | solution.py:391
  161.6 0.8 copy.18
  162.5 0.8 copy.19
  (51 shorter events, 4.4 us)
Async XLA Ops:
  1.7 8.1 %copy-start.7 = (bf16[128,512]{1,0:T(8,128)(2,1)S(1)}, bf16[128,512]{1,0:T(8,128)(2,1)}, u32[]{:S(2)}) copy-start(bf16[128,512]{1,0:T(8,128)(2,1)} %param.9) | copy-start | bytes 393220
  3.0 7.5 %copy-start.3 = (bf16[128,1024]{1,0:T(8,128)(2,1)S(1)}, bf16[128,1024]{1,0:T(8,128)(2,1)}, u32[]{:S(2)}) copy-start(bf16[128,1024]{1,0:T(8,128)(2,1)} %param.6) | copy-start | bytes 786436
  3.9 17.4 %all-to-all-start.1 = ((bf16[8,320,128]{2,1,0:T(8,128)(2,1)}), bf16[8,320,128]{2,1,0:T(8,128)(2,1)S(1)}, u32[]{:S(2)}, u32[]{:S(2)}) async-start(bf16[8,320,128]{2,1,0:T(8,128)(2,1)} %pad_maximum_fusion), calls=%async_computation.1 | async-start | bytes 1310720 | tf_op jit(solution)/shard_map/all_to_all | solution.py:365
  21.4 30.4 %copy-start = (bf16[8,320,128]{2,1,0:T(8,128)(2,1)}, bf16[8,320,128]{2,1,0:T(8,128)(2,1)S(1)}, u32[]{:S(2)}) copy-start(bf16[8,320,128]{2,1,0:T(8,128)(2,1)S(1)} %all-to-all-done.1.refs_4_.rest_0_) | copy-start | bytes 1966084
  21.4 22.1 %collective-permute-start.1 = (bf16[8,320,128]{2,1,0:T(8,128)(2,1)S(1)}, bf16[8,320,128]{2,1,0:T(8,128)(2,1)}, u32[]{:S(2)}, u32[]{:S(2)}) collective-permute-start(bf16[8,320,128]{2,1,0:T(8,128)(2,1)S(1)} %all-to-all-done.1.refs_4_.rest_0_), channel_id=1, source_target_pairs={{0,8},{8,0},{1,9},{9,1},{2,10},{10,2},{3,11},{11,3},{4,12},{12,4},... | collective-permute-start | bytes 1966088 | tf_op jit(solution)/shard_map/ppermute | solution.py:356
  25.7 17.7 %all-to-all-start = ((bf16[8,192,128]{2,1,0:T(8,128)(2,1)}), bf16[8,192,128]{2,1,0:T(8,128)(2,1)S(1)}, u32[]{:S(2)}, u32[]{:S(2)}) async-start(bf16[8,192,128]{2,1,0:T(8,128)(2,1)} %pad_maximum_fusion.2), calls=%async_computation | async-start | bytes 786432 | tf_op jit(solution)/shard_map/all_to_all | solution.py:370
  29.2 18.2 %collective-permute-start.2 = (bf16[8,320,128]{2,1,0:T(8,128)(2,1)S(1)}, bf16[8,320,128]{2,1,0:T(8,128)(2,1)S(1)}, u32[]{:S(2)}, u32[]{:S(2)}) collective-permute-start(bf16[8,320,128]{2,1,0:T(8,128)(2,1)S(1)} %all-to-all-done.1.refs_4_.rest_0_), channel_id=1, source_target_pairs={{0,2},{2,4},{4,6},{6,0},{1,3},{3,5},{5,7},{7,1},{8,10},{10,12},{12... | collective-permute-start | bytes 1966088 | tf_op jit(solution)/shard_map/ppermute | solution.py:352
  30.7 17.0 %collective-permute-start.3 = (bf16[8,320,128]{2,1,0:T(8,128)(2,1)S(1)}, bf16[8,320,128]{2,1,0:T(8,128)(2,1)}, u32[]{:S(2)}, u32[]{:S(2)}) collective-permute-start(bf16[8,320,128]{2,1,0:T(8,128)(2,1)S(1)} %all-to-all-done.1.refs_4_.rest_0_), channel_id=1, source_target_pairs={{0,6},{2,0},{4,2},{6,4},{1,7},{3,1},{5,3},{7,5},{8,14},{10,8},{12,... | collective-permute-start | bytes 1966088 | tf_op jit(solution)/shard_map/ppermute | solution.py:352
  43.4 8.3 %copy-start.2 = (bf16[8,192,128]{2,1,0:T(8,128)(2,1)}, bf16[8,192,128]{2,1,0:T(8,128)(2,1)S(1)}, u32[]{:S(2)}) copy-start(bf16[8,192,128]{2,1,0:T(8,128)(2,1)S(1)} %all-to-all-done.refs_2_.own) | copy-start | bytes 1179652
  43.4 8.3 %collective-permute-start = (bf16[8,192,128]{2,1,0:T(8,128)(2,1)S(1)}, bf16[8,192,128]{2,1,0:T(8,128)(2,1)S(1)}, u32[]{:S(2)}, u32[]{:S(2)}) collective-permute-start(bf16[8,192,128]{2,1,0:T(8,128)(2,1)S(1)} %all-to-all-done.refs_2_.own), channel_id=1, source_target_pairs={{0,1},{1,0},{2,3},{3,2},{4,5},{5,4},{6,7},{7,6},{8,9},{9,8},{10,11... | collective-permute-start | bytes 1179656 | tf_op jit(solution)/shard_map/ppermute | solution.py:356
  43.5 24.8 %collective-permute-start.4 = (bf16[8,320,128]{2,1,0:T(8,128)(2,1)}, bf16[8,320,128]{2,1,0:T(8,128)(2,1)}, u32[]{:S(2)}, u32[]{:S(2)}) collective-permute-start(bf16[8,320,128]{2,1,0:T(8,128)(2,1)} %collective-permute-done.1.refs_5_.rest_1_), channel_id=1, source_target_pairs={{0,2},{2,4},{4,6},{6,0},{1,3},{3,5},{5,7},{7,1},{8,10},{10,12},{12... | collective-permute-start | bytes 1966088 | tf_op jit(solution)/shard_map/ppermute | solution.py:352
  45.0 23.3 %collective-permute-start.5 = (bf16[8,320,128]{2,1,0:T(8,128)(2,1)}, bf16[8,320,128]{2,1,0:T(8,128)(2,1)}, u32[]{:S(2)}, u32[]{:S(2)}) collective-permute-start(bf16[8,320,128]{2,1,0:T(8,128)(2,1)} %collective-permute-done.1.refs_5_.rest_1_), channel_id=1, source_target_pairs={{0,6},{2,0},{4,2},{6,4},{1,7},{3,1},{5,3},{7,5},{8,14},{10,8},{12,... | collective-permute-start | bytes 1966088 | tf_op jit(solution)/shard_map/ppermute | solution.py:352
  47.4 4.4 %copy-start.4 = (bf16[8,320,128]{2,1,0:T(8,128)(2,1)}, bf16[8,320,128]{2,1,0:T(8,128)(2,1)S(1)}, u32[]{:S(2)}) copy-start(bf16[8,320,128]{2,1,0:T(8,128)(2,1)S(1)} %collective-permute-done.2.refs_6_.rest_2_) | copy-start | bytes 1966084
  47.4 26.3 %collective-permute-start.6 = (bf16[4,320,128]{2,1,0:T(8,128)(2,1)S(1)}, bf16[4,320,128]{2,1,0:T(8,128)(2,1)S(1)}, u32[]{:S(2)}, u32[]{:S(2)}) collective-permute-start(bf16[4,320,128]{2,1,0:T(8,128)(2,1)S(1)} %slice.24), channel_id=1, source_target_pairs={{0,2},{2,4},{4,6},{6,0},{1,3},{3,5},{5,7},{7,1},{8,10},{10,12},{12... | collective-permute-start | bytes 983048 | tf_op jit(solution)/shard_map/ppermute | solution.py:352
  48.7 25.0 %collective-permute-start.7 = (bf16[4,320,128]{2,1,0:T(8,128)(2,1)S(1)}, bf16[4,320,128]{2,1,0:T(8,128)(2,1)S(1)}, u32[]{:S(2)}, u32[]{:S(2)}) collective-permute-start(bf16[4,320,128]{2,1,0:T(8,128)(2,1)S(1)} %slice.25), channel_id=1, source_target_pairs={{0,6},{2,0},{4,2},{6,4},{1,7},{3,1},{5,3},{7,5},{8,14},{10,8},{12,... | collective-permute-start | bytes 983048 | tf_op jit(solution)/shard_map/ppermute | solution.py:352
  51.8 0.8 copy-start.9
  69.3 10.2 %collective-permute-start.8 = (bf16[4,320,128]{2,1,0:T(8,128)(2,1)S(1)}, bf16[4,320,128]{2,1,0:T(8,128)(2,1)S(1)}, u32[]{:S(2)}, u32[]{:S(2)}) collective-permute-start(bf16[4,320,128]{2,1,0:T(8,128)(2,1)S(1)} %slice.20), channel_id=1, source_target_pairs={{0,2},{2,4},{4,6},{6,0},{1,3},{3,5},{5,7},{7,1},{8,10},{10,12},{12... | collective-permute-start | bytes 983048 | tf_op jit(solution)/shard_map/ppermute | solution.py:352
  70.4 9.5 %collective-permute-start.9 = (bf16[4,320,128]{2,1,0:T(8,128)(2,1)S(1)}, bf16[4,320,128]{2,1,0:T(8,128)(2,1)S(1)}, u32[]{:S(2)}, u32[]{:S(2)}) collective-permute-start(bf16[4,320,128]{2,1,0:T(8,128)(2,1)S(1)} %slice.21), channel_id=1, source_target_pairs={{0,6},{2,0},{4,2},{6,4},{1,7},{3,1},{5,3},{7,5},{8,14},{10,8},{12,... | collective-permute-start | bytes 983048 | tf_op jit(solution)/shard_map/ppermute | solution.py:352
  73.8 6.1 %copy-start.5 = (bf16[8,320,128]{2,1,0:T(8,128)(2,1)}, bf16[8,320,128]{2,1,0:T(8,128)(2,1)S(1)}, u32[]{:S(2)}) copy-start(bf16[8,320,128]{2,1,0:T(8,128)(2,1)S(1)} %constant_dynamic-update-slice_fusion.refs_6_.rest_6_) | copy-start | bytes 1966084
  79.9 0.9 copy-start.6
  97.9 4.7 %collective-permute-start.10 = (f32[8,264,256]{2,1,0:T(8,128)}, f32[8,264,256]{2,1,0:T(8,128)S(1)}, u32[]{:S(2)}, u32[]{:S(2)}) collective-permute-start(f32[8,264,256]{2,1,0:T(8,128)} %get-tuple-element.19.rest_8_), channel_id=1, source_target_pairs={{0,1},{1,0},{2,3},{3,2},{4,5},{5,4},{6,7},{7,6},{8,9},{9,8},{10,11... | collective-permute-start | bytes 6488072 | tf_op jit(solution)/shard_map/ppermute | solution.py:356
  102.6 1.3 copy-start.8
  125.0 6.0 %copy-start.1 = (f32[8,64,256]{2,1,0:T(8,128)S(1)}, f32[8,64,256]{2,1,0:T(8,128)}, u32[]{:S(2)}) copy-start(f32[8,64,256]{2,1,0:T(8,128)} %get-tuple-element.22) | copy-start | bytes 1572868
  125.0 23.4 %all-to-all-start.2 = ((bf16[8,512,128]{2,1,0:T(8,128)(2,1)}), bf16[8,512,128]{2,1,0:T(8,128)(2,1)S(1)}, u32[]{:S(2)}, u32[]{:S(2)}) async-start(bf16[8,512,128]{2,1,0:T(8,128)(2,1)} %get-tuple-element.23), calls=%async_computation.2 | async-start | bytes 2097152 | tf_op jit(solution)/shard_map/all_to_all | solution.py:385
  131.8 1.6 collective-permute-start.11

commit v5 on v4

v5 whole, which is shorter than its diff:
```python
import math

import jax
import jax.numpy as jnp
from jax import lax
from jax.experimental import pallas as pl
from jax.experimental.pallas import tpu as pltpu
from jax.sharding import Mesh, PartitionSpec as P

FLOOR = -1e30
LOW = -1e29
F32 = jnp.float32
BF16 = jnp.bfloat16
HEADS = ("zl", "y")
COLS = ("zh", "x")
BLK = 128
GROUPS = 8
COLUMNS = 8
HD = 128
FD = 64
TR = 2 * BLK
TK = COLUMNS * BLK
PAIRS = GROUPS // 2
HALF = BLK // 2
PART = BLK + HALF
SAFE = 2.0**100
VROWS = 208
PACK = 2 * HD + 8
PLACES = ((0, 0), (1, 0), (0, 3), (0, 1), (1, 3), (1, 1), (0, 2), (1, 2))
KEY_SCALE = 1.0 / math.sqrt(HD)
FEAT_SCALE = 1.0 / math.sqrt(FD)
SCORE = KEY_SCALE * math.log2(math.e)


def nn(a, b):
    return lax.dot_general(a, b, (((1,), (0,)), ((), ())), preferred_element_type=F32)


def nt(a, b):
    return lax.dot_general(a, b, (((1,), (1,)), ((), ())), preferred_element_type=F32)


def tn(a, b):
    return lax.dot_general(a, b, (((0,), (0,)), ((), ())), preferred_element_type=F32)


def split(a):
    high = a.astype(BF16)
    return high, (a - high.astype(F32)).astype(BF16)


def stacked(a):
    return jnp.concatenate(split(a), axis=0)


def halves(a):
    return a[: a.shape[0] // 2] + a[a.shape[0] // 2 :]


def iota(shape, dim):
    return lax.broadcasted_iota(jnp.int32, shape, dim)


def column(where, j):
    zh, x = PLACES[j]
    return (where[0] + zh) % 2, (where[1] + x) % 4


def row_positions(blocks, where, k):
    lane = iota((1, TR), 1)
    at = k * 16 + where[0] * 8 + where[1] * 2
    first = blocks[at] * BLK
    second = blocks[at + 1] * BLK - BLK
    return lane + jnp.where(lane < BLK, first, second)


def tile_mask(blocks, where, k, columns):
    pos_rows = row_positions(blocks, where, k)
    step = iota((BLK, 1), 0)
    parts = []
    for j in columns:
        zh, x = column(where, j)
        parts.append(pos_rows >= step + blocks[k * 16 + zh * 8 + x * 2 + where[2]] * BLK)
    return jnp.concatenate(parts, axis=0)


def feats_of(ref, e, at):
    packed = ref[e, at : at + HALF, :]
    return packed[:, :FD], packed[:, FD:]


def core_slices(where):
    for mine, slot in ((True, where[2]), (False, 1 - where[2])):
        yield mine, pl.ds(pl.multiple_of(slot * BLK, BLK), BLK)


def forward_kernel(blocks, where, own, other, values, *refs):
    slabs = refs[:COLUMNS]
    pack, okf, states, k_buf, vft, q_buf, qf_buf, sums, tops, prefix = refs[COLUMNS:]
    i = pl.program_id(0)
    a, b = 2 * i, 2 * i + 1

    @pl.when(i == 0)
    def _():
        prefix[...] = jnp.zeros_like(prefix)

    for mine, at in core_slices(where):
        ref = own if mine else other
        for e in range(2):
            q_buf[e, at, :] = ref[e, :BLK, :]
            qf_buf[e, at, :] = jnp.concatenate(feats_of(ref, e, BLK), axis=0)

    def scores_of(e, g, mask=None):
        found = []
        for at in range(0, TK, TR):
            s = nt(k_buf[g, at : at + TR, :], q_buf[e])
            found.append(s if mask is None else jnp.where(mask[at : at + TR], s, FLOOR))
        return found

    def mixed(g, found, top):
        total = None
        for at, s in zip(range(0, TK, TR), found):
            part = nn(vft[g, :, at : at + TR], jnp.exp2((s - top) * SCORE).astype(BF16))
            total = part if total is None else total + part
        return total

    def update(plans):
        scores = [[(g, scores_of(e, g, mask)) for g, mask in plan] for e, plan in enumerate(plans)]
        for e, plan in enumerate(scores):
            old, top = sums[e], tops[e]
            new = top
            for _, found in plan:
                for s in found:
                    new = jnp.maximum(new, jnp.max(s, axis=0, keepdims=True))
            total = old * jnp.exp2((top - new) * SCORE)
            for g, found in plan:
                total = total + mixed(g, found, new)
            sums[e] = total
            tops[e] = new

    def restart(top):
        for e in range(2):
            sums[e] = jnp.zeros((VROWS, TR), F32)
            tops[e] = top[e]

    lowest = jnp.full((1, TR), LOW, F32)

    @pl.when(i == 0)
    def _():
        restart((lowest, lowest))

    @pl.when(i > 0)
    def _():
        restart([jnp.max(nt(k_buf[0, :BLK, :], q_buf[e]), axis=0, keepdims=True) for e in range(2)])

        def quick(g, c):
            scores = [scores_of(e, g) for e in range(2)]
            totals = [sums[e] + mixed(g, scores[e], tops[e]) for e in range(2)]
            for e in range(2):
                sums[e] = totals[e]
            return c

        lax.fori_loop(0, a, quick, 0)
        row = slice(HD + FD, HD + FD + 1)
        largest = jnp.max(jnp.maximum(sums[0, row, :], sums[1, row, :]))

        @pl.when(jnp.logical_not(largest < SAFE))
        def _():
            restart((lowest, lowest))

            def slow(g, c):
                update([[(g, None)]] * 2)
                return c

            lax.fori_loop(0, a, slow, 0)

    tail_rows = jnp.where(iota((VROWS - HD - FD, TK), 0) == 0, 1.0, 0.0).astype(BF16)
    feats = []
    for e, g in enumerate((a, b)):
        parts = []
        for j, slab in enumerate(slabs):
            at = slice(j * BLK, (j + 1) * BLK)
            zh, x = column(where, j)
            part = jnp.concatenate(feats_of(slab, e, BLK), axis=0)
            parts.append(part)
            k_buf[g, at, :] = slab[e, :BLK, :]
            vft[g, :HD, at] = values[e, zh * 4 + x].T
            vft[g, HD : HD + FD, at] = part.T
        vft[g, HD + FD :, :] = tail_rows
        feats.append(jnp.concatenate(parts, axis=0))
    masks = [tile_mask(blocks, where, g, range(COLUMNS)) for g in (a, b)]
    update([[(a, masks[0])], [(a, None), (b, masks[1])]])
    for e, g in enumerate((a, b)):
        inv_n = FEAT_SCALE / (row_positions(blocks, where, g) + 1).astype(F32)
        student = jnp.where(masks[e], nt(feats[e], qf_buf[e]) * inv_n, 0.0).astype(BF16)
        state = prefix[...]
        high, low = split(state[:HD])
        linear = (nt(high, qf_buf[e]) + nt(low, qf_buf[e])) * inv_n
        pack[e, :HD, :] = sums[e, :HD, :]
        pack[e, HD : 2 * HD, :] = nn(vft[g, :HD, :], student) + linear
        pack[e, 2 * HD :, :] = jnp.where(iota((8, TR), 0) == 0, sums[e, HD + FD : HD + FD + 1, :], tops[e])
        okf[e] = sums[e, HD : HD + FD, :]
        states[e] = state.T
        prefix[...] = state + nn(vft[g, : HD + FD, :], feats[e])


def backward_kernel(blocks, where, own, other, values, *rest):
    slabs = rest[:COLUMNS]
    mine, theirs, okf, states, dk_out, dq_out = rest[COLUMNS : COLUMNS + 6]
    k_buf, vk_buf, kft, q_buf, qf_buf, rk_buf, bias, acc, state = rest[COLUMNS + 6 :]
    step = pl.program_id(0)
    i = PAIRS - 1 - step
    a, b = 2 * i, 2 * i + 1

    @pl.when(step == 0)
    def _():
        state[...] = jnp.zeros_like(state)

    for here, at in core_slices(where):
        ref = own if here else other
        for e, k in enumerate((a, b)):
            q_buf[k, at, :] = ref[e, :BLK, :]
            qf_buf[k, :, at] = jnp.concatenate([part.T for part in feats_of(ref, e, BLK)], axis=1)
    for e, k in enumerate((a, b)):
        l0, m0 = mine[e, 2 * HD : 2 * HD + 1, :], mine[e, 2 * HD + 1 : 2 * HD + 2, :]
        l1, m1 = theirs[e, 2 * HD : 2 * HD + 1, :], theirs[e, 2 * HD + 1 : 2 * HD + 2, :]
        top = jnp.maximum(m0, m1)
        w0, w1 = jnp.exp2((m0 - top) * SCORE), jnp.exp2((m1 - top) * SCORE)
        total = l0 * w0 + l1 * w1
        w0, w1 = w0 / total, w1 / total
        mixed = (mine[e, :HD, :] * w0 + theirs[e, :HD, :] * w1) - (
            mine[e, HD : 2 * HD, :] + theirs[e, HD : 2 * HD, :]
        )
        n = (row_positions(blocks, where, k) + 1).astype(F32)
        student = split(qf_buf[k].astype(F32) * (-FEAT_SCALE / (KEY_SCALE * jnp.sqrt(n))))
        rk_buf[e] = jnp.concatenate([mixed.astype(BF16), *student], axis=0)
        bias[k] = (0.5 * jnp.log2(n) - jnp.log2(total)) - top * SCORE
        dq_out[e] = okf[e] * (w0 * jnp.sqrt(n))
        for j, slab in enumerate(slabs):
            at = slice(j * BLK, (j + 1) * BLK)
            zh, x = column(where, j)
            feats = jnp.concatenate(feats_of(slab, e, BLK), axis=0)
            k_buf[e, at, :] = slab[e, :BLK, :]
            vk_buf[e, at, :] = jnp.concatenate([values[e, zh * 4 + x], feats, feats], axis=1)
            kft[e, :, at] = feats.T

    def teach(e, k):
        return nt(k_buf[e], q_buf[k]) * SCORE + bias[k]

    def diagonal(g, e):
        mask = tile_mask(blocks, where, g, range(COLUMNS))
        rk_tile, qf_tile, vk_tile = rk_buf[e], qf_buf[g], vk_buf[e]
        linear = jnp.where(mask, nn(vk_tile, rk_tile) * KEY_SCALE, 0.0)
        p = jnp.exp2(jnp.where(mask, teach(e, g), FLOOR))
        total = halves(nt(stacked(state[...]), vk_tile)) * KEY_SCALE
        total = total + nt(qf_tile, (p + linear).astype(BF16))
        if e == 0:
            p = jnp.exp2(teach(e, b)).astype(BF16)
            total = total + nt(qf_buf[b], p)
        acc[e] = total
        past = states[e]
        query = halves(nn(stacked(jnp.concatenate([past, past[:, HD:]], axis=1)), rk_tile)) * KEY_SCALE
        query = query + nn(kft[e], linear.astype(BF16))
        dq_out[e] = -(dq_out[e] + query)
        state[...] += nt(qf_tile, rk_tile)

    diagonal(b, 1)
    diagonal(a, 0)

    def full(t, c):
        olds = [acc[e] for e in range(2)]
        for e in range(2):
            p = [jnp.exp2(score).astype(BF16) for score in [teach(e, 2 * t), teach(e, 2 * t + 1)]]
            olds[e] = olds[e] + (nt(qf_buf[2 * t], p[0]) + nt(qf_buf[2 * t + 1], p[1]))
        for e in range(2):
            acc[e] = olds[e]
        return c

    lax.fori_loop(i + 1, PAIRS, full, 0)
    result = -jnp.concatenate([acc[0], acc[1]], axis=0).astype(dk_out.dtype)
    for j in range(COLUMNS):
        zh, x = column(where, j)
        dk_out[zh * 4 + x] = result[:, j * BLK : (j + 1) * BLK]


def smem(count):
    return [pl.BlockSpec(memory_space=pltpu.SMEM)] * count


def by_pair(rows, lanes, down=False):
    return pl.BlockSpec((2, rows, lanes), lambda s: (PAIRS - 1 - s if down else s, 0, 0))


def values_by_pair(down=False):
    return pl.BlockSpec((2, COLUMNS, BLK, HD), lambda s: (PAIRS - 1 - s if down else s, 0, 0, 0))


def forward(blocks, where, own, other, values, slabs):
    return pl.pallas_call(
        forward_kernel,
        grid=(PAIRS,),
        out_shape=(
            jax.ShapeDtypeStruct((GROUPS, PACK, TR), F32),
            jax.ShapeDtypeStruct((GROUPS, FD, TR), F32),
            jax.ShapeDtypeStruct((GROUPS, FD, HD + FD), F32),
        ),
        in_specs=smem(2) + [by_pair(PART, HD)] * 2 + [values_by_pair()] + [by_pair(PART, HD)] * COLUMNS,
        out_specs=[by_pair(PACK, TR), by_pair(FD, TR), by_pair(FD, HD + FD)],
        scratch_shapes=[
            pltpu.VMEM((GROUPS, TK, HD), BF16),
            pltpu.VMEM((GROUPS, VROWS, TK), BF16),
            pltpu.VMEM((2, TR, HD), BF16),
            pltpu.VMEM((2, TR, FD), BF16),
            pltpu.VMEM((2, VROWS, TR), F32),
            pltpu.VMEM((2, 1, TR), F32),
            pltpu.VMEM((HD + FD, FD), F32),
        ],
        cost_estimate=pl.CostEstimate(flops=20_000_000_000, transcendentals=9_400_000, bytes_accessed=16_000_000),
        name="forward",
    )(blocks, where, own, other, values, *slabs)


def backward(blocks, where, own, other, values, slabs, mine, theirs, okf, states):
    in_specs = smem(2) + [by_pair(PART, HD, True)] * 2 + [values_by_pair(True)]
    in_specs += [by_pair(PART, HD, True)] * COLUMNS
    in_specs += [by_pair(PACK, TR, True)] * 2 + [by_pair(FD, TR, True), by_pair(FD, HD + FD, True)]
    return pl.pallas_call(
        backward_kernel,
        grid=(PAIRS,),
        out_shape=(
            jax.ShapeDtypeStruct((COLUMNS, PAIRS * BLK, BLK), BF16),
            jax.ShapeDtypeStruct((GROUPS, FD, TR), F32),
        ),
        in_specs=in_specs,
        out_specs=[
            pl.BlockSpec((COLUMNS, BLK, BLK), lambda s: (0, PAIRS - 1 - s, 0)),
            by_pair(FD, TR, True),
        ],
        scratch_shapes=[
            pltpu.VMEM((2, TK, HD), BF16),
            pltpu.VMEM((2, TK, TR), BF16),
            pltpu.VMEM((2, FD, TK), BF16),
            pltpu.VMEM((GROUPS, TR, HD), BF16),
            pltpu.VMEM((GROUPS, FD, TR), BF16),
            pltpu.VMEM((2, TR, TR), BF16),
            pltpu.VMEM((GROUPS, 1, TR), F32),
            pltpu.VMEM((2, FD, TK), F32),
            pltpu.VMEM((FD, TR), F32),
        ],
        cost_estimate=pl.CostEstimate(flops=20_000_000_000, transcendentals=9_400_000, bytes_accessed=16_000_000),
        name="backward",
    )(blocks, where, own, other, values, *slabs, mine, theirs, okf, states)


def shifted(a, step):
    return lax.ppermute(a, "x", [(i, (i + step) % 4) for i in range(4)])


def across(a, axis):
    return lax.ppermute(a, axis, [(0, 1), (1, 0)])


def by_head(feats):
    return feats.reshape(2, HALF, GROUPS, FD).transpose(2, 1, 0, 3).reshape(GROUPS, HALF, 2 * FD)


def to_all(a, axes):
    return lax.all_to_all(jnp.broadcast_to(a[None], (8, *a.shape)), axes, 0, 0, tiled=True)


def per_device(queries, keys, values, query_feats, key_feats, block_pos):
    shared = jnp.broadcast_to(keys[None], (GROUPS, BLK, HD))
    slab = lax.all_to_all(jnp.concatenate([shared, by_head(key_feats)], axis=1), HEADS, 0, 0, tiled=True)
    left, right = shifted(slab, 1), shifted(slab, 3)
    far = across(slab, "zh")
    values = to_all(to_all(values, COLS), HEADS)
    q_heads = queries.reshape(BLK, GROUPS, HD).transpose(1, 0, 2)
    own = lax.all_to_all(jnp.concatenate([q_heads, by_head(query_feats)], axis=1), HEADS, 0, 0, tiled=True)
    other = across(own, "c")
    far_left, far_right = shifted(far, 1), shifted(far, 3)
    behind = jnp.concatenate([shifted(left[:4], 1), shifted(right[4:], 3)], axis=0)
    far_behind = jnp.concatenate([shifted(far_left[:4], 1), shifted(far_right[4:], 3)], axis=0)
    slabs = (slab, far, left, right, far_left, far_right, behind, far_behind)
    c = lax.axis_index("c")
    where = jnp.stack([lax.axis_index("zh"), lax.axis_index("x"), c]).astype(jnp.int32)

    mine, okf, states = forward(block_pos, where, own, other, values, slabs)
    theirs = across(mine, "c")
    dk, dq = backward(block_pos, where, own, other, values, slabs, mine, theirs, okf, states)

    dk = lax.all_to_all(dk, COLS, 0, 0, tiled=True).astype(F32).sum(axis=0)
    dq = dq.reshape(GROUPS, FD, 2, BLK)
    keep = lax.dynamic_slice_in_dim(dq, c, 1, 2)
    give = lax.dynamic_slice_in_dim(dq, 1 - c, 1, 2)
    dq = (keep + across(give, "c"))[:, :, 0]
    final = jnp.concatenate([dq, dk.reshape(GROUPS, FD, BLK)], axis=1)
    final = lax.all_to_all(final, HEADS, 0, 0, tiled=True)
    return final[:, :FD].reshape(-1, BLK).T, final[:, FD:].reshape(-1, BLK).T


def solution(mesh):
    split_mesh = Mesh(mesh.devices.reshape(2, 4, 2, 4, 2), ("zl", "y", "zh", "x", "c"))
    spec = P(("zl", "y", "zh", "x", "c"), None)
    return jax.shard_map(
        per_device,
        mesh=split_mesh,
        in_specs=(spec,) * 5 + (P(),),
        out_specs=(spec, spec),
        check_vma=False,
    )
```

time: 164 us -> 193 us (1.18)
  waiting for transfers between devices: 48.4 us -> 66.1 us
  blocking collectives: 13 us -> 28.3 us
  Pallas kernels: 53.8 us -> 43.5 us
  local copies, waits for them, and re-layouts: 11.3 us -> 15.6 us
  starting transfers between devices: 32.6 us -> 36.1 us
    ppermute x4, waiting for transfers between devices: 5.98 us -> 30.8 us  [across(): return lax.ppermute(a, axis, [(0, 1), (1, 0)])]
    all_to_all x0 -> x1, blocking collectives: none -> 10.5 us  [per_device(): lax.all_to_all(jnp.concatenate([q_heads, by_head(query_feats)], axis=1),...]
    pallas_call x2 -> x1, Pallas kernels: 32.8 us -> 22.3 us  [forward(): pl.pallas_call(forward_kernel, grid=(PAIRS,), out_shape=(jax.ShapeDtypeSt...]
    all_to_all x1 -> x2, starting transfers between devices: 3.45 us -> 11.3 us  [to_all(): lax.all_to_all(jnp.broadcast_to(a[None], (8, *a.shape)), axes, 0, 0, tile...]
    all_to_all x1, blocking collectives: 13 us -> 17.8 us  [per_device(): final = lax.all_to_all(final, HEADS, 0, 0, tiled=True)]
    all_to_all x1 -> x2, waiting for transfers between devices: 11 us -> 6.41 us  [to_all(): lax.all_to_all(jnp.broadcast_to(a[None], (8, *a.shape)), axes, 0, 0, tile...]
    all_to_all x1, waiting for transfers between devices: 10.5 us -> 6.95 us  [per_device(): lax.all_to_all(jnp.concatenate([shared, by_head(key_feats)], axis=1), HEA...]
    broadcast_in_dim x1 -> x3, local copies, waits for them, and re-layouts: 0.07 us -> 3.43 us  [the longest x2 3.4 us: to_all(): jnp.broadcast_to(a[None], (8, *a.shape))]
  transfers between devices with their start and end apart: 15 -> 16, of which waited for: 7 -> 10; matrix products, arithmetic and copies ran while one was open for 4% -> 4% of each run, Pallas kernels for 10% -> 0%
where the time goes in v5:
time: 193 us; the launch traced here: 192 us
  waiting for transfers between devices  66.1 us (34%)
  Pallas kernels  43.5 us (23%)
  starting transfers between devices  36.1 us (19%)
  blocking collectives  28.3 us (15%)
  local copies, waits for them, and re-layouts  15.6 us (8%)
    ppermute x4, waiting for transfers between devices, across(): return lax.ppermute(a, axis, [(0, 1), (1, 0)])  30.8 us
    pallas_call x1, Pallas kernels, forward(): pl.pallas_call(forward_kernel, grid=(PAIRS,), out_shape=(jax.ShapeDtypeSt...  22.3 us
    pallas_call x1, Pallas kernels, backward(): pl.pallas_call(backward_kernel, grid=(PAIRS,), out_shape=(jax.ShapeDtypeS...  21.1 us
    all_to_all x1, blocking collectives, per_device(): final = lax.all_to_all(final, HEADS, 0, 0, tiled=True)  17.8 us
    all_to_all x1, waiting for transfers between devices, per_device(): dk = lax.all_to_all(dk, COLS, 0, 0, tiled=True).astype(F32).sum(axis=0)  15 us
    ppermute x8, starting transfers between devices, shifted(): return lax.ppermute(a, 'x', [(i, (i + step) % 4) for i in range(4)])  11.6 us
    all_to_all x2, starting transfers between devices, to_all(): lax.all_to_all(jnp.broadcast_to(a[None], (8, *a.shape)), axes, 0, 0, tile...  11.3 us
    all_to_all x1, blocking collectives, per_device(): lax.all_to_all(jnp.concatenate([q_heads, by_head(query_feats)], axis=1),...  10.5 us
  transfers between devices with their start and end apart: 16, of which 10 were waited for; matrix products, arithmetic and copies ran while one was open for 4% of the time, Pallas kernels for 0%

profile of v5, /device:TPU:0, one launch (start us, length us, event | category | flops | bytes accessed | tf_op | source)
XLA Modules:
  0.0 192.2 jit_solution(14499500209877631395)
XLA Ops:
  0.7 1.5 broadcast_in_dim.6
  2.2 7.7 %all-to-all-start.1 = ((bf16[8,128,128]{2,1,0:T(8,128)(2,1)}), bf16[8,128,128]{2,1,0:T(8,128)(2,1)S(1)}, u32[]{:S(2)}, u32[]{:S(2)}) async-start(bf16[8,128,128]{2,1,0:T(8,128)(2,1)} %broadcast_in_dim.6), calls=%async_computation.1 | async-start | bytes 524288 | tf_op jit(solution)/shard_map/all_to_all | solution.py:368
  9.9 1.1 reshape.37
  12.3 6.4 %all-to-all-done.1 = bf16[8,128,128]{2,1,0:T(8,128)(2,1)S(1)} async-done(((bf16[8,128,128]{2,1,0:T(8,128)(2,1)}), bf16[8,128,128]{2,1,0:T(8,128)(2,1)S(1)}, u32[]{:S(2)}, u32[]{:S(2)}) %all-to-all-start.1) | async-done | bytes 262176 | tf_op jit(solution)/shard_map/all_to_all | solution.py:368
  18.7 4.9 %all-to-all-start.3 = ((bf16[8,192,128]{2,1,0:T(8,128)(2,1)}), bf16[8,192,128]{2,1,0:T(8,128)(2,1)S(1)}, u32[]{:S(2)}, u32[]{:S(2)}) async-start(bf16[8,192,128]{2,1,0:T(8,128)(2,1)} %pad_maximum_fusion.2), calls=%async_computation.3 | async-start | bytes 786432 | tf_op jit(solution)/shard_map/all_to_all | solution.py:373
  24.7 7.0 %all-to-all-done.3.refs_0_.rest_0_ = bf16[8,192,128]{2,1,0:T(8,128)(2,1)S(1)} async-done(((bf16[8,192,128]{2,1,0:T(8,128)(2,1)}), bf16[8,192,128]{2,1,0:T(8,128)(2,1)S(1)}, u32[]{:S(2)}, u32[]{:S(2)}) %all-to-all-start.3) | async-done | bytes 393248 | tf_op jit(solution)/shard_map/all_to_all | solution.py:373
  31.6 10.5 %all_to_all.30.own = bf16[8,192,128]{2,1,0:T(8,128)(2,1)S(1)} all-to-all(bf16[8,192,128]{2,1,0:T(8,128)(2,1)S(1)} %pad_maximum_fusion.1), channel_id=1, replica_groups=mesh['zl'=2,'y'=4,'zh'=2,'x'=4,'c'=2] {'zl','y'}, dimensions={0} | all-to-all | bytes 786432 | tf_op jit(solution)/shard_map/all_to_all | solution.py:378
  42.1 1.9 broadcast_in_dim.7
  44.0 3.6 %all-to-all-start.2 = ((bf16[8,8,128,128]{3,2,1,0:T(8,128)(2,1)}), bf16[8,8,128,128]{3,2,1,0:T(8,128)(2,1)S(1)}, u32[]{:S(2)}, u32[]{:S(2)}) async-start(bf16[8,8,128,128]{3,2,1,0:T(8,128)(2,1)} %broadcast_in_dim.7), calls=%async_computation.2 | async-start | bytes 4194304 | tf_op jit(solution)/shard_map/all_to_all | solution.py:368
  47.6 1.2 collective-permute-start.1
  48.8 0.9 collective-permute-start.2
  49.7 2.4 %collective-permute-start.3 = (bf16[8,192,128]{2,1,0:T(8,128)(2,1)S(1)}, bf16[8,192,128]{2,1,0:T(8,128)(2,1)}, u32[]{:S(2)}, u32[]{:S(2)}) collective-permute-start(bf16[8,192,128]{2,1,0:T(8,128)(2,1)S(1)} %all-to-all-done.3.refs_0_.rest_0_), channel_id=1, source_target_pairs={{0,6},{2,0},{4,2},{6,4},{1,7},{3,1},{5,3},{7,5},{8,14},{10,8},{12,... | collective-permute-start | bytes 1179656 | tf_op jit(solution)/shard_map/ppermute | solution.py:356
  52.1 24.9 %collective-permute-done.1.refs_1_.rest_1_ = bf16[8,192,128]{2,1,0:T(8,128)(2,1)} collective-permute-done((bf16[8,192,128]{2,1,0:T(8,128)(2,1)S(1)}, bf16[8,192,128]{2,1,0:T(8,128)(2,1)}, u32[]{:S(2)}, u32[]{:S(2)}) %collective-permute-start.1) | collective-permute-done | bytes 393248 | tf_op jit(solution)/shard_map/ppermute | solution.py:360
  77.7 2.5 %collective-permute-start.5 = (bf16[8,192,128]{2,1,0:T(8,128)(2,1)}, bf16[8,192,128]{2,1,0:T(8,128)(2,1)}, u32[]{:S(2)}, u32[]{:S(2)}) collective-permute-start(bf16[8,192,128]{2,1,0:T(8,128)(2,1)} %collective-permute-done.1.refs_1_.rest_1_), channel_id=1, source_target_pairs={{0,6},{2,0},{4,2},{6,4},{1,7},{3,1},{5,3},{7,5},{8,14},{10,8},{12,... | collective-permute-start | bytes 1179656 | tf_op jit(solution)/shard_map/ppermute | solution.py:356
  81.0 0.9 slice.25
  81.9 2.6 %collective-permute-start.7 = (bf16[4,192,128]{2,1,0:T(8,128)(2,1)S(1)}, bf16[4,192,128]{2,1,0:T(8,128)(2,1)S(1)}, u32[]{:S(2)}, u32[]{:S(2)}) collective-permute-start(bf16[4,192,128]{2,1,0:T(8,128)(2,1)S(1)} %slice.25), channel_id=1, source_target_pairs={{0,6},{2,0},{4,2},{6,4},{1,7},{3,1},{5,3},{7,5},{8,14},{10,8},{12,... | collective-permute-start | bytes 589832 | tf_op jit(solution)/shard_map/ppermute | solution.py:356
  85.1 2.6 %collective-permute-done.4.refs_4_.rest_4_ = bf16[8,192,128]{2,1,0:T(8,128)(2,1)} collective-permute-done((bf16[8,192,128]{2,1,0:T(8,128)(2,1)}, bf16[8,192,128]{2,1,0:T(8,128)(2,1)}, u32[]{:S(2)}, u32[]{:S(2)}) %collective-permute-start.4) | collective-permute-done | bytes 393248 | tf_op jit(solution)/shard_map/ppermute | solution.py:356
  87.7 0.9 slice.26
  88.8 1.0 collective-permute-done.6
  89.8 0.9 slice.27
  90.7 2.3 %collective-permute-start.9 = (bf16[4,192,128]{2,1,0:T(8,128)(2,1)S(1)}, bf16[4,192,128]{2,1,0:T(8,128)(2,1)S(1)}, u32[]{:S(2)}, u32[]{:S(2)}) collective-permute-start(bf16[4,192,128]{2,1,0:T(8,128)(2,1)S(1)} %slice.27), channel_id=1, source_target_pairs={{0,6},{2,0},{4,2},{6,4},{1,7},{3,1},{5,3},{7,5},{8,14},{10,8},{12,... | collective-permute-start | bytes 589832 | tf_op jit(solution)/shard_map/ppermute | solution.py:356
  93.1 2.6 %collective-permute-done.8 = bf16[4,192,128]{2,1,0:T(8,128)(2,1)S(1)} collective-permute-done((bf16[4,192,128]{2,1,0:T(8,128)(2,1)S(1)}, bf16[4,192,128]{2,1,0:T(8,128)(2,1)S(1)}, u32[]{:S(2)}, u32[]{:S(2)}) %collective-permute-start.8) | collective-permute-done | bytes 196640 | tf_op jit(solution)/shard_map/ppermute | solution.py:356
  97.3 1.4 copy-done
  98.6 22.3 %forward.1 = (f32[8,264,256]{2,1,0:T(8,128)}, f32[8,64,256]{2,1,0:T(8,128)}, f32[8,64,192]{2,1,0:T(8,128)}) custom-call(s32[128]{0:T(128)} %blocks.3, s32[3]{0:T(128)} %pad_add_fusion.where, bf16[8,192,128]{2,1,0:T(8,128)(2,1)} %copy-done.3, bf16[8,192,128]{2,1,0:T(8,128)(2,1)} %collective-permute-done.other, bf16[8,8,128,128]{3,2,1,0:T(8,128)(2,1)} %copy-done, ...), custom_call_target="tpu_custom_call" | custom-call | flops 20000000000 | bytes 16000000 | tf_op jit(solution)/shard_map/forward/pallas_call | solution.py:299
  121.3 4.5 %collective-permute-done.10.rest_9_ = f32[8,264,256]{2,1,0:T(8,128)S(1)} collective-permute-done((f32[8,264,256]{2,1,0:T(8,128)}, f32[8,264,256]{2,1,0:T(8,128)S(1)}, u32[]{:S(2)}, u32[]{:S(2)}) %collective-permute-start.10) | collective-permute-done | bytes 2162720 | tf_op jit(solution)/shard_map/ppermute | solution.py:360
  125.7 1.4 copy-done.10
  127.1 21.1 %backward.1 = (bf16[8,512,128]{2,1,0:T(8,128)(2,1)}, f32[8,64,256]{2,1,0:T(8,128)}) custom-call(s32[128]{0:T(128)} %blocks.3, s32[3]{0:T(128)} %pad_add_fusion.where, bf16[8,192,128]{2,1,0:T(8,128)(2,1)} %copy-done.3, bf16[8,192,128]{2,1,0:T(8,128)(2,1)} %collective-permute-done.other, bf16[8,8,128,128]{3,2,1,0:T(8,128)(2,1)} %copy-done, ...), custom_call_target="tpu_custom_call" | custom-call | flops 20000000000 | bytes 16000000 | tf_op jit(solution)/shard_map/backward/pallas_call | solution.py:327
  148.2 6.7 %all-to-all-start.4 = ((bf16[8,512,128]{2,1,0:T(8,128)(2,1)}), bf16[8,512,128]{2,1,0:T(8,128)(2,1)S(1)}, u32[]{:S(2)}, u32[]{:S(2)}) async-start(bf16[8,512,128]{2,1,0:T(8,128)(2,1)} %get-tuple-element.11), calls=%async_computation.4 | async-start | bytes 2097152 | tf_op jit(solution)/shard_map/all_to_all | solution.py:391
  155.9 1.5 collective-permute-done.11
  157.4 15.0 %all-to-all-done.4 = bf16[8,512,128]{2,1,0:T(8,128)(2,1)S(1)} async-done(((bf16[8,512,128]{2,1,0:T(8,128)(2,1)}), bf16[8,512,128]{2,1,0:T(8,128)(2,1)S(1)}, u32[]{:S(2)}, u32[]{:S(2)}) %all-to-all-start.4) | async-done | bytes 1048608 | tf_op jit(solution)/shard_map/all_to_all | solution.py:391
  172.6 17.8 %all_to_all.31 = f32[8,128,128]{2,1,0:T(8,128)S(1)} all-to-all(f32[8,128,128]{2,1,0:T(8,128)S(1)} %pad_maximum_fusion), channel_id=1, replica_groups=mesh['zl'=2,'y'=4,'zh'=2,'x'=4,'c'=2] {'zl','y'}, dimensions={0} | all-to-all | bytes 1048576 | tf_op jit(solution)/shard_map/all_to_all | solution.py:397
  190.5 0.8 copy.18
  (56 shorter events, 8.3 us)
Async XLA Ops:
  0.6 10.8 %copy-start.9 = (bf16[128,128]{1,0:T(8,128)(2,1)S(1)}, bf16[128,128]{1,0:T(8,128)(2,1)}, u32[]{:S(2)}) copy-start(bf16[128,128]{1,0:T(8,128)(2,1)} %param.7) | copy-start | bytes 98308
  0.6 23.0 %copy-start.5 = (bf16[128,512]{1,0:T(8,128)(2,1)S(1)}, bf16[128,512]{1,0:T(8,128)(2,1)}, u32[]{:S(2)}) copy-start(bf16[128,512]{1,0:T(8,128)(2,1)} %param.9) | copy-start | bytes 393220
  2.2 16.5 %all-to-all-start.1 = ((bf16[8,128,128]{2,1,0:T(8,128)(2,1)}), bf16[8,128,128]{2,1,0:T(8,128)(2,1)S(1)}, u32[]{:S(2)}, u32[]{:S(2)}) async-start(bf16[8,128,128]{2,1,0:T(8,128)(2,1)} %broadcast_in_dim.6), calls=%async_computation.1 | async-start | bytes 524288 | tf_op jit(solution)/shard_map/all_to_all | solution.py:368
  11.0 13.2 %copy-start.4 = (bf16[128,1024]{1,0:T(8,128)(2,1)S(1)}, bf16[128,1024]{1,0:T(8,128)(2,1)}, u32[]{:S(2)}) copy-start(bf16[128,1024]{1,0:T(8,128)(2,1)} %param.6) | copy-start | bytes 786436
  18.7 12.9 %all-to-all-start.3 = ((bf16[8,192,128]{2,1,0:T(8,128)(2,1)}), bf16[8,192,128]{2,1,0:T(8,128)(2,1)S(1)}, u32[]{:S(2)}, u32[]{:S(2)}) async-start(bf16[8,192,128]{2,1,0:T(8,128)(2,1)} %pad_maximum_fusion.2), calls=%async_computation.3 | async-start | bytes 786432 | tf_op jit(solution)/shard_map/all_to_all | solution.py:373
  31.6 18.1 %copy-start.2 = (bf16[8,192,128]{2,1,0:T(8,128)(2,1)}, bf16[8,192,128]{2,1,0:T(8,128)(2,1)S(1)}, u32[]{:S(2)}) copy-start(bf16[8,192,128]{2,1,0:T(8,128)(2,1)S(1)} %all-to-all-done.3.refs_0_.rest_0_) | copy-start | bytes 1179652
  42.1 43.0 %copy-start.3 = (bf16[8,192,128]{2,1,0:T(8,128)(2,1)}, bf16[8,192,128]{2,1,0:T(8,128)(2,1)S(1)}, u32[]{:S(2)}) copy-start(bf16[8,192,128]{2,1,0:T(8,128)(2,1)S(1)} %all_to_all.30.own) | copy-start | bytes 1179652
  44.0 52.5 %all-to-all-start.2 = ((bf16[8,8,128,128]{3,2,1,0:T(8,128)(2,1)}), bf16[8,8,128,128]{3,2,1,0:T(8,128)(2,1)S(1)}, u32[]{:S(2)}, u32[]{:S(2)}) async-start(bf16[8,8,128,128]{3,2,1,0:T(8,128)(2,1)} %broadcast_in_dim.7), calls=%async_computation.2 | async-start | bytes 4194304 | tf_op jit(solution)/shard_map/all_to_all | solution.py:368
  47.6 29.4 %collective-permute-start.1 = (bf16[8,192,128]{2,1,0:T(8,128)(2,1)S(1)}, bf16[8,192,128]{2,1,0:T(8,128)(2,1)}, u32[]{:S(2)}, u32[]{:S(2)}) collective-permute-start(bf16[8,192,128]{2,1,0:T(8,128)(2,1)S(1)} %all-to-all-done.3.refs_0_.rest_0_), channel_id=1, source_target_pairs={{0,8},{8,0},{1,9},{9,1},{2,10},{10,2},{3,11},{11,3},{4,12},{12,4},... | collective-permute-start | bytes 1179656 | tf_op jit(solution)/shard_map/ppermute | solution.py:360
  48.8 31.4 %collective-permute-start.2 = (bf16[8,192,128]{2,1,0:T(8,128)(2,1)S(1)}, bf16[8,192,128]{2,1,0:T(8,128)(2,1)S(1)}, u32[]{:S(2)}, u32[]{:S(2)}) collective-permute-start(bf16[8,192,128]{2,1,0:T(8,128)(2,1)S(1)} %all-to-all-done.3.refs_0_.rest_0_), channel_id=1, source_target_pairs={{0,2},{2,4},{4,6},{6,0},{1,3},{3,5},{5,7},{7,1},{8,10},{10,12},{12... | collective-permute-start | bytes 1179656 | tf_op jit(solution)/shard_map/ppermute | solution.py:356
  49.7 31.3 %collective-permute-start.3 = (bf16[8,192,128]{2,1,0:T(8,128)(2,1)S(1)}, bf16[8,192,128]{2,1,0:T(8,128)(2,1)}, u32[]{:S(2)}, u32[]{:S(2)}) collective-permute-start(bf16[8,192,128]{2,1,0:T(8,128)(2,1)S(1)} %all-to-all-done.3.refs_0_.rest_0_), channel_id=1, source_target_pairs={{0,6},{2,0},{4,2},{6,4},{1,7},{3,1},{5,3},{7,5},{8,14},{10,8},{12,... | collective-permute-start | bytes 1179656 | tf_op jit(solution)/shard_map/ppermute | solution.py:356
  77.0 10.8 %collective-permute-start.4 = (bf16[8,192,128]{2,1,0:T(8,128)(2,1)}, bf16[8,192,128]{2,1,0:T(8,128)(2,1)}, u32[]{:S(2)}, u32[]{:S(2)}) collective-permute-start(bf16[8,192,128]{2,1,0:T(8,128)(2,1)} %collective-permute-done.1.refs_1_.rest_1_), channel_id=1, source_target_pairs={{0,2},{2,4},{4,6},{6,0},{1,3},{3,5},{5,7},{7,1},{8,10},{10,12},{12... | collective-permute-start | bytes 1179656 | tf_op jit(solution)/shard_map/ppermute | solution.py:356
  77.7 12.1 %collective-permute-start.5 = (bf16[8,192,128]{2,1,0:T(8,128)(2,1)}, bf16[8,192,128]{2,1,0:T(8,128)(2,1)}, u32[]{:S(2)}, u32[]{:S(2)}) collective-permute-start(bf16[8,192,128]{2,1,0:T(8,128)(2,1)} %collective-permute-done.1.refs_1_.rest_1_), channel_id=1, source_target_pairs={{0,6},{2,0},{4,2},{6,4},{1,7},{3,1},{5,3},{7,5},{8,14},{10,8},{12,... | collective-permute-start | bytes 1179656 | tf_op jit(solution)/shard_map/ppermute | solution.py:356
  80.2 0.8 copy-start.6
  80.2 9.5 %collective-permute-start.6 = (bf16[4,192,128]{2,1,0:T(8,128)(2,1)S(1)}, bf16[4,192,128]{2,1,0:T(8,128)(2,1)S(1)}, u32[]{:S(2)}, u32[]{:S(2)}) collective-permute-start(bf16[4,192,128]{2,1,0:T(8,128)(2,1)S(1)} %slice.24), channel_id=1, source_target_pairs={{0,2},{2,4},{4,6},{6,0},{1,3},{3,5},{5,7},{7,1},{8,10},{10,12},{12... | collective-permute-start | bytes 589832 | tf_op jit(solution)/shard_map/ppermute | solution.py:356
  81.9 11.1 %collective-permute-start.7 = (bf16[4,192,128]{2,1,0:T(8,128)(2,1)S(1)}, bf16[4,192,128]{2,1,0:T(8,128)(2,1)S(1)}, u32[]{:S(2)}, u32[]{:S(2)}) collective-permute-start(bf16[4,192,128]{2,1,0:T(8,128)(2,1)S(1)} %slice.25), channel_id=1, source_target_pairs={{0,6},{2,0},{4,2},{6,4},{1,7},{3,1},{5,3},{7,5},{8,14},{10,8},{12,... | collective-permute-start | bytes 589832 | tf_op jit(solution)/shard_map/ppermute | solution.py:356
  85.1 11.4 %collective-permute-start = (bf16[8,192,128]{2,1,0:T(8,128)(2,1)S(1)}, bf16[8,192,128]{2,1,0:T(8,128)(2,1)}, u32[]{:S(2)}, u32[]{:S(2)}) collective-permute-start(bf16[8,192,128]{2,1,0:T(8,128)(2,1)S(1)} %all_to_all.30.own), channel_id=1, source_target_pairs={{0,1},{1,0},{2,3},{3,2},{4,5},{5,4},{6,7},{7,6},{8,9},{9,8},{10,11... | collective-permute-start | bytes 1179656 | tf_op jit(solution)/shard_map/ppermute | solution.py:360
  88.7 6.9 %collective-permute-start.8 = (bf16[4,192,128]{2,1,0:T(8,128)(2,1)S(1)}, bf16[4,192,128]{2,1,0:T(8,128)(2,1)S(1)}, u32[]{:S(2)}, u32[]{:S(2)}) collective-permute-start(bf16[4,192,128]{2,1,0:T(8,128)(2,1)S(1)} %slice.26), channel_id=1, source_target_pairs={{0,2},{2,4},{4,6},{6,0},{1,3},{3,5},{5,7},{7,1},{8,10},{10,12},{12... | collective-permute-start | bytes 589832 | tf_op jit(solution)/shard_map/ppermute | solution.py:356
  90.7 5.7 %collective-permute-start.9 = (bf16[4,192,128]{2,1,0:T(8,128)(2,1)S(1)}, bf16[4,192,128]{2,1,0:T(8,128)(2,1)S(1)}, u32[]{:S(2)}, u32[]{:S(2)}) collective-permute-start(bf16[4,192,128]{2,1,0:T(8,128)(2,1)S(1)} %slice.27), channel_id=1, source_target_pairs={{0,6},{2,0},{4,2},{6,4},{1,7},{3,1},{5,3},{7,5},{8,14},{10,8},{12,... | collective-permute-start | bytes 589832 | tf_op jit(solution)/shard_map/ppermute | solution.py:356
  93.1 3.4 %copy-start.7 = (bf16[8,192,128]{2,1,0:T(8,128)(2,1)}, bf16[8,192,128]{2,1,0:T(8,128)(2,1)S(1)}, u32[]{:S(2)}) copy-start(bf16[8,192,128]{2,1,0:T(8,128)(2,1)S(1)} %constant_dynamic-update-slice_fusion.refs_6_.rest_6_) | copy-start | bytes 1179652
  96.5 0.8 copy-start.8
  97.3 1.4 copy-start
  121.0 4.7 %collective-permute-start.10 = (f32[8,264,256]{2,1,0:T(8,128)}, f32[8,264,256]{2,1,0:T(8,128)S(1)}, u32[]{:S(2)}, u32[]{:S(2)}) collective-permute-start(f32[8,264,256]{2,1,0:T(8,128)} %get-tuple-element.7.rest_8_), channel_id=1, source_target_pairs={{0,1},{1,0},{2,3},{3,2},{4,5},{5,4},{6,7},{7,6},{8,9},{9,8},{10,11... | collective-permute-start | bytes 6488072 | tf_op jit(solution)/shard_map/ppermute | solution.py:360
  125.7 1.4 copy-start.10
  148.2 6.7 %copy-start.1 = (f32[8,64,256]{2,1,0:T(8,128)S(1)}, f32[8,64,256]{2,1,0:T(8,128)}, u32[]{:S(2)}) copy-start(f32[8,64,256]{2,1,0:T(8,128)} %get-tuple-element.10) | copy-start | bytes 1572868
  148.2 24.2 %all-to-all-start.4 = ((bf16[8,512,128]{2,1,0:T(8,128)(2,1)}), bf16[8,512,128]{2,1,0:T(8,128)(2,1)S(1)}, u32[]{:S(2)}, u32[]{:S(2)}) async-start(bf16[8,512,128]{2,1,0:T(8,128)(2,1)} %get-tuple-element.11), calls=%async_computation.4 | async-start | bytes 2097152 | tf_op jit(solution)/shard_map/all_to_all | solution.py:391
  155.8 1.6 collective-permute-start.11

commit v6 on v4

--- a/solution.py
+++ b/solution.py
@@ -7,6 +7,7 @@
 from jax.experimental import pallas as pl
 from jax.experimental.pallas import tpu as pltpu
 from jax.sharding import Mesh, PartitionSpec as P
+
 
 FLOOR = -1e30
 LOW = -1e29
@@ -25,7 +26,7 @@
 HALF = BLK // 2
 WIDTH = 4
 KEYS = WIDTH * BLK
-STEP = 4 // WIDTH
+SAFE = 2.0**100
 SLAB = 2 * BLK + HALF
 ROWS = BLK + HALF
 VROWS = 208
@@ -47,10 +48,6 @@
     return lax.dot_general(a, b, (((1,), (1,)), ((), ())), preferred_element_type=F32)
 
 
-def tn(a, b):
-    return lax.dot_general(a, b, (((0,), (0,)), ((), ())), preferred_element_type=F32)
-
-
 def split(a):
     high = a.astype(BF16)
     return high, (a - high.astype(F32)).astype(BF16)
@@ -110,12 +107,12 @@
         refs = refs[2:]
     if last:
         pack, okf, states = refs[:3]
-        carry, sums, prefix = refs[3:6]
-        refs = refs[6:]
+        carry, prefix = refs[3:5]
+        refs = refs[5:]
     else:
         carry, sums = refs[:2]
         refs = refs[2:]
-    k_buf, kf_buf, vft, q_buf, qf_buf = refs
+    k_buf, vft, q_buf, qf_buf = refs
     i = pl.program_id(0)
     a, b = 2 * i, 2 * i + 1
     if last:
@@ -124,80 +121,120 @@
         def _():
             prefix[...] = jnp.zeros_like(prefix)
 
-    if first:
-        carry[...] = jnp.zeros_like(carry)
-        for e in range(2):
-            carry[e, ROW_M : ROW_M + 1, :] = jnp.full((1, TR), LOW, F32)
-        sums[...] = jnp.zeros_like(sums)
-    else:
-        carry[...] = carry_in[...]
-        sums[...] = sums_in[...]
     for mine, at in core_slices(where):
         ref = own if mine else other
         for e in range(2):
             q_buf[e, at, :] = ref[e, :BLK, :]
             qf_buf[e, at, :] = jnp.concatenate(feats_of(ref, e, BLK), axis=0)
 
+    def scores_of(e, g, mask=None):
+        found = []
+        for at in range(0, KEYS, TR):
+            s = nt(k_buf[g, at : at + TR, :], q_buf[e])
+            found.append(s if mask is None else jnp.where(mask[at : at + TR], s, FLOOR))
+        return found
+
+    def added(total, g, found, top):
+        for at, s in zip(range(0, KEYS, TR), found):
+            total = total + nn(vft[g, :, at : at + TR], jnp.exp2((s - top) * SCORE).astype(BF16))
+        return total
+
     def update(plans):
-        olds = [carry[e, :VROWS, :] for e in range(2)]
-        tops = [carry[e, ROW_M : ROW_M + 1, :] for e in range(2)]
-        scores = []
-        for e, plan in enumerate(plans):
-            found = []
-            for g, mask in plan:
-                for at in range(0, KEYS, TR):
-                    s = nt(k_buf[g, at : at + TR, :], q_buf[e])
-                    s = s if mask is None else jnp.where(mask[at : at + TR], s, FLOOR)
-                    found.append((s, g, at))
-            scores.append(found)
-        results = []
-        for old, top, found in zip(olds, tops, scores):
+        scores = [[(g, scores_of(e, g, mask)) for g, mask in plan] for e, plan in enumerate(plans)]
+        for e, plan in enumerate(scores):
+            top = carry[e, ROW_M : ROW_M + 1, :]
             new = top
-            for s, _, _ in found:
-                new = jnp.maximum(new, jnp.max(s, axis=0, keepdims=True))
-            total = old * jnp.exp2((top - new) * SCORE)
-            probs = [jnp.exp2((s - new) * SCORE).astype(BF16) for s, _, _ in found]
-            for p, (_, g, at) in zip(probs, found):
-                total = total + nn(vft[g, :, at : at + TR], p)
-            results.append((total, new))
-        for e, (total, new) in enumerate(results):
+            for _, found in plan:
+                for s in found:
+                    new = jnp.maximum(new, jnp.max(s, axis=0, keepdims=True))
+            total = carry[e, :VROWS, :] * jnp.exp2((top - new) * SCORE)
+            for g, found in plan:
+                total = added(total, g, found, new)
             carry[e, :VROWS, :] = total
             carry[e, ROW_M : ROW_M + 1, :] = new
 
-    def full(u, c):
-        update([[(STEP * u + e, None) for e in range(STEP)]] * 2)
-        return c
-
-    lax.fori_loop(0, 2 * i // STEP, full, 0)
+    def restart():
+        for e in range(2):
+            if first:
+                carry[e, :VROWS, :] = jnp.zeros((VROWS, TR), F32)
+                carry[e, ROW_M : ROW_M + 1, :] = jnp.full((1, TR), LOW, F32)
+            else:
+                carry[e, :VROWS, :] = carry_in[e, :VROWS, :]
+                carry[e, ROW_M : ROW_M + 1, :] = carry_in[e, ROW_M : ROW_M + 1, :]
+
+    restart()
+
+    @pl.when(i > 0)
+    def _():
+        if first:
+            for e in range(2):
+                s = nt(k_buf[0, :BLK, :], q_buf[e])
+                carry[e, ROW_M : ROW_M + 1, :] = jnp.max(s, axis=0, keepdims=True)
+
+        def quick(u, c):
+            scores = [[scores_of(e, 2 * u + d) for d in range(2)] for e in range(2)]
+            totals = []
+            for e in range(2):
+                top = carry[e, ROW_M : ROW_M + 1, :]
+                total = carry[e, :VROWS, :]
+                for d in range(2):
+                    total = added(total, 2 * u + d, scores[e][d], top)
+                totals.append(total)
+            for e in range(2):
+                carry[e, :VROWS, :] = totals[e]
+            return c
+
+        lax.fori_loop(0, i, quick, 0)
+        row = slice(HD + FD, HD + FD + 1)
+        largest = jnp.max(jnp.maximum(carry[0, row, :], carry[1, row, :]))
+
+        @pl.when(jnp.logical_not(largest < SAFE))
+        def _():
+            restart()
+
+            def slow(g, c):
+                update([[(g, None)]] * 2)
+                return c
+
+            lax.fori_loop(0, a, slow, 0)
+
     tail_rows = jnp.where(iota((VROWS - HD - FD, KEYS), 0) == 0, 1.0, 0.0).astype(BF16)
+    feats = []
     for e, g in enumerate((a, b)):
+        parts = []
         for j, slab in enumerate(slabs):
             at = slice(j * BLK, (j + 1) * BLK)
-            feats = jnp.concatenate(feats_of(slab, e, 2 * BLK), axis=0)
+            part = jnp.concatenate(feats_of(slab, e, 2 * BLK), axis=0)
+            parts.append(part)
             k_buf[g, at, :] = slab[e, :BLK, :]
-            kf_buf[g, at, :] = feats
             vft[g, :HD, at] = slab[e, BLK : 2 * BLK, :].T
-            vft[g, HD : HD + FD, at] = feats.T
+            vft[g, HD : HD + FD, at] = part.T
         vft[g, HD + FD :, :] = tail_rows
+        feats.append(jnp.concatenate(parts, axis=0))
     masks = [tile_mask(blocks, where, g, columns) for g in (a, b)]
     update([[(a, masks[0])], [(a, None), (b, masks[1])]])
-    for e, (g, mask) in enumerate(zip((a, b), masks)):
+    for e, g in enumerate((a, b)):
         inv_n = FEAT_SCALE / (row_positions(blocks, where, g) + 1).astype(F32)
-        student = jnp.where(mask, nt(kf_buf[g], qf_buf[e]) * inv_n, 0.0).astype(BF16)
-        carry[e, ROW_L:ROW_M, :] += nn(vft[g, :HD, :], student)
-        sums[e] += nn(vft[g, : HD + FD, :], kf_buf[g])
-        if last:
+        student = jnp.where(masks[e], nt(feats[e], qf_buf[e]) * inv_n, 0.0).astype(BF16)
+        linear = nn(vft[g, :HD, :], student)
+        moment = nn(vft[g, : HD + FD, :], feats[e])
+        if not first:
+            linear = linear + carry_in[e, ROW_L:ROW_M, :]
+            moment = moment + sums_in[e]
+        if not last:
+            carry[e, ROW_L:ROW_M, :] = linear
+            sums[e] = moment
+        else:
             state = prefix[...]
             high, low = split(state[:HD])
-            linear = (nt(high, qf_buf[e]) + nt(low, qf_buf[e])) * inv_n
             pack[e, :HD, :] = carry[e, :HD, :]
-            pack[e, HD : 2 * HD, :] = carry[e, ROW_L:ROW_M, :] + linear
+            pack[e, HD : 2 * HD, :] = linear + (nt(high, qf_buf[e]) + nt(low, qf_buf[e])) * inv_n
             norm = carry[e, HD + FD : HD + FD + 1, :]
             top = carry[e, ROW_M : ROW_M + 1, :]
             pack[e, 2 * HD :, :] = jnp.where(iota((8, TR), 0) == 0, norm, top)
             okf[e] = carry[e, HD : HD + FD, :]
             states[e] = state.T
-            prefix[...] = state + sums[e]
+            prefix[...] = state + moment
 
 
 def backward_kernel(blocks, where, own, other, *rest):
@@ -293,13 +330,11 @@
     if last:
         outs = [((GROUPS, PACK, TR), F32), ((GROUPS, FD, TR), F32), ((GROUPS, FD, HD + FD), F32)]
         out_specs = [by_pair(PACK, TR), by_pair(FD, TR), by_pair(FD, HD + FD)]
-        scratch = [pltpu.VMEM((2, CARRY, TR), F32), pltpu.VMEM((2, HD + FD, FD), F32)]
-        scratch += [pltpu.VMEM((HD + FD, FD), F32)]
+        scratch = [pltpu.VMEM((2, CARRY, TR), F32), pltpu.VMEM((HD + FD, FD), F32)]
     else:
         outs, out_specs, scratch = [carry, sums], carry_specs, []
     scratch += [
         pltpu.VMEM((GROUPS, KEYS, HD), BF16),
-        pltpu.VMEM((GROUPS, KEYS, FD), BF16),
         pltpu.VMEM((GROUPS, VROWS, KEYS), BF16),
         pltpu.VMEM((2, TR, HD), BF16),
         pltpu.VMEM((2, TR, FD), BF16),
@@ -313,7 +348,6 @@
         out_specs=out_specs,
         scratch_shapes=scratch,
         cost_estimate=pl.CostEstimate(flops=6_000_000_000, transcendentals=2_400_000, bytes_accessed=8_000_000),
-        name="forward" + str(columns[0]),
     )(blocks, where, own, other, *slabs, *carried)
 
 
@@ -360,11 +394,12 @@
     return feats.reshape(2, HALF, GROUPS, FD).transpose(2, 1, 0, 3).reshape(GROUPS, HALF, 2 * FD)
 
 
-def per_device(queries, keys, values, query_feats, key_feats, block_pos):
+def step(queries, keys, values, query_feats, key_feats, block_pos):
     shared = jnp.broadcast_to(jnp.concatenate([keys, values], axis=0)[None], (GROUPS, 2 * BLK, HD))
     slab = lax.all_to_all(jnp.concatenate([shared, by_head(key_feats)], axis=1), HEADS, 0, 0, tiled=True)
+    left = shifted(slab, 1)
+    right = shifted(slab, 3)
     far = across(slab, "zh")
-    left, right = shifted(slab, 1), shifted(slab, 3)
     q_heads = queries.reshape(BLK, GROUPS, HD).transpose(1, 0, 2)
     rows = jnp.concatenate([q_heads, by_head(query_feats)], axis=1)
     own = lax.all_to_all(rows, HEADS, 0, 0, tiled=True)
@@ -396,7 +431,7 @@
     split_mesh = Mesh(mesh.devices.reshape(2, 4, 2, 4, 2), ("zl", "y", "zh", "x", "c"))
     spec = P(("zl", "y", "zh", "x", "c"), None)
     return jax.shard_map(
-        per_device,
+        step,
         mesh=split_mesh,
         in_specs=(spec,) * 5 + (P(),),
         out_specs=(spec, spec),

time: 164 us -> 158 us (0.963)
  Pallas kernels: 53.8 us -> 47.7 us
    pallas_call x2, Pallas kernels: 32.8 us -> 26.6 us  [forward(): pl.pallas_call(functools.partial(forward_kernel, columns, not carried, la...]
  transfers between devices with their start and end apart: 15 -> 15, of which waited for: 7 -> 7; matrix products, arithmetic and copies ran while one was open for 4% -> 4% of each run, Pallas kernels for 10% -> 8%
where the time goes in v6:
time: 158 us; the launch traced here: 157 us
  waiting for transfers between devices  48.5 us (31%)
  Pallas kernels  47.7 us (30%)
  starting transfers between devices  32.7 us (21%)
  blocking collectives  12.9 us (8%)
  local copies, waits for them, and re-layouts  11.3 us (7%)
  other arithmetic  3.26 us (2%)
    pallas_call x2, Pallas kernels, forward(): pl.pallas_call(functools.partial(forward_kernel, columns, not carried, la...  26.6 us
    pallas_call x1, Pallas kernels, backward(): pl.pallas_call(backward_kernel, grid=(PAIRS,), out_shape=(jax.ShapeDtypeS...  21.1 us
    all_to_all x1, waiting for transfers between devices, step(): dk = lax.all_to_all(dk, COLS, 0, 0, tiled=True).astype(F32).sum(axis=0)  15 us
    ppermute x8, starting transfers between devices, shifted(): return lax.ppermute(a, 'x', [(i, (i + step) % 4) for i in range(4)])  13.3 us
    all_to_all x1, blocking collectives, step(): final = lax.all_to_all(final, HEADS, 0, 0, tiled=True)  12.9 us
    all_to_all x1, waiting for transfers between devices, step(): own = lax.all_to_all(rows, HEADS, 0, 0, tiled=True)  11 us
    all_to_all x1, waiting for transfers between devices, step(): lax.all_to_all(jnp.concatenate([shared, by_head(key_feats)], axis=1), HEA...  10.5 us
    all_to_all x1, starting transfers between devices, step(): dk = lax.all_to_all(dk, COLS, 0, 0, tiled=True).astype(F32).sum(axis=0)  6.06 us
  transfers between devices with their start and end apart: 15, of which 7 were waited for; matrix products, arithmetic and copies ran while one was open for 4% of the time, Pallas kernels for 8%

profile of v6, /device:TPU:0, one launch (start us, length us, event | category | flops | bytes accessed | tf_op | source)
XLA Modules:
  0.0 157.2 jit_solution(3735012982506279830)
XLA Ops:
  0.6 1.1 reshape.35
  2.2 0.8 pad_maximum_fusion.3
  3.0 0.9 pad_maximum_fusion
  3.9 5.9 %all-to-all-start.1 = ((bf16[8,320,128]{2,1,0:T(8,128)(2,1)}), bf16[8,320,128]{2,1,0:T(8,128)(2,1)S(1)}, u32[]{:S(2)}, u32[]{:S(2)}) async-start(bf16[8,320,128]{2,1,0:T(8,128)(2,1)} %pad_maximum_fusion), calls=%async_computation.1 | async-start | bytes 1310720 | tf_op jit(solution)/shard_map/all_to_all | solution.py:399
  10.9 10.5 %all-to-all-done.1.refs_4_.rest_0_ = bf16[8,320,128]{2,1,0:T(8,128)(2,1)S(1)} async-done(((bf16[8,320,128]{2,1,0:T(8,128)(2,1)}), bf16[8,320,128]{2,1,0:T(8,128)(2,1)S(1)}, u32[]{:S(2)}, u32[]{:S(2)}) %all-to-all-start.1) | async-done | bytes 655392 | tf_op jit(solution)/shard_map/all_to_all | solution.py:399
  21.4 3.6 %collective-permute-start.1 = (bf16[8,320,128]{2,1,0:T(8,128)(2,1)S(1)}, bf16[8,320,128]{2,1,0:T(8,128)(2,1)}, u32[]{:S(2)}, u32[]{:S(2)}) collective-permute-start(bf16[8,320,128]{2,1,0:T(8,128)(2,1)S(1)} %all-to-all-done.1.refs_4_.rest_0_), channel_id=1, source_target_pairs={{0,8},{8,0},{1,9},{9,1},{2,10},{10,2},{3,11},{11,3},{4,12},{12,4},... | collective-permute-start | bytes 1966088 | tf_op jit(solution)/shard_map/ppermute | solution.py:390
  24.9 0.8 pad_maximum_fusion.2
  25.7 3.5 %all-to-all-start = ((bf16[8,192,128]{2,1,0:T(8,128)(2,1)}), bf16[8,192,128]{2,1,0:T(8,128)(2,1)S(1)}, u32[]{:S(2)}, u32[]{:S(2)}) async-start(bf16[8,192,128]{2,1,0:T(8,128)(2,1)} %pad_maximum_fusion.2), calls=%async_computation | async-start | bytes 786432 | tf_op jit(solution)/shard_map/all_to_all | solution.py:405
  29.2 1.6 collective-permute-start.2
  30.7 1.7 %collective-permute-start.3 = (bf16[8,320,128]{2,1,0:T(8,128)(2,1)S(1)}, bf16[8,320,128]{2,1,0:T(8,128)(2,1)}, u32[]{:S(2)}, u32[]{:S(2)}) collective-permute-start(bf16[8,320,128]{2,1,0:T(8,128)(2,1)S(1)} %all-to-all-done.1.refs_4_.rest_0_), channel_id=1, source_target_pairs={{0,6},{2,0},{4,2},{6,4},{1,7},{3,1},{5,3},{7,5},{8,14},{10,8},{12,... | collective-permute-start | bytes 1966088 | tf_op jit(solution)/shard_map/ppermute | solution.py:386
  32.5 11.0 %all-to-all-done.refs_2_.own = bf16[8,192,128]{2,1,0:T(8,128)(2,1)S(1)} async-done(((bf16[8,192,128]{2,1,0:T(8,128)(2,1)}), bf16[8,192,128]{2,1,0:T(8,128)(2,1)S(1)}, u32[]{:S(2)}, u32[]{:S(2)}) %all-to-all-start) | async-done | bytes 393248 | tf_op jit(solution)/shard_map/all_to_all | solution.py:405
  43.5 1.6 collective-permute-start.4
  45.0 1.7 %collective-permute-start.5 = (bf16[8,320,128]{2,1,0:T(8,128)(2,1)}, bf16[8,320,128]{2,1,0:T(8,128)(2,1)}, u32[]{:S(2)}, u32[]{:S(2)}) collective-permute-start(bf16[8,320,128]{2,1,0:T(8,128)(2,1)} %collective-permute-done.1.refs_5_.rest_1_), channel_id=1, source_target_pairs={{0,6},{2,0},{4,2},{6,4},{1,7},{3,1},{5,3},{7,5},{8,14},{10,8},{12,... | collective-permute-start | bytes 1966088 | tf_op jit(solution)/shard_map/ppermute | solution.py:386
  47.7 1.0 slice.25
  48.7 3.0 %collective-permute-start.7 = (bf16[4,320,128]{2,1,0:T(8,128)(2,1)S(1)}, bf16[4,320,128]{2,1,0:T(8,128)(2,1)S(1)}, u32[]{:S(2)}, u32[]{:S(2)}) collective-permute-start(bf16[4,320,128]{2,1,0:T(8,128)(2,1)S(1)} %slice.25), channel_id=1, source_target_pairs={{0,6},{2,0},{4,2},{6,4},{1,7},{3,1},{5,3},{7,5},{8,14},{10,8},{12,... | collective-permute-start | bytes 983048 | tf_op jit(solution)/shard_map/ppermute | solution.py:386
  51.8 0.8 copy-done.9
  52.6 13.0 %shard_map.77 = (f32[8,344,256]{2,1,0:T(8,128)}, f32[8,192,64]{2,1,0:T(8,128)}) custom-call(s32[128]{0:T(128)} %blocks.1, s32[3]{0:T(128)} %pad_add_fusion.refs_1_.where, bf16[8,192,128]{2,1,0:T(8,128)(2,1)} %copy-done.2, bf16[8,192,128]{2,1,0:T(8,128)(2,1)} %copy-done.9, bf16[8,320,128]{2,1,0:T(8,128)(2,1)} %copy-done, ...), custom_call_target="tpu_custom_call" | custom-call | flops 6000000000 | bytes 8000000 | tf_op jit(solution)/shard_map/pallas_call | solution.py:343
  65.6 1.0 slice.20
  66.7 1.0 slice.21
  67.7 3.3 %collective-permute-start.9 = (bf16[4,320,128]{2,1,0:T(8,128)(2,1)S(1)}, bf16[4,320,128]{2,1,0:T(8,128)(2,1)S(1)}, u32[]{:S(2)}, u32[]{:S(2)}) collective-permute-start(bf16[4,320,128]{2,1,0:T(8,128)(2,1)S(1)} %slice.21), channel_id=1, source_target_pairs={{0,6},{2,0},{4,2},{6,4},{1,7},{3,1},{5,3},{7,5},{8,14},{10,8},{12,... | collective-permute-start | bytes 983048 | tf_op jit(solution)/shard_map/ppermute | solution.py:386
  71.1 5.7 %collective-permute-done.8 = bf16[4,320,128]{2,1,0:T(8,128)(2,1)S(1)} collective-permute-done((bf16[4,320,128]{2,1,0:T(8,128)(2,1)S(1)}, bf16[4,320,128]{2,1,0:T(8,128)(2,1)S(1)}, u32[]{:S(2)}, u32[]{:S(2)}) %collective-permute-start.8) | collective-permute-done | bytes 327712 | tf_op jit(solution)/shard_map/ppermute | solution.py:386
  77.2 0.9 copy-done.6
  78.1 13.6 %shard_map.78 = (f32[8,264,256]{2,1,0:T(8,128)}, f32[8,64,256]{2,1,0:T(8,128)}, f32[8,64,192]{2,1,0:T(8,128)}) custom-call(s32[128]{0:T(128)} %blocks.1, s32[3]{0:T(128)} %pad_add_fusion.refs_1_.where, bf16[8,192,128]{2,1,0:T(8,128)(2,1)} %copy-done.2, bf16[8,192,128]{2,1,0:T(8,128)(2,1)} %copy-done.9, ...), custom_call_target="tpu_custom_call" | custom-call | flops 6000000000 | bytes 8000000 | tf_op jit(solution)/shard_map/pallas_call | solution.py:343
  91.9 4.5 %collective-permute-done.10.rest_9_ = f32[8,264,256]{2,1,0:T(8,128)S(1)} collective-permute-done((f32[8,264,256]{2,1,0:T(8,128)}, f32[8,264,256]{2,1,0:T(8,128)S(1)}, u32[]{:S(2)}, u32[]{:S(2)}) %collective-permute-start.10) | collective-permute-done | bytes 2162720 | tf_op jit(solution)/shard_map/ppermute | solution.py:390
  96.4 1.3 copy-done.8
  97.7 21.1 %backward.1 = (bf16[8,512,128]{2,1,0:T(8,128)(2,1)}, f32[8,64,256]{2,1,0:T(8,128)}) custom-call(s32[128]{0:T(128)} %blocks.1, s32[3]{0:T(128)} %pad_add_fusion.refs_1_.where, bf16[8,192,128]{2,1,0:T(8,128)(2,1)} %copy-done.2, bf16[8,192,128]{2,1,0:T(8,128)(2,1)} %copy-done.9, bf16[8,320,128]{2,1,0:T(8,128)(2,1)} %copy-done, ...), custom_call_target="tpu_custom_call" | custom-call | flops 20000000000 | bytes 16000000 | tf_op jit(solution)/shard_map/backward/pallas_call | solution.py:357
  118.8 6.1 %all-to-all-start.2 = ((bf16[8,512,128]{2,1,0:T(8,128)(2,1)}), bf16[8,512,128]{2,1,0:T(8,128)(2,1)S(1)}, u32[]{:S(2)}, u32[]{:S(2)}) async-start(bf16[8,512,128]{2,1,0:T(8,128)(2,1)} %get-tuple-element.23), calls=%async_computation.2 | async-start | bytes 2097152 | tf_op jit(solution)/shard_map/all_to_all | solution.py:420
  125.8 1.5 collective-permute-done.11
  127.4 15.0 %all-to-all-done.2 = bf16[8,512,128]{2,1,0:T(8,128)(2,1)S(1)} async-done(((bf16[8,512,128]{2,1,0:T(8,128)(2,1)}), bf16[8,512,128]{2,1,0:T(8,128)(2,1)S(1)}, u32[]{:S(2)}, u32[]{:S(2)}) %all-to-all-start.2) | async-done | bytes 1048608 | tf_op jit(solution)/shard_map/all_to_all | solution.py:420
  142.6 12.9 %all_to_all.20 = f32[8,128,128]{2,1,0:T(8,128)S(1)} all-to-all(f32[8,128,128]{2,1,0:T(8,128)S(1)} %pad_maximum_fusion.1), channel_id=1, replica_groups=mesh['zl'=2,'y'=4,'zh'=2,'x'=4,'c'=2] {'zl','y'}, dimensions={0} | all-to-all | bytes 1048576 | tf_op jit(solution)/shard_map/all_to_all | solution.py:426
  155.6 0.8 copy.18
  156.4 0.8 copy.19
  (51 shorter events, 4.4 us)
Async XLA Ops:
  1.7 8.1 %copy-start.7 = (bf16[128,512]{1,0:T(8,128)(2,1)S(1)}, bf16[128,512]{1,0:T(8,128)(2,1)}, u32[]{:S(2)}) copy-start(bf16[128,512]{1,0:T(8,128)(2,1)} %param.9) | copy-start | bytes 393220
  3.0 7.5 %copy-start.3 = (bf16[128,1024]{1,0:T(8,128)(2,1)S(1)}, bf16[128,1024]{1,0:T(8,128)(2,1)}, u32[]{:S(2)}) copy-start(bf16[128,1024]{1,0:T(8,128)(2,1)} %param.6) | copy-start | bytes 786436
  3.9 17.4 %all-to-all-start.1 = ((bf16[8,320,128]{2,1,0:T(8,128)(2,1)}), bf16[8,320,128]{2,1,0:T(8,128)(2,1)S(1)}, u32[]{:S(2)}, u32[]{:S(2)}) async-start(bf16[8,320,128]{2,1,0:T(8,128)(2,1)} %pad_maximum_fusion), calls=%async_computation.1 | async-start | bytes 1310720 | tf_op jit(solution)/shard_map/all_to_all | solution.py:399
  21.4 30.4 %copy-start = (bf16[8,320,128]{2,1,0:T(8,128)(2,1)}, bf16[8,320,128]{2,1,0:T(8,128)(2,1)S(1)}, u32[]{:S(2)}) copy-start(bf16[8,320,128]{2,1,0:T(8,128)(2,1)S(1)} %all-to-all-done.1.refs_4_.rest_0_) | copy-start | bytes 1966084
  21.4 22.1 %collective-permute-start.1 = (bf16[8,320,128]{2,1,0:T(8,128)(2,1)S(1)}, bf16[8,320,128]{2,1,0:T(8,128)(2,1)}, u32[]{:S(2)}, u32[]{:S(2)}) collective-permute-start(bf16[8,320,128]{2,1,0:T(8,128)(2,1)S(1)} %all-to-all-done.1.refs_4_.rest_0_), channel_id=1, source_target_pairs={{0,8},{8,0},{1,9},{9,1},{2,10},{10,2},{3,11},{11,3},{4,12},{12,4},... | collective-permute-start | bytes 1966088 | tf_op jit(solution)/shard_map/ppermute | solution.py:390
  25.7 17.7 %all-to-all-start = ((bf16[8,192,128]{2,1,0:T(8,128)(2,1)}), bf16[8,192,128]{2,1,0:T(8,128)(2,1)S(1)}, u32[]{:S(2)}, u32[]{:S(2)}) async-start(bf16[8,192,128]{2,1,0:T(8,128)(2,1)} %pad_maximum_fusion.2), calls=%async_computation | async-start | bytes 786432 | tf_op jit(solution)/shard_map/all_to_all | solution.py:405
  29.2 18.2 %collective-permute-start.2 = (bf16[8,320,128]{2,1,0:T(8,128)(2,1)S(1)}, bf16[8,320,128]{2,1,0:T(8,128)(2,1)S(1)}, u32[]{:S(2)}, u32[]{:S(2)}) collective-permute-start(bf16[8,320,128]{2,1,0:T(8,128)(2,1)S(1)} %all-to-all-done.1.refs_4_.rest_0_), channel_id=1, source_target_pairs={{0,2},{2,4},{4,6},{6,0},{1,3},{3,5},{5,7},{7,1},{8,10},{10,12},{12... | collective-permute-start | bytes 1966088 | tf_op jit(solution)/shard_map/ppermute | solution.py:386
  30.7 17.0 %collective-permute-start.3 = (bf16[8,320,128]{2,1,0:T(8,128)(2,1)S(1)}, bf16[8,320,128]{2,1,0:T(8,128)(2,1)}, u32[]{:S(2)}, u32[]{:S(2)}) collective-permute-start(bf16[8,320,128]{2,1,0:T(8,128)(2,1)S(1)} %all-to-all-done.1.refs_4_.rest_0_), channel_id=1, source_target_pairs={{0,6},{2,0},{4,2},{6,4},{1,7},{3,1},{5,3},{7,5},{8,14},{10,8},{12,... | collective-permute-start | bytes 1966088 | tf_op jit(solution)/shard_map/ppermute | solution.py:386
  43.4 8.3 %copy-start.2 = (bf16[8,192,128]{2,1,0:T(8,128)(2,1)}, bf16[8,192,128]{2,1,0:T(8,128)(2,1)S(1)}, u32[]{:S(2)}) copy-start(bf16[8,192,128]{2,1,0:T(8,128)(2,1)S(1)} %all-to-all-done.refs_2_.own) | copy-start | bytes 1179652
  43.4 8.3 %collective-permute-start = (bf16[8,192,128]{2,1,0:T(8,128)(2,1)S(1)}, bf16[8,192,128]{2,1,0:T(8,128)(2,1)S(1)}, u32[]{:S(2)}, u32[]{:S(2)}) collective-permute-start(bf16[8,192,128]{2,1,0:T(8,128)(2,1)S(1)} %all-to-all-done.refs_2_.own), channel_id=1, source_target_pairs={{0,1},{1,0},{2,3},{3,2},{4,5},{5,4},{6,7},{7,6},{8,9},{9,8},{10,11... | collective-permute-start | bytes 1179656 | tf_op jit(solution)/shard_map/ppermute | solution.py:390
  43.5 22.1 %collective-permute-start.4 = (bf16[8,320,128]{2,1,0:T(8,128)(2,1)}, bf16[8,320,128]{2,1,0:T(8,128)(2,1)}, u32[]{:S(2)}, u32[]{:S(2)}) collective-permute-start(bf16[8,320,128]{2,1,0:T(8,128)(2,1)} %collective-permute-done.1.refs_5_.rest_1_), channel_id=1, source_target_pairs={{0,2},{2,4},{4,6},{6,0},{1,3},{3,5},{5,7},{7,1},{8,10},{10,12},{12... | collective-permute-start | bytes 1966088 | tf_op jit(solution)/shard_map/ppermute | solution.py:386
  45.0 20.6 %collective-permute-start.5 = (bf16[8,320,128]{2,1,0:T(8,128)(2,1)}, bf16[8,320,128]{2,1,0:T(8,128)(2,1)}, u32[]{:S(2)}, u32[]{:S(2)}) collective-permute-start(bf16[8,320,128]{2,1,0:T(8,128)(2,1)} %collective-permute-done.1.refs_5_.rest_1_), channel_id=1, source_target_pairs={{0,6},{2,0},{4,2},{6,4},{1,7},{3,1},{5,3},{7,5},{8,14},{10,8},{12,... | collective-permute-start | bytes 1966088 | tf_op jit(solution)/shard_map/ppermute | solution.py:386
  47.4 4.4 %copy-start.4 = (bf16[8,320,128]{2,1,0:T(8,128)(2,1)}, bf16[8,320,128]{2,1,0:T(8,128)(2,1)S(1)}, u32[]{:S(2)}) copy-start(bf16[8,320,128]{2,1,0:T(8,128)(2,1)S(1)} %collective-permute-done.2.refs_6_.rest_2_) | copy-start | bytes 1966084
  47.4 23.6 %collective-permute-start.6 = (bf16[4,320,128]{2,1,0:T(8,128)(2,1)S(1)}, bf16[4,320,128]{2,1,0:T(8,128)(2,1)S(1)}, u32[]{:S(2)}, u32[]{:S(2)}) collective-permute-start(bf16[4,320,128]{2,1,0:T(8,128)(2,1)S(1)} %slice.24), channel_id=1, source_target_pairs={{0,2},{2,4},{4,6},{6,0},{1,3},{3,5},{5,7},{7,1},{8,10},{10,12},{12... | collective-permute-start | bytes 983048 | tf_op jit(solution)/shard_map/ppermute | solution.py:386
  48.7 22.3 %collective-permute-start.7 = (bf16[4,320,128]{2,1,0:T(8,128)(2,1)S(1)}, bf16[4,320,128]{2,1,0:T(8,128)(2,1)S(1)}, u32[]{:S(2)}, u32[]{:S(2)}) collective-permute-start(bf16[4,320,128]{2,1,0:T(8,128)(2,1)S(1)} %slice.25), channel_id=1, source_target_pairs={{0,6},{2,0},{4,2},{6,4},{1,7},{3,1},{5,3},{7,5},{8,14},{10,8},{12,... | collective-permute-start | bytes 983048 | tf_op jit(solution)/shard_map/ppermute | solution.py:386
  51.8 0.8 copy-start.9
  66.6 10.2 %collective-permute-start.8 = (bf16[4,320,128]{2,1,0:T(8,128)(2,1)S(1)}, bf16[4,320,128]{2,1,0:T(8,128)(2,1)S(1)}, u32[]{:S(2)}, u32[]{:S(2)}) collective-permute-start(bf16[4,320,128]{2,1,0:T(8,128)(2,1)S(1)} %slice.20), channel_id=1, source_target_pairs={{0,2},{2,4},{4,6},{6,0},{1,3},{3,5},{5,7},{7,1},{8,10},{10,12},{12... | collective-permute-start | bytes 983048 | tf_op jit(solution)/shard_map/ppermute | solution.py:386
  67.7 9.5 %collective-permute-start.9 = (bf16[4,320,128]{2,1,0:T(8,128)(2,1)S(1)}, bf16[4,320,128]{2,1,0:T(8,128)(2,1)S(1)}, u32[]{:S(2)}, u32[]{:S(2)}) collective-permute-start(bf16[4,320,128]{2,1,0:T(8,128)(2,1)S(1)} %slice.21), channel_id=1, source_target_pairs={{0,6},{2,0},{4,2},{6,4},{1,7},{3,1},{5,3},{7,5},{8,14},{10,8},{12,... | collective-permute-start | bytes 983048 | tf_op jit(solution)/shard_map/ppermute | solution.py:386
  71.0 6.1 %copy-start.5 = (bf16[8,320,128]{2,1,0:T(8,128)(2,1)}, bf16[8,320,128]{2,1,0:T(8,128)(2,1)S(1)}, u32[]{:S(2)}) copy-start(bf16[8,320,128]{2,1,0:T(8,128)(2,1)S(1)} %constant_dynamic-update-slice_fusion.refs_6_.rest_6_) | copy-start | bytes 1966084
  77.2 0.9 copy-start.6
  91.7 4.7 %collective-permute-start.10 = (f32[8,264,256]{2,1,0:T(8,128)}, f32[8,264,256]{2,1,0:T(8,128)S(1)}, u32[]{:S(2)}, u32[]{:S(2)}) collective-permute-start(f32[8,264,256]{2,1,0:T(8,128)} %get-tuple-element.19.rest_8_), channel_id=1, source_target_pairs={{0,1},{1,0},{2,3},{3,2},{4,5},{5,4},{6,7},{7,6},{8,9},{9,8},{10,11... | collective-permute-start | bytes 6488072 | tf_op jit(solution)/shard_map/ppermute | solution.py:390
  96.4 1.3 copy-start.8
  118.8 6.1 %copy-start.1 = (f32[8,64,256]{2,1,0:T(8,128)S(1)}, f32[8,64,256]{2,1,0:T(8,128)}, u32[]{:S(2)}) copy-start(f32[8,64,256]{2,1,0:T(8,128)} %get-tuple-element.22) | copy-start | bytes 1572868
  118.8 23.6 %all-to-all-start.2 = ((bf16[8,512,128]{2,1,0:T(8,128)(2,1)}), bf16[8,512,128]{2,1,0:T(8,128)(2,1)S(1)}, u32[]{:S(2)}, u32[]{:S(2)}) async-start(bf16[8,512,128]{2,1,0:T(8,128)(2,1)} %get-tuple-element.23), calls=%async_computation.2 | async-start | bytes 2097152 | tf_op jit(solution)/shard_map/all_to_all | solution.py:420
  125.7 1.6 %collective-permute-start.11 = (f32[8,64,1,128]{3,1,0,2:T(8,128)S(1)}, f32[8,64,1,128]{3,1,0,2:T(8,128)S(1)}, u32[]{:S(2)}, u32[]{:S(2)}) collective-permute-start(f32[8,64,1,128]{3,1,0,2:T(8,128)S(1)} %bitcast.30), channel_id=1, source_target_pairs={{0,1},{1,0},{2,3},{3,2},{4,5},{5,4},{6,7},{7,6},{8,9},{9,8},{10,11... | collective-permute-start | bytes 786440 | tf_op jit(solution)/shard_map/ppermute | solution.py:390
